TPU v7x, 32 devices: a whole 2x2x4 slice. The times are simulated.
32 devices in a mesh: slab: 4 (over y, core), tile: 8 (over z, x).
Axes of the slice: x: 2, y: 2, z: 4, core: 2. Of those that a mesh axis runs over, the one named last changes fastest.
Arguments:
- electric: float32 [3, 56, 256, 1024], P(None, 'slab', 'tile'), may hold values from -6 to 6
- current: float32 [3, 56, 256, 1024], P(None, 'slab', 'tile'), may hold values from -6 to 6
- mass_shift: float32 [56, 256, 1024], P('slab', 'tile'), may hold values from 0.5 to 4
- interface: float32 [4, 2, 2, 256, 1024], P('slab', None, None, 'tile'), may hold values from -6 to 6
- auxiliary: float32 [4, 2, 4, 2, 256, 1024], P('slab', None, None, None, 'tile'), may hold values from -3 to 3
Outputs:
- smoothed: float32 [3, 56, 256, 1024], P(None, 'slab', 'tile')
- next_interface: float32 [4, 2, 2, 256, 1024], P('slab', None, None, 'tile')
- next_auxiliary: float32 [4, 2, 4, 2, 256, 1024], P('slab', None, None, None, 'tile')
All inputs are finite; a program needn't handle non-finite values.
Results may differ from a plain program's by a relative error of at most 0.0001.
Values sent between devices are 32-bit elements; how exact they have to be, the bound alone decides.
No kernel may reach another device: no remote copies, remote signals or barrier semaphores. Data moves between devices by JAX's collectives and lax.ppermute only.
A program may use at most 128 MiB of HBM per device.

v0:
```python
import math

import jax
import jax.numpy as jnp
from jax import lax
from jax.sharding import PartitionSpec as P

pade_weights = [2.0 / 9.0 * math.sin(j * math.pi / 9.0) ** 2 for j in range(1, 5)]
pade_decays = [math.cos(j * math.pi / 9.0) ** 2 for j in range(1, 5)]


def extended(cells, sides, width):
    for axis, dim in sides:
        count = lax.axis_size(axis)
        ends = count - 1
        head = lax.slice_in_dim(cells, 0, width, axis=dim)
        tail = lax.slice_in_dim(cells, cells.shape[dim] - width, cells.shape[dim], axis=dim)
        cells = jnp.concatenate(
            [
                lax.ppermute(tail, axis, [(i, (i + 1) % count) for i in range(ends)]),
                cells,
                lax.ppermute(head, axis, [((i + 1) % count, i) for i in range(ends)]),
            ],
            axis=dim,
        )
    return cells


def from_behind(block, axis, distance):
    devices = range(lax.axis_size(axis))
    route = [(i - distance, i) for i in devices if i - distance in devices]
    return lax.ppermute(block, axis, route)


def forward_diff(values, along):
    along = along % values.ndim
    count = values.shape[along]
    shifted = jnp.concatenate(
        [
            lax.slice_in_dim(values, 1, count, axis=along),
            jnp.zeros_like(lax.slice_in_dim(values, 0, 1, axis=along)),
        ],
        along,
    )
    return shifted - values


def backward_diff(values, along):
    along = along % values.ndim
    count = values.shape[along]
    shifted = jnp.concatenate(
        [
            jnp.zeros_like(lax.slice_in_dim(values, 0, 1, axis=along)),
            lax.slice_in_dim(values, 0, count - 1, axis=along),
        ],
        along,
    )
    return values - shifted


def curl_curl(padded):
    field_x, field_y, field_z = (padded[0], padded[1], padded[2])
    flux_x = forward_diff(field_z, 1) - forward_diff(field_y, 0)
    flux_y = forward_diff(field_x, 0) - forward_diff(field_z, 2)
    flux_z = forward_diff(field_y, 2) - forward_diff(field_x, 1)
    image_x = backward_diff(flux_z, 1) - backward_diff(flux_y, 0)
    image_y = backward_diff(flux_x, 0) - backward_diff(flux_z, 2)
    image_z = backward_diff(flux_y, 2) - backward_diff(flux_x, 1)
    return jnp.stack([image_x, image_y, image_z])[:, 1:-1, 1:-1, :]


def update(padded, current, mass_shift):
    interior = padded[:, 1:-1, 1:-1, :]
    residual = current - (curl_curl(padded) + mass_shift * interior)
    return interior + 0.5 * residual / (mass_shift + 4.0)


def surface(padded):
    comp_x = padded[..., 0, :, :]
    comp_y = padded[..., 1, :, :]
    divergence = backward_diff(comp_x, -1) + backward_diff(comp_y, -2)
    rotation = forward_diff(comp_y, -1) - forward_diff(comp_x, -2)
    vort_x = backward_diff(rotation, -2) - forward_diff(divergence, -1)
    vort_y = -backward_diff(rotation, -1) - forward_diff(divergence, -2)
    return (jnp.stack([vort_x, vort_y], axis=-3) / 8.0)[..., 1:-1, :]


def shards(electric, current, mass_shift, interface, auxiliary):
    weights = jnp.asarray(pade_weights, jnp.float32).reshape(1, 4, 1, 1, 1)
    decays = jnp.asarray(pade_decays, jnp.float32).reshape(1, 4, 1, 1, 1)
    strip = electric.shape[2]
    width = electric.shape[3]
    zero_plane = jnp.zeros((1, strip, width), jnp.float32)
    below_ghost = jnp.concatenate([interface[0, 0], zero_plane], 0)
    above_ghost = jnp.concatenate([interface[0, 1], zero_plane], 0)
    local_field = electric
    for sweep_index in range(2):
        padded = extended(
            jnp.concatenate([below_ghost[:, None], local_field, above_ghost[:, None]], 1),
            (("tile", 2),),
            1,
        )
        local_field = update(padded, current, mass_shift)
    traces = jnp.stack([local_field[0:2, 0], local_field[0:2, -1]])
    combined = traces[:, None] - decays * auxiliary[0]
    padded_surface = extended(combined, (("tile", 3),), 1)
    new_auxiliary = surface(padded_surface)
    outgoing = traces + jnp.sum(weights * new_auxiliary, axis=1)
    from_below = from_behind(outgoing[1], "slab", 1)
    from_above = from_behind(outgoing[0], "slab", -1)
    next_interface = jnp.stack([from_below, from_above])[None]
    return (local_field, next_interface, new_auxiliary[None])


def solution(mesh):
    placed = (
        P(None, "slab", "tile", None),
        P(None, "slab", "tile", None),
        P("slab", "tile", None),
        P("slab", None, None, "tile", None),
        P("slab", None, None, None, "tile", None),
    )
    return jax.shard_map(
        shards,
        mesh=mesh,
        in_specs=placed,
        out_specs=(
            P(None, "slab", "tile", None),
            P("slab", None, None, "tile", None),
            P("slab", None, None, None, "tile", None),
        ),
        check_vma=False,
    )
```

profile of v0, /device:TPU:3, one launch (start us, length us, event | category | flops | bytes accessed | tf_op | source)
XLA Modules:
  0.0 139.7 jit_solution(5218495401321182626)
XLA Ops:
  0.6 1.1 slice_bitcast_fusion.17
  1.8 3.6 %pad_maximum_fusion.5 = f32[3,16,32,1024]{3,2,1,0:T(8,128)S(1)} fusion(f32[3,1,32,1024]{3,2,1,0:T(8,128)S(1)} %get-tuple-element.45, f32[3,1,32,1024]{3,2,1,0:T(8,128)S(1)} %get-tuple-element.46, f32[3,14,32,1024]{3,2,1,0:T(8,128)} %param.7), kind=kLoop, calls=%fused_computation.5 | loop fusion | flops 3145728 | bytes 12582912 | tf_op jit(solution)/shard_map/concatenate | solution.py:99
  5.8 3.2 %collective-permute-start = (f32[3,16,1,1024]{3,2,1,0:T(1,128)S(1)}, f32[3,16,1,1024]{3,2,1,0:T(1,128)S(1)}, u32[]{:S(2)}, u32[]{:S(2)}) collective-permute-start(f32[3,16,1,1024]{3,2,1,0:T(1,128)S(1)} %get-tuple-element.21), channel_id=1, source_target_pairs={{0,1},{1,2},{2,3},{3,4},{4,5},{5,6},{6,7},{8,9},{9,10},{10,11},{11... | collective-permute-start | bytes 589832 | tf_op jit(solution)/shard_map/ppermute | solution.py:20
  8.9 2.1 %collective-permute-start.1 = (f32[3,16,1,1024]{3,2,1,0:T(1,128)S(1)}, f32[3,16,1,1024]{3,2,1,0:T(1,128)S(1)}, u32[]{:S(2)}, u32[]{:S(2)}) collective-permute-start(f32[3,16,1,1024]{3,2,1,0:T(1,128)S(1)} %get-tuple-element.22), channel_id=1, source_target_pairs={{1,0},{2,1},{3,2},{4,3},{5,4},{6,5},{7,6},{9,8},{10,9},{11,10},{12... | collective-permute-start | bytes 589832 | tf_op jit(solution)/shard_map/ppermute | solution.py:22
  11.3 2.1 %collective-permute-done = f32[3,16,1,1024]{3,2,1,0:T(1,128)S(1)} collective-permute-done((f32[3,16,1,1024]{3,2,1,0:T(1,128)S(1)}, f32[3,16,1,1024]{3,2,1,0:T(1,128)S(1)}, u32[]{:S(2)}, u32[]{:S(2)}) %collective-permute-start) | collective-permute-done | bytes 196640 | tf_op jit(solution)/shard_map/ppermute | solution.py:20
  13.4 3.9 %collective-permute-done.1 = f32[3,16,1,1024]{3,2,1,0:T(1,128)S(1)} collective-permute-done((f32[3,16,1,1024]{3,2,1,0:T(1,128)S(1)}, f32[3,16,1,1024]{3,2,1,0:T(1,128)S(1)}, u32[]{:S(2)}, u32[]{:S(2)}) %collective-permute-start.1) | collective-permute-done | bytes 196640 | tf_op jit(solution)/shard_map/ppermute | solution.py:22
  17.4 1.9 %fusion.1 = f32[3,16,34,1024]{3,2,1,0:T(8,128)S(1)} fusion(f32[3,1,32,1024]{3,2,1,0:T(8,128)S(1)} %get-tuple-element.45, f32[3,1,32,1024]{3,2,1,0:T(8,128)S(1)} %get-tuple-element.46, f32[3,16,1,1024]{3,2,1,0:T(1,128)S(1)} %collective-permute-done.1, f32[3,14,32,1024]{3,2,1,0:T(8,128)S(1)} %bitcast.117, f32[3,16,1,1024]{3,2,1,0:T(1,128)S(1)} %collective-permute-done), kind=kLoop, calls=%fused_computation.9 | loop fusion | flops 6684672 | bytes 13369344 | tf_op jit(solution)/shard_map/concatenate | solution.py:18
  19.3 2.7 %slice_bitcast_fusion.9 = (f32[15,34,1024]{2,1,0:T(8,128)}, f32[15,34,1024]{2,1,0:T(8,128)}) fusion(f32[3,16,34,1024]{3,2,1,0:T(8,128)S(1)} %fusion.1), kind=kLoop, calls=%fused_computation.48 | loop fusion | bytes 8355840 | tf_op jit(solution)/shard_map/slice | solution.py:40
  22.0 1.5 %slice_bitcast_fusion.5 = (f32[16,34,1024]{2,1,0:T(8,128)S(1)}, f32[16,34,1024]{2,1,0:T(8,128)S(1)}, f32[16,34,1024]{2,1,0:T(8,128)S(1)}) fusion(f32[3,16,34,1024]{3,2,1,0:T(8,128)S(1)} %fusion.1), kind=kLoop, calls=%fused_computation.31 | loop fusion | bytes 13369344 | tf_op jit(solution)/shard_map/squeeze | solution.py:62
  23.5 1.9 %slice.251 = f32[16,33,1024]{2,1,0:T(8,128)} slice(f32[16,34,1024]{2,1,0:T(8,128)S(1)} %get-tuple-element.15), slice={[0:16], [1:34], [0:1024]} | slice | bytes 4325376 | tf_op jit(solution)/shard_map/slice | solution.py:40
  25.3 2.3 %slice.249 = f32[16,34,1023]{2,1,0:T(8,128)} slice(f32[16,34,1024]{2,1,0:T(8,128)S(1)} %get-tuple-element.15), slice={[0:16], [0:34], [1:1024]} | slice | bytes 4452096 | tf_op jit(solution)/shard_map/slice | solution.py:40
  27.6 2.2 %slice.243 = f32[16,34,1023]{2,1,0:T(8,128)} slice(f32[16,34,1024]{2,1,0:T(8,128)S(1)} %get-tuple-element.14), slice={[0:16], [0:34], [1:1024]} | slice | bytes 4452096 | tf_op jit(solution)/shard_map/slice | solution.py:40
  29.8 1.9 %slice.245 = f32[16,33,1024]{2,1,0:T(8,128)} slice(f32[16,34,1024]{2,1,0:T(8,128)S(1)} %get-tuple-element.16), slice={[0:16], [1:34], [0:1024]} | slice | bytes 4325376 | tf_op jit(solution)/shard_map/slice | solution.py:40
  31.7 6.9 %subtract_subtract_fusion.5 = (f32[16,34,1024]{2,1,0:T(8,128)S(1)}, f32[16,34,1024]{2,1,0:T(8,128)S(1)}, f32[16,34,1024]{2,1,0:T(8,128)S(1)}) fusion(f32[16,33,1024]{2,1,0:T(8,128)} %slice.245, f32[16,34,1023]{2,1,0:T(8,128)} %slice.243, f32[3,16,34,1024]{3,2,1,0:T(8,128)S(1)} %fusion.1, f32[16,34,1023]{2,1,0:T(8,128)} %slice.249, ...), kind=kLoop, calls=%fused_computation.44 | loop fusion | flops 5013504 | bytes 26324736 | tf_op jit(solution)/shard_map/sub | solution.py:65
  38.6 1.6 %slice.250 = f32[15,34,1024]{2,1,0:T(8,128)} slice(f32[16,34,1024]{2,1,0:T(8,128)S(1)} %get-tuple-element.12), slice={[0:15], [0:34], [0:1024]} | slice | bytes 4177920 | tf_op jit(solution)/shard_map/slice | solution.py:54
  40.2 1.7 %slice.253 = f32[15,34,1024]{2,1,0:T(8,128)} slice(f32[16,34,1024]{2,1,0:T(8,128)S(1)} %get-tuple-element.13), slice={[0:15], [0:34], [0:1024]} | slice | bytes 4177920 | tf_op jit(solution)/shard_map/slice | solution.py:54
  41.9 7.3 %subtract_bitcast_fusion.5 = (f32[1,16,34,1024]{3,2,1,0:T(8,128)}, f32[1,16,34,1024]{3,2,1,0:T(8,128)}, f32[1,16,34,1024]{3,2,1,0:T(8,128)}) fusion(f32[16,34,1024]{2,1,0:T(8,128)S(1)} %get-tuple-element.12, f32[15,34,1024]{2,1,0:T(8,128)} %slice.250, f32[16,34,1024]{2,1,0:T(8,128)S(1)} %get-tuple-element.11, f32[16,33,1024]{2,1,0:T(8,128)S(1)} %bitcast.118, ...), kind=kLoop, calls=%fused_computation.42 | loop fusion | flops 5013504 | bytes 26324736 | tf_op jit(solution)/shard_map/stack | solution.py:69
  49.3 4.8 %fusion.13 = f32[3,14,32,1024]{3,2,1,0:T(8,128)S(1)} fusion(f32[3,14,32,1024]{3,2,1,0:T(8,128)S(1)} %bitcast.117, f32[3,14,32,1024]{3,2,1,0:T(8,128)S(1)} %bitcast.127, f32[1,16,34,1024]{3,2,1,0:T(8,128)} %get-tuple-element.38, f32[1,16,34,1024]{3,2,1,0:T(8,128)} %get-tuple-element.37, f32[1,16,34,1024]{3,2,1,0:T(8,128)} %get-tuple-element.36, ...), kind=kLoop, calls=%fused_computation.24 | loop fusion | flops 11010048 | bytes 26869760 | tf_op jit(solution)/shard_map/add | solution.py:75
  54.0 1.1 pad_maximum_fusion.4
  55.5 5.4 %collective-permute-start.2 = (f32[3,16,1,1024]{3,2,1,0:T(1,128)S(1)}, f32[3,16,1,1024]{3,2,1,0:T(1,128)S(1)}, u32[]{:S(2)}, u32[]{:S(2)}) collective-permute-start(f32[3,16,1,1024]{3,2,1,0:T(1,128)S(1)} %get-tuple-element.19), channel_id=1, source_target_pairs={{0,1},{1,2},{2,3},{3,4},{4,5},{5,6},{6,7},{8,9},{9,10},{10,11},{11... | collective-permute-start | bytes 589832 | tf_op jit(solution)/shard_map/ppermute | solution.py:20
  61.0 2.1 %collective-permute-start.3 = (f32[3,16,1,1024]{3,2,1,0:T(1,128)S(1)}, f32[3,16,1,1024]{3,2,1,0:T(1,128)S(1)}, u32[]{:S(2)}, u32[]{:S(2)}) collective-permute-start(f32[3,16,1,1024]{3,2,1,0:T(1,128)S(1)} %get-tuple-element.20), channel_id=1, source_target_pairs={{1,0},{2,1},{3,2},{4,3},{5,4},{6,5},{7,6},{9,8},{10,9},{11,10},{12... | collective-permute-start | bytes 589832 | tf_op jit(solution)/shard_map/ppermute | solution.py:22
  63.1 1.6 %collective-permute-done.2 = f32[3,16,1,1024]{3,2,1,0:T(1,128)S(1)} collective-permute-done((f32[3,16,1,1024]{3,2,1,0:T(1,128)S(1)}, f32[3,16,1,1024]{3,2,1,0:T(1,128)S(1)}, u32[]{:S(2)}, u32[]{:S(2)}) %collective-permute-start.2) | collective-permute-done | bytes 196640 | tf_op jit(solution)/shard_map/ppermute | solution.py:20
  64.7 4.7 %collective-permute-done.3 = f32[3,16,1,1024]{3,2,1,0:T(1,128)S(1)} collective-permute-done((f32[3,16,1,1024]{3,2,1,0:T(1,128)S(1)}, f32[3,16,1,1024]{3,2,1,0:T(1,128)S(1)}, u32[]{:S(2)}, u32[]{:S(2)}) %collective-permute-start.3) | collective-permute-done | bytes 196640 | tf_op jit(solution)/shard_map/ppermute | solution.py:22
  69.5 1.8 %fusion.3 = f32[3,16,34,1024]{3,2,1,0:T(8,128)S(1)} fusion(f32[3,1,32,1024]{3,2,1,0:T(8,128)S(1)} %get-tuple-element.45, f32[3,1,32,1024]{3,2,1,0:T(8,128)S(1)} %copy-done.2, f32[3,16,1,1024]{3,2,1,0:T(1,128)S(1)} %collective-permute-done.3, f32[3,14,32,1024]{3,2,1,0:T(8,128)S(1)} %fusion.13, f32[3,16,1,1024]{3,2,1,0:T(1,128)S(1)} %collective-permute-done.2), kind=kLoop, calls=%fused_computation.11 | loop fusion | flops 6684672 | bytes 13369344 | tf_op jit(solution)/shard_map/concatenate | solution.py:18
  71.3 2.7 %slice_bitcast_fusion.7 = (f32[15,34,1024]{2,1,0:T(8,128)}, f32[15,34,1024]{2,1,0:T(8,128)}) fusion(f32[3,16,34,1024]{3,2,1,0:T(8,128)S(1)} %fusion.3), kind=kLoop, calls=%fused_computation.46 | loop fusion | bytes 8355840 | tf_op jit(solution)/shard_map/slice | solution.py:40
  74.0 1.5 %slice_bitcast_fusion.2 = (f32[16,34,1024]{2,1,0:T(8,128)S(1)}, f32[16,34,1024]{2,1,0:T(8,128)S(1)}, f32[16,34,1024]{2,1,0:T(8,128)S(1)}) fusion(f32[3,16,34,1024]{3,2,1,0:T(8,128)S(1)} %fusion.3), kind=kLoop, calls=%fused_computation.28 | loop fusion | bytes 13369344 | tf_op jit(solution)/shard_map/squeeze | solution.py:62
  75.5 1.9 %slice.268 = f32[16,33,1024]{2,1,0:T(8,128)} slice(f32[16,34,1024]{2,1,0:T(8,128)S(1)} %get-tuple-element.7), slice={[0:16], [1:34], [0:1024]} | slice | bytes 4325376 | tf_op jit(solution)/shard_map/slice | solution.py:40
  77.4 2.3 %slice.266 = f32[16,34,1023]{2,1,0:T(8,128)} slice(f32[16,34,1024]{2,1,0:T(8,128)S(1)} %get-tuple-element.7), slice={[0:16], [0:34], [1:1024]} | slice | bytes 4452096 | tf_op jit(solution)/shard_map/slice | solution.py:40
  79.6 2.2 %slice.260 = f32[16,34,1023]{2,1,0:T(8,128)} slice(f32[16,34,1024]{2,1,0:T(8,128)S(1)} %get-tuple-element.6), slice={[0:16], [0:34], [1:1024]} | slice | bytes 4452096 | tf_op jit(solution)/shard_map/slice | solution.py:40
  81.9 1.9 %slice.262 = f32[16,33,1024]{2,1,0:T(8,128)} slice(f32[16,34,1024]{2,1,0:T(8,128)S(1)} %get-tuple-element.8), slice={[0:16], [1:34], [0:1024]} | slice | bytes 4325376 | tf_op jit(solution)/shard_map/slice | solution.py:40
  83.7 6.9 %subtract_subtract_fusion.2 = (f32[16,34,1024]{2,1,0:T(8,128)S(1)}, f32[16,34,1024]{2,1,0:T(8,128)S(1)}, f32[16,34,1024]{2,1,0:T(8,128)S(1)}) fusion(f32[16,33,1024]{2,1,0:T(8,128)} %slice.262, f32[16,34,1023]{2,1,0:T(8,128)} %slice.260, f32[3,16,34,1024]{3,2,1,0:T(8,128)S(1)} %fusion.3, f32[16,34,1023]{2,1,0:T(8,128)} %slice.266, ...), kind=kLoop, calls=%fused_computation.38 | loop fusion | flops 5013504 | bytes 26324736 | tf_op jit(solution)/shard_map/sub | solution.py:65
  90.6 1.6 %slice.267 = f32[15,34,1024]{2,1,0:T(8,128)} slice(f32[16,34,1024]{2,1,0:T(8,128)S(1)} %get-tuple-element.4), slice={[0:15], [0:34], [0:1024]} | slice | bytes 4177920 | tf_op jit(solution)/shard_map/slice | solution.py:54
  92.3 1.7 %slice.270 = f32[15,34,1024]{2,1,0:T(8,128)} slice(f32[16,34,1024]{2,1,0:T(8,128)S(1)} %get-tuple-element.5), slice={[0:15], [0:34], [0:1024]} | slice | bytes 4177920 | tf_op jit(solution)/shard_map/slice | solution.py:54
  93.9 7.3 %subtract_bitcast_fusion.2 = (f32[1,16,34,1024]{3,2,1,0:T(8,128)}, f32[1,16,34,1024]{3,2,1,0:T(8,128)}, f32[1,16,34,1024]{3,2,1,0:T(8,128)}) fusion(f32[16,34,1024]{2,1,0:T(8,128)S(1)} %get-tuple-element.4, f32[15,34,1024]{2,1,0:T(8,128)} %slice.267, f32[16,34,1024]{2,1,0:T(8,128)S(1)} %get-tuple-element.3, f32[16,33,1024]{2,1,0:T(8,128)S(1)} %bitcast.120, ...), kind=kLoop, calls=%fused_computation.36 | loop fusion | flops 5013504 | bytes 26324736 | tf_op jit(solution)/shard_map/stack | solution.py:69
  101.3 4.9 %fusion.8 = f32[3,14,32,1024]{3,2,1,0:T(8,128)S(1)} fusion(f32[3,14,32,1024]{3,2,1,0:T(8,128)S(1)} %fusion.13, f32[3,14,32,1024]{3,2,1,0:T(8,128)S(1)} %bitcast.129, f32[1,16,34,1024]{3,2,1,0:T(8,128)} %get-tuple-element.35, f32[1,16,34,1024]{3,2,1,0:T(8,128)} %get-tuple-element.34, f32[1,16,34,1024]{3,2,1,0:T(8,128)} %get-tuple-element.33, ...), kind=kLoop, calls=%fused_computation.17 | loop fusion | flops 11010048 | bytes 26869760 | tf_op jit(solution)/shard_map/add | solution.py:75
  106.6 2.0 %copy-done.3 = f32[3,14,32,1024]{3,2,1,0:T(8,128)} copy-done((f32[3,14,32,1024]{3,2,1,0:T(8,128)}, f32[3,14,32,1024]{3,2,1,0:T(8,128)S(1)}, u32[]{:S(2)}) %copy-start.3) | copy-done | bytes 5505048
  108.7 5.3 %collective-permute-start.4 = (f32[2,4,2,1,1024]{4,3,1,0,2:T(1,128)S(1)}, f32[2,4,2,1,1024]{4,3,1,0,2:T(1,128)S(1)}, u32[]{:S(2)}, u32[]{:S(2)}) collective-permute-start(f32[2,4,2,1,1024]{4,3,1,0,2:T(1,128)S(1)} %get-tuple-element.39), channel_id=1, source_target_pairs={{0,1},{1,2},{2,3},{3,4},{4,5},{5,6},{6,7},{8,9},{9,10},{10,11},{11... | collective-permute-start | bytes 196616 | tf_op jit(solution)/shard_map/ppermute | solution.py:20
  114.1 2.1 %collective-permute-start.5 = (f32[2,4,2,1,1024]{4,3,1,0,2:T(1,128)S(1)}, f32[2,4,2,1,1024]{4,3,1,0,2:T(1,128)S(1)}, u32[]{:S(2)}, u32[]{:S(2)}) collective-permute-start(f32[2,4,2,1,1024]{4,3,1,0,2:T(1,128)S(1)} %get-tuple-element.40), channel_id=1, source_target_pairs={{1,0},{2,1},{3,2},{4,3},{5,4},{6,5},{7,6},{9,8},{10,9},{11,10},{12... | collective-permute-start | bytes 196616 | tf_op jit(solution)/shard_map/ppermute | solution.py:22
  116.3 3.7 %collective-permute-done.5 = f32[2,4,2,1,1024]{4,3,1,0,2:T(1,128)S(1)} collective-permute-done((f32[2,4,2,1,1024]{4,3,1,0,2:T(1,128)S(1)}, f32[2,4,2,1,1024]{4,3,1,0,2:T(1,128)S(1)}, u32[]{:S(2)}, u32[]{:S(2)}) %collective-permute-start.5) | collective-permute-done | bytes 65568 | tf_op jit(solution)/shard_map/ppermute | solution.py:22
  121.0 0.4 slice.279
  121.4 1.1 subtract_subtract_fusion.6
  123.2 1.2 subtract_bitcast_fusion.7
  124.3 1.8 %fusion.16 = (f32[1,2,4,2,32,1024]{5,4,3,2,1,0:T(8,128)}, f32[2,2,32,1024]{3,2,1,0:T(8,128)S(1)}) fusion(f32[2,4,1,34,1024]{4,3,2,1,0:T(8,128)S(1)} %get-tuple-element.28, f32[2,4,1,34,1024]{4,3,2,1,0:T(8,128)S(1)} %get-tuple-element.27, f32[4]{0:T(128)S(1)} %copy-done.6), kind=kLoop, calls=%fused_computation.54 | loop fusion | flops 1966080 | bytes 4849680 | tf_op jit(solution)/shard_map/broadcast_in_dim | solution.py:112
  126.3 5.0 %collective-permute-start.6 = (f32[2,32,1024]{2,1,0:T(8,128)S(1)}, f32[2,32,1024]{2,1,0:T(8,128)S(1)}, u32[]{:S(2)}, u32[]{:S(2)}) collective-permute-start(f32[2,32,1024]{2,1,0:T(8,128)S(1)} %get-tuple-element.41), channel_id=1, source_target_pairs={{0,8},{8,16},{16,24},{1,9},{9,17},{17,25},{2,10},{10,18},{18,26},{... | collective-permute-start | bytes 786440 | tf_op jit(solution)/shard_map/ppermute | solution.py:32
  131.2 1.9 %collective-permute-start.7 = (f32[2,32,1024]{2,1,0:T(8,128)S(1)}, f32[2,32,1024]{2,1,0:T(8,128)S(1)}, u32[]{:S(2)}, u32[]{:S(2)}) collective-permute-start(f32[2,32,1024]{2,1,0:T(8,128)S(1)} %get-tuple-element.42), channel_id=1, source_target_pairs={{8,0},{16,8},{24,16},{9,1},{17,9},{25,17},{10,2},{18,10},{26,18},{... | collective-permute-start | bytes 786440 | tf_op jit(solution)/shard_map/ppermute | solution.py:32
  133.1 1.4 collective-permute-done.6
  134.5 4.4 %collective-permute-done.7 = f32[2,32,1024]{2,1,0:T(8,128)S(1)} collective-permute-done((f32[2,32,1024]{2,1,0:T(8,128)S(1)}, f32[2,32,1024]{2,1,0:T(8,128)S(1)}, u32[]{:S(2)}, u32[]{:S(2)}) %collective-permute-start.7) | collective-permute-done | bytes 262176 | tf_op jit(solution)/shard_map/ppermute | solution.py:32
  138.9 0.8 maximum_bitcast_fusion
  (43 shorter events, 3.3 us)
Async XLA Ops:
  1.8 15.6 %copy-start.1 = (f32[3,1,32,1024]{3,2,1,0:T(8,128)}, f32[3,1,32,1024]{3,2,1,0:T(8,128)S(1)}, u32[]{:S(2)}) copy-start(f32[3,1,32,1024]{3,2,1,0:T(8,128)S(1)} %get-tuple-element.46) | copy-start | bytes 1179652
  1.8 15.6 %slice-start = ((s8[5505024]{0:T(1024)(128)(4,1)}), s8[4194304]{0:T(1024)(128)(4,1)S(1)}, s32[]{:S(2)}) async-start(s8[5505024]{0:T(1024)(128)(4,1)} %bitcast.116), calls=%async_computation | async-start | bytes 8388608
  1.8 9.3 %copy-start = (f32[14,32,1024]{2,1,0:T(8,128)S(1)}, f32[14,32,1024]{2,1,0:T(8,128)}, u32[]{:S(2)}) copy-start(f32[14,32,1024]{2,1,0:T(8,128)} %param.9) | copy-start | bytes 5505028
  1.8 15.5 %slice-start.1 = ((s8[5505024]{0:T(1024)(128)(4,1)}), s8[1310720]{0:T(1024)(128)(4,1)S(1)}, s32[]{:S(2)}) async-start(s8[5505024]{0:T(1024)(128)(4,1)} %bitcast.116), calls=%async_computation.1 | async-start | bytes 2621440
  5.8 7.7 %collective-permute-start = (f32[3,16,1,1024]{3,2,1,0:T(1,128)S(1)}, f32[3,16,1,1024]{3,2,1,0:T(1,128)S(1)}, u32[]{:S(2)}, u32[]{:S(2)}) collective-permute-start(f32[3,16,1,1024]{3,2,1,0:T(1,128)S(1)} %get-tuple-element.21), channel_id=1, source_target_pairs={{0,1},{1,2},{2,3},{3,4},{4,5},{5,6},{6,7},{8,9},{9,10},{10,11},{11... | collective-permute-start | bytes 589832 | tf_op jit(solution)/shard_map/ppermute | solution.py:20
  8.9 8.4 %collective-permute-start.1 = (f32[3,16,1,1024]{3,2,1,0:T(1,128)S(1)}, f32[3,16,1,1024]{3,2,1,0:T(1,128)S(1)}, u32[]{:S(2)}, u32[]{:S(2)}) collective-permute-start(f32[3,16,1,1024]{3,2,1,0:T(1,128)S(1)} %get-tuple-element.22), channel_id=1, source_target_pairs={{1,0},{2,1},{3,2},{4,3},{5,4},{6,5},{7,6},{9,8},{10,9},{11,10},{12... | collective-permute-start | bytes 589832 | tf_op jit(solution)/shard_map/ppermute | solution.py:22
  41.9 7.4 %slice-start.2 = ((s8[5505024]{0:T(1024)(128)(4,1)}), s8[4194304]{0:T(1024)(128)(4,1)S(1)}, s32[]{:S(2)}) async-start(s8[5505024]{0:T(1024)(128)(4,1)} %bitcast.126), calls=%async_computation.2 | async-start | bytes 8388608
  41.9 7.4 %slice-start.3 = ((s8[5505024]{0:T(1024)(128)(4,1)}), s8[1310720]{0:T(1024)(128)(4,1)S(1)}, s32[]{:S(2)}) async-start(s8[5505024]{0:T(1024)(128)(4,1)} %bitcast.126), calls=%async_computation.3 | async-start | bytes 2621440
  49.3 4.8 %copy-start.2 = (f32[3,1,32,1024]{3,2,1,0:T(8,128)S(1)}, f32[3,1,32,1024]{3,2,1,0:T(8,128)}, u32[]{:S(2)}) copy-start(f32[3,1,32,1024]{3,2,1,0:T(8,128)} %copy-done.1) | copy-start | bytes 1179652
  55.5 9.2 %collective-permute-start.2 = (f32[3,16,1,1024]{3,2,1,0:T(1,128)S(1)}, f32[3,16,1,1024]{3,2,1,0:T(1,128)S(1)}, u32[]{:S(2)}, u32[]{:S(2)}) collective-permute-start(f32[3,16,1,1024]{3,2,1,0:T(1,128)S(1)} %get-tuple-element.19), channel_id=1, source_target_pairs={{0,1},{1,2},{2,3},{3,4},{4,5},{5,6},{6,7},{8,9},{9,10},{10,11},{11... | collective-permute-start | bytes 589832 | tf_op jit(solution)/shard_map/ppermute | solution.py:20
  61.0 8.5 %collective-permute-start.3 = (f32[3,16,1,1024]{3,2,1,0:T(1,128)S(1)}, f32[3,16,1,1024]{3,2,1,0:T(1,128)S(1)}, u32[]{:S(2)}, u32[]{:S(2)}) collective-permute-start(f32[3,16,1,1024]{3,2,1,0:T(1,128)S(1)} %get-tuple-element.20), channel_id=1, source_target_pairs={{1,0},{2,1},{3,2},{4,3},{5,4},{6,5},{7,6},{9,8},{10,9},{11,10},{12... | collective-permute-start | bytes 589832 | tf_op jit(solution)/shard_map/ppermute | solution.py:22
  93.9 7.4 %slice-start.4 = ((s8[5505024]{0:T(1024)(128)(4,1)}), s8[4194304]{0:T(1024)(128)(4,1)S(1)}, s32[]{:S(2)}) async-start(s8[5505024]{0:T(1024)(128)(4,1)} %bitcast.128), calls=%async_computation.4 | async-start | bytes 8388608
  93.9 7.4 %slice-start.5 = ((s8[5505024]{0:T(1024)(128)(4,1)}), s8[1310720]{0:T(1024)(128)(4,1)S(1)}, s32[]{:S(2)}) async-start(s8[5505024]{0:T(1024)(128)(4,1)} %bitcast.128), calls=%async_computation.5 | async-start | bytes 2621440
  101.3 4.9 %copy-start.4 = (f32[1,2,4,2,32,1024]{5,4,3,2,1,0:T(8,128)S(1)}, f32[1,2,4,2,32,1024]{5,4,3,2,1,0:T(8,128)}, u32[]{:S(2)}) copy-start(f32[1,2,4,2,32,1024]{5,4,3,2,1,0:T(8,128)} %param.11) | copy-start | bytes 6291460
  101.3 4.9 %copy-start.5 = (f32[4]{0:T(128)S(1)}, f32[4]{0:T(128)}, u32[]{:S(2)}) copy-start(f32[4]{0:T(128)} %constant.11.clone) | copy-start | bytes 52
  106.2 2.4 %copy-start.3 = (f32[3,14,32,1024]{3,2,1,0:T(8,128)}, f32[3,14,32,1024]{3,2,1,0:T(8,128)S(1)}, u32[]{:S(2)}) copy-start(f32[3,14,32,1024]{3,2,1,0:T(8,128)S(1)} %fusion.8) | copy-start | bytes 16515076
  108.7 7.5 %collective-permute-start.4 = (f32[2,4,2,1,1024]{4,3,1,0,2:T(1,128)S(1)}, f32[2,4,2,1,1024]{4,3,1,0,2:T(1,128)S(1)}, u32[]{:S(2)}, u32[]{:S(2)}) collective-permute-start(f32[2,4,2,1,1024]{4,3,1,0,2:T(1,128)S(1)} %get-tuple-element.39), channel_id=1, source_target_pairs={{0,1},{1,2},{2,3},{3,4},{4,5},{5,6},{6,7},{8,9},{9,10},{10,11},{11... | collective-permute-start | bytes 196616 | tf_op jit(solution)/shard_map/ppermute | solution.py:20
  114.1 5.9 %collective-permute-start.5 = (f32[2,4,2,1,1024]{4,3,1,0,2:T(1,128)S(1)}, f32[2,4,2,1,1024]{4,3,1,0,2:T(1,128)S(1)}, u32[]{:S(2)}, u32[]{:S(2)}) collective-permute-start(f32[2,4,2,1,1024]{4,3,1,0,2:T(1,128)S(1)} %get-tuple-element.40), channel_id=1, source_target_pairs={{1,0},{2,1},{3,2},{4,3},{5,4},{6,5},{7,6},{9,8},{10,9},{11,10},{12... | collective-permute-start | bytes 196616 | tf_op jit(solution)/shard_map/ppermute | solution.py:22
  123.2 1.2 copy-start.6
  126.3 8.3 %collective-permute-start.6 = (f32[2,32,1024]{2,1,0:T(8,128)S(1)}, f32[2,32,1024]{2,1,0:T(8,128)S(1)}, u32[]{:S(2)}, u32[]{:S(2)}) collective-permute-start(f32[2,32,1024]{2,1,0:T(8,128)S(1)} %get-tuple-element.41), channel_id=1, source_target_pairs={{0,8},{8,16},{16,24},{1,9},{9,17},{17,25},{2,10},{10,18},{18,26},{... | collective-permute-start | bytes 786440 | tf_op jit(solution)/shard_map/ppermute | solution.py:32
  131.2 7.7 %collective-permute-start.7 = (f32[2,32,1024]{2,1,0:T(8,128)S(1)}, f32[2,32,1024]{2,1,0:T(8,128)S(1)}, u32[]{:S(2)}, u32[]{:S(2)}) collective-permute-start(f32[2,32,1024]{2,1,0:T(8,128)S(1)} %get-tuple-element.42), channel_id=1, source_target_pairs={{8,0},{16,8},{24,16},{9,1},{17,9},{25,17},{10,2},{18,10},{26,18},{... | collective-permute-start | bytes 786440 | tf_op jit(solution)/shard_map/ppermute | solution.py:32
where the time goes:
time: 140 us
  other arithmetic  52.5 us (38%)
  local copies, waits for them, and re-layouts  37.1 us (26%)
  starting transfers between devices  27.2 us (19%)
  waiting for transfers between devices  21.9 us (16%)
    slice x14, local copies, waits for them, and re-layouts, forward_diff(): lax.slice_in_dim(values, 1, count, axis=along)  23 us
    another operation x2, other arithmetic, curl_curl(): return jnp.stack([image_x, image_y, image_z])[:, 1:-1, 1:-1, :]  14.7 us
    ppermute x3, starting transfers between devices, extended(): lax.ppermute(tail, axis, [(i, (i + 1) % count) for i in range(ends)])  14 us
    sub x2, other arithmetic, curl_curl(): flux_z = forward_diff(field_y, 2) - forward_diff(field_x, 1)  13.9 us
    ppermute x3, waiting for transfers between devices, extended(): lax.ppermute(head, axis, [((i + 1) % count, i) for i in range(ends)])  12.4 us
    add x3, other arithmetic, update(): return interior + 0.5 * residual / (mass_shift + 4.0)  9.85 us
    ppermute x2, starting transfers between devices, from_behind(): return lax.ppermute(block, axis, route)  6.87 us
    slice x4, local copies, waits for them, and re-layouts, backward_diff(): lax.slice_in_dim(values, 0, count - 1, axis=along)  6.58 us
  transfers between devices with their start and end apart: 8, of which 7 were waited for; matrix products, arithmetic and copies ran while one was open for 0% of the time, Pallas kernels for 0%

commit v1 on v0

v1 whole, which is shorter than its diff:
```python
import functools
import math

import jax
import jax.numpy as jnp
from jax import lax
from jax.experimental import pallas as pl
from jax.experimental.pallas import tpu as pltpu
from jax.sharding import PartitionSpec as P

pade_weights = [2.0 / 9.0 * math.sin(j * math.pi / 9.0) ** 2 for j in range(1, 5)]
pade_decays = [math.cos(j * math.pi / 9.0) ** 2 for j in range(1, 5)]
TERMS = 4
SUB, LANE = 8, 128
F32 = jnp.float32
HBM = pl.BlockSpec(memory_space=pltpu.HBM)
VM = pl.BlockSpec(memory_space=pltpu.VMEM)


def params(mib):
    return pltpu.CompilerParams(vmem_limit_bytes=mib << 20)


def shape(*dims):
    return jax.ShapeDtypeStruct(dims, F32)


def cost(flops, count):
    return pl.CostEstimate(flops=flops, bytes_accessed=count, transcendentals=0)


def vm(*dims):
    return pltpu.VMEM(dims, F32)


def row_next(row):
    n = row.shape[1]
    at = lax.broadcasted_iota(jnp.int32, row.shape, 1)
    return jnp.where(at == n - 1, 0.0, pltpu.roll(row, n - 1, 1))


def row_prev(row):
    at = lax.broadcasted_iota(jnp.int32, row.shape, 1)
    return jnp.where(at == 0, 0.0, pltpu.roll(row, 1, 1))


def pack_rows(nz, first, last, top_y, send_up, send_down):
    here = last(0)
    for z in range(nz):
        low_x, low_z = first(z)
        send_down[z, 0:1, :] = low_x
        send_down[z, 1:2, :] = low_z
        x, y, zc = here
        here = last(z + 1) if z + 1 < nz else None
        y_above = top_y() if here is None else here[1]
        send_up[z, 0:1, :] = row_next(y) - y + x
        send_up[z, 1:2, :] = zc + (y_above - y)


def fixed_first(field, weight, low, z):
    w = weight[z, 0:1, :]
    return field[0, z, 0:1, :] + w * low[z, 0:1, :], field[2, z, 0:1, :] + w * low[z, 1:2, :]


def fixed_last(field, weight, high, z, ny):
    end = slice(ny - 1, ny)
    w = weight[z, end, :]
    hx, hz = high[z, 0:1, :], high[z, 1:2, :]
    rise = hz - high[z - 1, 1:2, :] if z else hz
    return (
        field[0, z, end, :] + w * hx,
        field[1, z, end, :] - w * (rise + (hx - row_prev(hx))),
        field[2, z, end, :] + w * hz,
    )


def lane_masks():
    lane = lax.broadcasted_iota(jnp.int32, (SUB, LANE), 1)
    sub = lax.broadcasted_iota(jnp.int32, (SUB, LANE), 0)
    return lane == 0, lane == LANE - 1, sub == 0, sub == SUB - 1


def tile_at(i, c):
    return slice(i * SUB, (i + 1) * SUB), slice(c * LANE, (c + 1) * LANE)


def pack_kernel(dims, electric, faces, send_up, send_down, first, last, top, sem):
    nz, ny, nx = dims
    copies = [
        pltpu.make_async_copy(electric.at[:, :, pl.ds(ny - SUB, SUB)], last, sem.at[0]),
        pltpu.make_async_copy(electric.at[:, :, pl.ds(0, SUB)], first, sem.at[1]),
        pltpu.make_async_copy(faces.at[0, 1, 1, pl.ds(ny - SUB, SUB)], top, sem.at[2]),
    ]
    for copy in copies:
        copy.start()
    for copy in copies:
        copy.wait()
    pack_rows(
        nz,
        lambda z: (first[0, z, 0:1, :], first[2, z, 0:1, :]),
        lambda z: tuple(last[k, z, SUB - 1 : SUB, :] for k in range(3)),
        lambda: top[SUB - 1 : SUB, :],
        send_up,
        send_down,
    )


def sweep_planes(load, store, current, weight, ghost, hx_s, hy_s, dims, before_plane, from_mass):
    nz, ny, nx = dims
    rows, cols = ny // SUB, nx // LANE
    is_first_lane, is_last_lane, is_first_sub, is_last_sub = lane_masks()

    for i in range(rows):
        for c in range(cols):
            r, s = tile_at(i, c)
            hx_s[r, s] = ghost[1, r, s] - load(1, 0, i, c)
            hy_s[r, s] = load(0, 0, i, c) - ghost[0, r, s]

    def plane(z, carry):
        before_plane(z)

        def left(k, i, c):
            return pltpu.roll(load(k, z, i, c), LANE - 1, 1)

        lefts = {(k, i): left(k, i, 0) for k in (1, 2) for i in range(rows)}
        right_y, right_z = {}, {}
        for c in range(cols):
            here = [[load(k, z, i, c) for k in range(3)] for i in range(rows)]
            ups = [{k: pltpu.roll(here[i][k], SUB - 1, 0) for k in (0, 2)} for i in range(rows)]
            down_x = down_z = None
            for i in range(rows):
                r, s = tile_at(i, c)

                def y_next(k):
                    return jnp.where(is_last_sub, ups[i + 1][k] if i + 1 < rows else 0.0, ups[i][k])

                def x_next(k):
                    after = left(k, i, c + 1) if c + 1 < cols else 0.0
                    value = jnp.where(is_last_lane, after, lefts[k, i])
                    lefts[k, i] = after
                    return value

                ex, ey, ez = here[i]
                hx = (y_next(2) - ez) - (load(1, z + 1, i, c) - ey)
                hy = (load(0, z + 1, i, c) - ex) - (x_next(2) - ez)
                hz = (x_next(1) - ey) - (y_next(0) - ex)
                hx_low, hy_low = hx_s[r, s], hy_s[r, s]
                hx_s[r, s] = hx
                hy_s[r, s] = hy
                dx = pltpu.roll(hx, 1, 0)
                dz = pltpu.roll(hz, 1, 0)
                hx_y = jnp.where(is_first_sub, ez if i == 0 else down_x, dx)
                hz_y = jnp.where(is_first_sub, -ex if i == 0 else down_z, dz)
                down_x, down_z = dx, dz
                ry = pltpu.roll(hy, 1, 1)
                rz = pltpu.roll(hz, 1, 1)
                hy_x = jnp.where(is_first_lane, 0.0 if c == 0 else right_y[i], ry)
                hz_x = jnp.where(is_first_lane, 0.0 if c == 0 else right_z[i], rz)
                right_y[i], right_z[i] = ry, rz
                cx = (hz - hz_y) - (hy - hy_low)
                cy = (hx - hx_low) - (hz - hz_x)
                cz = (hy - hy_x) - (hx - hx_y)
                w = weight[z, r, s]
                if from_mass:
                    w = 0.5 / (w + 4.0)
                    weight[z, r, s] = w
                keep = 4.0 * w + 0.5
                store(0, z, i, c, keep * ex + w * (current[0, z, r, s] - cx))
                store(1, z, i, c, keep * ey + w * (current[1, z, r, s] - cy))
                store(2, z, i, c, keep * ez + w * (current[2, z, r, s] - cz))
        return carry

    lax.fori_loop(0, nz, plane, 0)


def first_kernel(
    dims, electric, current_h, mass, faces, aux_h,
    field, current, weight, ghost, aux, hx_s, hy_s, field_sem, current_sem, weight_sem, face_sem,
):
    nz, ny, nx = dims
    copy = pltpu.make_async_copy

    def field_copy(z):
        return copy(electric.at[:, pl.ds(z, 1)], field.at[:, pl.ds(z, 1)], field_sem.at[z])

    def current_copy(z):
        return copy(current_h.at[:, pl.ds(z, 1)], current.at[:, pl.ds(z, 1)], current_sem.at[z])

    def weight_copy(z):
        return copy(mass.at[pl.ds(z, 1)], weight.at[pl.ds(z, 1)], weight_sem.at[z])

    low_copy = copy(faces.at[0, 0], ghost, face_sem.at[0])
    high_copies = [copy(faces.at[0, 1, k], field.at[k, nz], face_sem.at[1 + k]) for k in range(2)]
    aux_copy = copy(aux_h.at[0], aux, face_sem.at[3])
    low_copy.start()
    field_copy(0).start()

    def start(z, carry):
        field_copy(z + 1).start()
        current_copy(z).start()
        weight_copy(z).start()
        return carry

    lax.fori_loop(0, nz - 1, start, 0)
    current_copy(nz - 1).start()
    weight_copy(nz - 1).start()
    for high in high_copies:
        high.start()
    aux_copy.start()

    def before_plane(z):
        @pl.when(z + 1 < nz)
        def _():
            field_copy(z + 1).wait()

        @pl.when(z + 1 == nz)
        def _():
            for high in high_copies:
                high.wait()

        current_copy(z).wait()
        weight_copy(z).wait()

    def load(k, z, i, c):
        r, s = tile_at(i, c)
        return field[k, z, r, s]

    def store(k, z, i, c, value):
        r, s = tile_at(i, c)
        field[k, z, r, s] = value

    low_copy.wait()
    field_copy(0).wait()
    sweep_planes(load, store, current, weight, ghost, hx_s, hy_s, dims, before_plane, True)
    aux_copy.wait()


def fix_pack_kernel(dims, field, weight, low, high, head, tail, send_up, send_down):
    nz, ny, nx = dims
    for z in range(nz):
        head[z, 0:1, :], head[z, 1:2, :] = fixed_first(field, weight, low, z)
        x, y, zc = fixed_last(field, weight, high, z, ny)
        tail[z, 0:1, :], tail[z, 1:2, :], tail[z, 2:3, :] = x, y, zc
    end = slice(ny - 1, ny)
    head[nz, 0:1, :] = field[0, nz, 0:1, :]
    tail[nz, 0:1, :] = field[0, nz, end, :]
    tail[nz, 1:2, :] = field[1, nz, end, :]
    pack_rows(
        nz,
        lambda z: (head[z, 0:1, :], head[z, 1:2, :]),
        lambda z: tuple(tail[z, k : k + 1, :] for k in range(3)),
        lambda: tail[nz, 1:2, :],
        send_up,
        send_down,
    )


def second_kernel(dims, old, current, weight, ghost, head, tail, field, hx_s, hy_s):
    nz, ny, nx = dims
    rows = ny // SUB
    _, _, is_first_sub, is_last_sub = lane_masks()

    def load(k, z, i, c):
        r, s = tile_at(i, c)
        value = old[k, z, r, s]
        if i == 0 and k != 1:
            value = jnp.where(is_first_sub, head[z, k // 2 : k // 2 + 1, s], value)
        if i == rows - 1:
            value = jnp.where(is_last_sub, tail[z, k : k + 1, s], value)
        return value

    def store(k, z, i, c, value):
        r, s = tile_at(i, c)
        field[k, z, r, s] = value

    sweep_planes(load, store, current, weight, ghost, hx_s, hy_s, dims, lambda z: None, False)


def fix_trace_kernel(dims, field, weight, aux, low, high, head, tail, traces, send_up, send_down):
    nz, ny, nx = dims
    end = slice(ny - 1, ny)
    for side in range(2):
        z = (nz - 1) * side
        for k in range(2):
            traces[side, k] = field[k, z]
    for z in range(nz):
        head[z, 0:1, :], head[z, 1:2, :] = fixed_first(field, weight, low, z)
        x, y, zc = fixed_last(field, weight, high, z, ny)
        tail[z, 0:1, :], tail[z, 1:2, :], tail[z, 2:3, :] = x, y, zc
        if z in (0, nz - 1):
            side = 0 if z == 0 else 1
            traces[side, 0, 0:1, :] = head[z, 0:1, :]
            traces[side, 0, end, :] = x
            traces[side, 1, end, :] = y
    for side in range(2):
        for k in range(2):
            first = traces[side, k, 0:1, :]
            last = traces[side, k, end, :]
            for j in range(TERMS):
                at = side * TERMS + j
                send_down[at, k : k + 1, :] = first - pade_decays[j] * aux[side, j, k, 0:1, :]
                send_up[at, k : k + 1, :] = last - pade_decays[j] * aux[side, j, k, end, :]


def surface_kernel(dims, field, head, tail, traces, aux, smoothed, fresh, outgoing, edges, sem):
    nz, ny, nx = dims
    rows, cols = ny // SUB, nx // LANE
    is_first_lane, is_last_lane, is_first_sub, is_last_sub = lane_masks()
    spans = [(0, SUB), (ny - SUB, SUB)]
    middle = pltpu.make_async_copy(
        field.at[:, pl.ds(0, nz), pl.ds(SUB, ny - 2 * SUB)], smoothed.at[:, :, pl.ds(SUB, ny - 2 * SUB)], sem.at[0]
    )
    middle.start()

    def merge(z, carry):
        for c in range(cols):
            s = slice(c * LANE, (c + 1) * LANE)
            for k in range(3):
                value = field[k, z, 0:SUB, s]
                if k != 1:
                    value = jnp.where(is_first_sub, head[z, k // 2 : k // 2 + 1, s], value)
                edges[0, k, z, :, s] = value
                value = field[k, z, ny - SUB : ny, s]
                edges[1, k, z, :, s] = jnp.where(is_last_sub, tail[z, k : k + 1, s], value)
        return carry

    lax.fori_loop(0, nz, merge, 0)
    outer = [
        pltpu.make_async_copy(edges.at[e], smoothed.at[:, :, pl.ds(*spans[e])], sem.at[1 + e]) for e in range(2)
    ]
    for copy in outer:
        copy.start()

    def part(side, carry):
        outgoing[side] = traces[side]

        def term(j, carry):
            decay = weight = F32(0.0)
            for q in range(TERMS):
                decay = jnp.where(j == q, F32(pade_decays[q]), decay)
                weight = jnp.where(j == q, F32(pade_weights[q]), weight)
            for k in range(2):

                def value(i, c):
                    r, s = tile_at(i, c)
                    return traces[side, k, r, s] - decay * aux[side, j, k, r, s]

                column = [value(i, 0) for i in range(rows)]
                lefts = [pltpu.roll(u, LANE - 1, 1) for u in column]
                rights = [0.0] * rows
                for c in range(cols):
                    ups = [pltpu.roll(u, SUB - 1, 0) for u in column]
                    downs = [pltpu.roll(u, 1, 0) for u in column]
                    after = [value(i, c + 1) for i in range(rows)] if c + 1 < cols else None
                    for i in range(rows):
                        r, s = tile_at(i, c)
                        u = column[i]
                        y_next = jnp.where(is_last_sub, ups[i + 1] if i + 1 < rows else 0.0, ups[i])
                        y_prev = jnp.where(is_first_sub, downs[i - 1] if i else 0.0, downs[i])
                        if after is not None:
                            beyond = pltpu.roll(after[i], LANE - 1, 1)
                        else:
                            beyond = u if k == 0 else 0.0
                        x_next = jnp.where(is_last_lane, beyond, lefts[i])
                        lefts[i] = beyond
                        right = pltpu.roll(u, 1, 1)
                        before = rights[i] if c else (u if k == 1 else 0.0)
                        x_prev = jnp.where(is_first_lane, before, right)
                        rights[i] = right
                        new = 0.5 * u - 0.125 * ((y_next + y_prev) + (x_next + x_prev))
                        fresh[side, j, k, r, s] = new
                        outgoing[side, k, r, s] += weight * new
                    column = after
            return carry

        return lax.fori_loop(0, TERMS, term, carry)

    lax.fori_loop(0, 2, part, 0)
    middle.wait()
    for copy in outer:
        copy.wait()


def close_kernel(dims, zero_halo, low, high, outgoing):
    nz, ny, nx = dims
    for side in range(2):
        for k in range(2):
            outgoing[side, k] = zero_halo[side, k]
            for source, r in ((low, slice(0, 1)), (high, slice(ny - 1, ny))):
                total = 0.0
                for j in range(TERMS):
                    total = total + (0.125 * pade_weights[j]) * source[side * TERMS + j, k : k + 1, :]
                outgoing[side, k, r, :] = zero_halo[side, k, r, :] - total


def store_kernel(dims, fresh, low, high, out, edges, sem):
    nz, ny, nx = dims
    inner = pl.ds(SUB, ny - 2 * SUB)
    middle = pltpu.make_async_copy(fresh.at[:, :, :, inner], out.at[0, :, :, :, inner], sem.at[0])
    middle.start()
    _, _, is_first_sub, is_last_sub = lane_masks()
    for side in range(2):
        for j in range(TERMS):
            for k in range(2):
                at = side * TERMS + j
                for c in range(nx // LANE):
                    s = slice(c * LANE, (c + 1) * LANE)
                    first = jnp.where(is_first_sub, 0.125 * low[at, k : k + 1, s], 0.0)
                    last = jnp.where(is_last_sub, 0.125 * high[at, k : k + 1, s], 0.0)
                    edges[0, side, j, k, :, s] = fresh[side, j, k, 0:SUB, s] - first
                    edges[1, side, j, k, :, s] = fresh[side, j, k, ny - SUB : ny, s] - last
    outer = [
        pltpu.make_async_copy(edges.at[e], out.at[0, :, :, :, pl.ds(start, SUB)], sem.at[1 + e])
        for e, start in enumerate((0, ny - SUB))
    ]
    for copy in outer:
        copy.start()
    middle.wait()
    for copy in outer:
        copy.wait()


def shift_up(block, axis):
    count = lax.axis_size(axis)
    return lax.ppermute(block, axis, [(i, i + 1) for i in range(count - 1)])


def shift_down(block, axis):
    count = lax.axis_size(axis)
    return lax.ppermute(block, axis, [(i + 1, i) for i in range(count - 1)])


def shards(electric, current, mass, faces, aux):
    nz, ny, nx = mass.shape
    dims = (nz, ny, nx)
    cells = nz * ny * nx
    bind = functools.partial
    rows_shape = (shape(nz, 2, nx),) * 2
    dma = pltpu.SemaphoreType.DMA
    electric, current, mass, faces, aux = (
        pltpu.with_memory_space_constraint(a, pltpu.HBM) for a in (electric, current, mass, faces, aux)
    )

    up1, down1 = pl.pallas_call(
        bind(pack_kernel, dims),
        out_shape=rows_shape,
        in_specs=[HBM] * 2,
        out_specs=(VM,) * 2,
        scratch_shapes=[vm(3, nz, SUB, nx), vm(3, nz, SUB, nx), vm(SUB, nx), dma((3,))],
        compiler_params=params(12),
        name="pack",
    )(electric, faces)
    low1 = shift_up(up1, "tile")
    high1 = shift_down(down1, "tile")

    field, current_v, weight, ghost, aux_v = pl.pallas_call(
        bind(first_kernel, dims),
        out_shape=(
            shape(3, nz + 1, ny, nx),
            shape(3, nz, ny, nx),
            shape(nz, ny, nx),
            shape(2, ny, nx),
            shape(2, TERMS, 2, ny, nx),
        ),
        in_specs=[HBM] * 5,
        out_specs=(VM,) * 5,
        scratch_shapes=[vm(ny, nx), vm(ny, nx), dma((nz,)), dma((nz,)), dma((nz,)), dma((4,))],
        compiler_params=params(24),
        cost_estimate=cost(45 * cells, 28 * cells),
        name="first_sweep",
    )(electric, current, mass, faces, aux)

    heads, tails = shape(nz + 1, 2, nx), shape(nz + 1, 3, nx)
    head, tail, up2, down2 = pl.pallas_call(
        bind(fix_pack_kernel, dims),
        out_shape=(heads, tails) + rows_shape,
        in_specs=[VM] * 4,
        out_specs=(VM,) * 4,
        compiler_params=params(16),
        name="fix_pack",
    )(field, weight, low1, high1)
    low2 = shift_up(up2, "tile")
    high2 = shift_down(down2, "tile")

    field = pl.pallas_call(
        bind(second_kernel, dims),
        out_shape=shape(3, nz, ny, nx),
        in_specs=[VM] * 6,
        out_specs=VM,
        scratch_shapes=[vm(ny, nx), vm(ny, nx)],
        compiler_params=params(24),
        cost_estimate=cost(40 * cells, 28 * cells),
        name="second_sweep",
    )(field, current_v, weight, ghost, head, tail)

    head, tail, traces, up3, down3 = pl.pallas_call(
        bind(fix_trace_kernel, dims),
        out_shape=(heads, tails, shape(2, 2, ny, nx)) + (shape(2 * TERMS, 2, nx),) * 2,
        in_specs=[VM] * 5,
        out_specs=(VM,) * 5,
        compiler_params=params(16),
        name="fix_trace",
    )(field, weight, aux_v, low2, high2)
    low3 = shift_up(up3, "tile")
    high3 = shift_down(down3, "tile")

    smoothed, fresh, outgoing = pl.pallas_call(
        bind(surface_kernel, dims),
        out_shape=(shape(3, nz, ny, nx), shape(2, TERMS, 2, ny, nx), shape(2, 2, ny, nx)),
        in_specs=[VM] * 5,
        out_specs=(HBM, VM, VM),
        scratch_shapes=[vm(2, 3, nz, SUB, nx), dma((3,))],
        compiler_params=params(24),
        cost_estimate=cost(20 * 16 * ny * nx, 12 * cells),
        name="surface",
    )(field, head, tail, traces, aux_v)

    outgoing = pl.pallas_call(
        bind(close_kernel, dims),
        out_shape=shape(2, 2, ny, nx),
        in_specs=[VM] * 3,
        out_specs=VM,
        compiler_params=params(8),
        name="close",
    )(outgoing, low3, high3)
    from_below = shift_up(outgoing[1], "slab")
    from_above = shift_down(outgoing[0], "slab")

    fresh = pl.pallas_call(
        bind(store_kernel, dims),
        out_shape=shape(1, 2, TERMS, 2, ny, nx),
        in_specs=[VM] * 3,
        out_specs=HBM,
        scratch_shapes=[vm(2, 2, TERMS, 2, SUB, nx), dma((3,))],
        compiler_params=params(8),
        cost_estimate=cost(16 * ny * nx, 8 * 16 * ny * nx),
        name="store",
    )(fresh, low3, high3)
    return smoothed, jnp.stack([from_below, from_above])[None], fresh


def solution(mesh):
    placed = (
        P(None, "slab", "tile", None),
        P(None, "slab", "tile", None),
        P("slab", "tile", None),
        P("slab", None, None, "tile", None),
        P("slab", None, None, None, "tile", None),
    )
    return jax.shard_map(
        shards,
        mesh=mesh,
        in_specs=placed,
        out_specs=(
            P(None, "slab", "tile", None),
            P("slab", None, None, "tile", None),
            P("slab", None, None, None, "tile", None),
        ),
        check_vma=False,
    )
```

time: 140 us -> 51.9 us (0.37)
  other arithmetic: 52.5 us -> 0.84 us
  local copies, waits for them, and re-layouts: 37.1 us -> 0.04 us
  Pallas kernels: 0 us -> 18.3 us
  waiting for transfers between devices: 21.9 us -> 5.92 us
  starting transfers between devices: 27.2 us -> 25.6 us
    slice x21 -> x0, local copies, waits for them, and re-layouts: 30.4 us -> none  [the longest x14 23 us: forward_diff(): lax.slice_in_dim(values, 1, count, axis=along)]
    pallas_call x0 -> x8, Pallas kernels: none -> 18.3 us  [the longest x1 6.76 us: shards(): pl.pallas_call(bind(first_kernel, dims), out_shape=(shape(3, nz + 1, ny,...]
    ppermute x8, waiting for transfers between devices: 21.9 us -> 5.92 us  [the longest x4 5.9 us: shift_down(): return lax.ppermute(block, axis, [(i + 1, i) for i in range(count - 1)])]
    another operation x3 -> x0, other arithmetic: 15.8 us -> none  [the longest x2 14.7 us: curl_curl(): return jnp.stack([image_x, image_y, image_z])[:, 1:-1, 1:-1, :]]
    sub x4 -> x0, other arithmetic: 15.4 us -> none  [the longest x2 13.9 us: curl_curl(): flux_z = forward_diff(field_y, 2) - forward_diff(field_x, 1)]
    add x4 -> x0, other arithmetic: 9.91 us -> none  [the longest x3 9.85 us: update(): return interior + 0.5 * residual / (mass_shift + 4.0)]
    concatenate x5 -> x0, other arithmetic: 8.78 us -> none  [the longest x2 4.64 us: shards(): jnp.concatenate([below_ghost[:, None], local_field, above_ghost[:, None]]...]
    squeeze x5 -> x1, local copies, waits for them, and re-layouts: 4.46 us -> 0.04 us  [shards(): from_below = shift_up(outgoing[1], 'slab')]
  transfers between devices with their start and end apart: 8 -> 8, of which waited for: 7 -> 2; matrix products, arithmetic and copies ran while one was open for 0% -> 0% of each run, Pallas kernels for 0% -> 30%
where the time goes in v1:
time: 51.9 us; the launch traced here: 51.6 us
  starting transfers between devices  25.6 us (49%)
  Pallas kernels  18.3 us (35%)
  waiting for transfers between devices  5.92 us (11%)
  other arithmetic  0.84 us (2%)
  between operations  0.79 us (2%)
    ppermute x4, starting transfers between devices, shift_up(): return lax.ppermute(block, axis, [(i, i + 1) for i in range(count - 1)])  17.8 us
    ppermute x4, starting transfers between devices, shift_down(): return lax.ppermute(block, axis, [(i + 1, i) for i in range(count - 1)])  7.87 us
    pallas_call x1, Pallas kernels, shards(): pl.pallas_call(bind(first_kernel, dims), out_shape=(shape(3, nz + 1, ny,...  6.76 us
    ppermute x4, waiting for transfers between devices, shift_down(): return lax.ppermute(block, axis, [(i + 1, i) for i in range(count - 1)])  5.9 us
    pallas_call x1, Pallas kernels, shards(): pl.pallas_call(bind(second_kernel, dims), out_shape=shape(3, nz, ny, nx),...  5.11 us
    pallas_call x1, Pallas kernels, shards(): pl.pallas_call(bind(surface_kernel, dims), out_shape=(shape(3, nz, ny, nx...  2.47 us
    pallas_call x1, Pallas kernels, shards(): pl.pallas_call(bind(pack_kernel, dims), out_shape=rows_shape, in_specs=[H...  2.01 us
    pallas_call x1, Pallas kernels, shards(): pl.pallas_call(bind(store_kernel, dims), out_shape=shape(1, 2, TERMS, 2,...  1.34 us
  transfers between devices with their start and end apart: 8, of which 2 were waited for; matrix products, arithmetic and copies ran while one was open for 0% of the time, Pallas kernels for 30%

profile of v1, /device:TPU:3, one launch (start us, length us, event | category | flops | bytes accessed | tf_op | source)
XLA Modules:
  0.0 51.6 jit_solution(17487724187286800419)
XLA Ops:
  0.6 2.0 %pack.1 = (f32[14,2,1024]{2,1,0:T(2,128)S(1)}, f32[14,2,1024]{2,1,0:T(2,128)S(1)}) custom-call(f32[3,14,32,1024]{3,2,1,0:T(8,128)} %electric.3, f32[1,2,2,32,1024]{4,3,2,1,0:T(8,128)} %faces.3), custom_call_target="tpu_custom_call" | custom-call | tf_op jit(solution)/shard_map/pack/pallas_call | solution.py:444
  2.6 3.2 %collective-permute-start = (f32[14,2,1024]{2,1,0:T(2,128)S(1)}, f32[14,2,1024]{2,1,0:T(2,128)S(1)}, u32[]{:S(2)}, u32[]{:S(2)}) collective-permute-start(f32[14,2,1024]{2,1,0:T(2,128)S(1)} %get-tuple-element.26), channel_id=1, source_target_pairs={{0,1},{1,2},{2,3},{3,4},{4,5},{5,6},{6,7},{8,9},{9,10},{10,11},{11... | collective-permute-start | bytes 344072 | tf_op jit(solution)/shard_map/ppermute | solution.py:425
  5.8 2.1 %collective-permute-start.1 = (f32[14,2,1024]{2,1,0:T(2,128)S(1)}, f32[14,2,1024]{2,1,0:T(2,128)S(1)}, u32[]{:S(2)}, u32[]{:S(2)}) collective-permute-start(f32[14,2,1024]{2,1,0:T(2,128)S(1)} %get-tuple-element.27), channel_id=1, source_target_pairs={{1,0},{2,1},{3,2},{4,3},{5,4},{6,5},{7,6},{9,8},{10,9},{11,10},{12... | collective-permute-start | bytes 344072 | tf_op jit(solution)/shard_map/ppermute | solution.py:430
  7.9 6.8 %first_sweep.1 = (f32[3,15,32,1024]{3,2,1,0:T(8,128)S(1)}, f32[3,14,32,1024]{3,2,1,0:T(8,128)S(1)}, f32[14,32,1024]{2,1,0:T(8,128)S(1)}, f32[2,32,1024]{2,1,0:T(8,128)S(1)}, f32[2,4,2,32,1024]{4,3,2,1,0:T(8,128)S(1)}) custom-call(f32[3,14,32,1024]{3,2,1,0:T(8,128)} %electric.3, f32[3,14,32,1024]{3,2,1,0:T(8,128)} %current_h.1, f32[14,32,1024]{2,1,0:T(8,128)} %mass.1, ...), custom_call_target="tpu_custom_call" | custom-call | flops 20643840 | bytes 12845056 | tf_op jit(solution)/shard_map/first_sweep/pallas_call | solution.py:456
  14.7 0.0 collective-permute-done.low
  14.7 0.0 collective-permute-done.1.high
  14.7 0.3 fix_pack.1
  15.1 4.1 %collective-permute-start.2 = (f32[14,2,1024]{2,1,0:T(2,128)S(1)}, f32[14,2,1024]{2,1,0:T(2,128)S(1)}, u32[]{:S(2)}, u32[]{:S(2)}) collective-permute-start(f32[14,2,1024]{2,1,0:T(2,128)S(1)} %get-tuple-element.31), channel_id=1, source_target_pairs={{0,1},{1,2},{2,3},{3,4},{4,5},{5,6},{6,7},{8,9},{9,10},{10,11},{11... | collective-permute-start | bytes 344072 | tf_op jit(solution)/shard_map/ppermute | solution.py:425
  19.2 1.9 %collective-permute-start.3 = (f32[14,2,1024]{2,1,0:T(2,128)S(1)}, f32[14,2,1024]{2,1,0:T(2,128)S(1)}, u32[]{:S(2)}, u32[]{:S(2)}) collective-permute-start(f32[14,2,1024]{2,1,0:T(2,128)S(1)} %get-tuple-element.32), channel_id=1, source_target_pairs={{1,0},{2,1},{3,2},{4,3},{5,4},{6,5},{7,6},{9,8},{10,9},{11,10},{12... | collective-permute-start | bytes 344072 | tf_op jit(solution)/shard_map/ppermute | solution.py:430
  21.1 5.1 %second_sweep.1.field = f32[3,14,32,1024]{3,2,1,0:T(8,128)S(1)} custom-call(f32[3,15,32,1024]{3,2,1,0:T(8,128)S(1)} %get-tuple-element.22.field.old, f32[3,14,32,1024]{3,2,1,0:T(8,128)S(1)} %get-tuple-element.23.current, f32[14,32,1024]{2,1,0:T(8,128)S(1)} %get-tuple-element.24.weight, f32[2,32,1024]{2,1,0:T(8,128)S(1)} %get-tuple-element.25.ghost, ...), custom_call_target="tpu_custom_call" | custom-call | flops 18350080 | bytes 12845056 | tf_op jit(solution)/shard_map/second_sweep/pallas_call | solution.py:485
  26.2 0.0 collective-permute-done.2.low
  26.2 0.0 collective-permute-done.3.high
  26.2 0.2 fix_trace.1
  26.5 4.3 %collective-permute-start.4 = (f32[8,2,1024]{2,1,0:T(2,128)S(1)}, f32[8,2,1024]{2,1,0:T(2,128)S(1)}, u32[]{:S(2)}, u32[]{:S(2)}) collective-permute-start(f32[8,2,1024]{2,1,0:T(2,128)S(1)} %get-tuple-element.38), channel_id=1, source_target_pairs={{0,1},{1,2},{2,3},{3,4},{4,5},{5,6},{6,7},{8,9},{9,10},{10,11},{11... | collective-permute-start | bytes 196616 | tf_op jit(solution)/shard_map/ppermute | solution.py:425
  30.7 1.9 %collective-permute-start.5 = (f32[8,2,1024]{2,1,0:T(2,128)S(1)}, f32[8,2,1024]{2,1,0:T(2,128)S(1)}, u32[]{:S(2)}, u32[]{:S(2)}) collective-permute-start(f32[8,2,1024]{2,1,0:T(2,128)S(1)} %get-tuple-element.39), channel_id=1, source_target_pairs={{1,0},{2,1},{3,2},{4,3},{5,4},{6,5},{7,6},{9,8},{10,9},{11,10},{12... | collective-permute-start | bytes 196616 | tf_op jit(solution)/shard_map/ppermute | solution.py:430
  32.7 2.5 %surface.1 = (f32[3,14,32,1024]{3,2,1,0:T(8,128)}, f32[2,4,2,32,1024]{4,3,2,1,0:T(8,128)S(1)}, f32[2,2,32,1024]{3,2,1,0:T(8,128)S(1)}) custom-call(f32[3,14,32,1024]{3,2,1,0:T(8,128)S(1)} %second_sweep.1.field, f32[15,2,1024]{2,1,0:T(2,128)S(1)} %get-tuple-element.33.head, f32[15,3,1024]{2,1,0:T(4,128)S(1)} %get-tuple-element.34.tail, ...), custom_call_target="tpu_custom_call" | custom-call | flops 10485760 | bytes 5505024 | tf_op jit(solution)/shard_map/surface/pallas_call | solution.py:507
  35.1 0.0 collective-permute-done.4.low
  35.2 1.5 %collective-permute-done.5.high = f32[8,2,1024]{2,1,0:T(2,128)S(1)} collective-permute-done((f32[8,2,1024]{2,1,0:T(2,128)S(1)}, f32[8,2,1024]{2,1,0:T(2,128)S(1)}, u32[]{:S(2)}, u32[]{:S(2)}) %collective-permute-start.5) | collective-permute-done | bytes 65568 | tf_op jit(solution)/shard_map/ppermute | solution.py:430
  36.6 0.1 close.1
  36.8 6.3 %collective-permute-start.6 = (f32[2,32,1024]{2,1,0:T(8,128)S(1)}, f32[2,32,1024]{2,1,0:T(8,128)S(1)}, u32[]{:S(2)}, u32[]{:S(2)}) collective-permute-start(f32[2,32,1024]{2,1,0:T(8,128)S(1)} %get-tuple-element.41), channel_id=1, source_target_pairs={{0,8},{8,16},{16,24},{1,9},{9,17},{17,25},{2,10},{10,18},{18,26},{... | collective-permute-start | bytes 786440 | tf_op jit(solution)/shard_map/ppermute | solution.py:425
  43.0 1.9 %collective-permute-start.7 = (f32[2,32,1024]{2,1,0:T(8,128)S(1)}, f32[2,32,1024]{2,1,0:T(8,128)S(1)}, u32[]{:S(2)}, u32[]{:S(2)}) collective-permute-start(f32[2,32,1024]{2,1,0:T(8,128)S(1)} %get-tuple-element.42), channel_id=1, source_target_pairs={{8,0},{16,8},{24,16},{9,1},{17,9},{25,17},{10,2},{18,10},{26,18},{... | collective-permute-start | bytes 786440 | tf_op jit(solution)/shard_map/ppermute | solution.py:430
  44.9 1.3 %store.1 = f32[1,2,4,2,32,1024]{5,4,3,2,1,0:T(8,128)} custom-call(f32[2,4,2,32,1024]{4,3,2,1,0:T(8,128)S(1)} %get-tuple-element.40.fresh, f32[8,2,1024]{2,1,0:T(2,128)S(1)} %collective-permute-done.4.low, f32[8,2,1024]{2,1,0:T(2,128)S(1)} %collective-permute-done.5.high), custom_call_target="tpu_custom_call" | custom-call | flops 524288 | bytes 4194304 | tf_op jit(solution)/shard_map/store/pallas_call | solution.py:529
  46.3 0.0 collective-permute-done.6
  46.3 4.4 %collective-permute-done.7 = f32[2,32,1024]{2,1,0:T(8,128)S(1)} collective-permute-done((f32[2,32,1024]{2,1,0:T(8,128)S(1)}, f32[2,32,1024]{2,1,0:T(8,128)S(1)}, u32[]{:S(2)}, u32[]{:S(2)}) %collective-permute-start.7) | collective-permute-done | bytes 262176 | tf_op jit(solution)/shard_map/ppermute | solution.py:430
  50.7 0.8 %maximum_bitcast_fusion = f32[1,2,2,32,1024]{4,3,2,1,0:T(8,128)} fusion(f32[1,2,32,1024]{3,2,1,0:T(8,128)S(1)} %bitcast.9, f32[1,2,32,1024]{3,2,1,0:T(8,128)S(1)} %bitcast.8), kind=kLoop, calls=%fused_computation | loop fusion | flops 131072 | bytes 1048576 | tf_op jit(solution)/shard_map/broadcast_in_dim | solution.py:539
  (1 shorter events, 0.0 us)
Async XLA Ops:
  2.6 12.1 %collective-permute-start = (f32[14,2,1024]{2,1,0:T(2,128)S(1)}, f32[14,2,1024]{2,1,0:T(2,128)S(1)}, u32[]{:S(2)}, u32[]{:S(2)}) collective-permute-start(f32[14,2,1024]{2,1,0:T(2,128)S(1)} %get-tuple-element.26), channel_id=1, source_target_pairs={{0,1},{1,2},{2,3},{3,4},{4,5},{5,6},{6,7},{8,9},{9,10},{10,11},{11... | collective-permute-start | bytes 344072 | tf_op jit(solution)/shard_map/ppermute | solution.py:425
  5.8 8.9 %collective-permute-start.1 = (f32[14,2,1024]{2,1,0:T(2,128)S(1)}, f32[14,2,1024]{2,1,0:T(2,128)S(1)}, u32[]{:S(2)}, u32[]{:S(2)}) collective-permute-start(f32[14,2,1024]{2,1,0:T(2,128)S(1)} %get-tuple-element.27), channel_id=1, source_target_pairs={{1,0},{2,1},{3,2},{4,3},{5,4},{6,5},{7,6},{9,8},{10,9},{11,10},{12... | collective-permute-start | bytes 344072 | tf_op jit(solution)/shard_map/ppermute | solution.py:430
  15.1 11.1 %collective-permute-start.2 = (f32[14,2,1024]{2,1,0:T(2,128)S(1)}, f32[14,2,1024]{2,1,0:T(2,128)S(1)}, u32[]{:S(2)}, u32[]{:S(2)}) collective-permute-start(f32[14,2,1024]{2,1,0:T(2,128)S(1)} %get-tuple-element.31), channel_id=1, source_target_pairs={{0,1},{1,2},{2,3},{3,4},{4,5},{5,6},{6,7},{8,9},{9,10},{10,11},{11... | collective-permute-start | bytes 344072 | tf_op jit(solution)/shard_map/ppermute | solution.py:425
  19.2 7.1 %collective-permute-start.3 = (f32[14,2,1024]{2,1,0:T(2,128)S(1)}, f32[14,2,1024]{2,1,0:T(2,128)S(1)}, u32[]{:S(2)}, u32[]{:S(2)}) collective-permute-start(f32[14,2,1024]{2,1,0:T(2,128)S(1)} %get-tuple-element.32), channel_id=1, source_target_pairs={{1,0},{2,1},{3,2},{4,3},{5,4},{6,5},{7,6},{9,8},{10,9},{11,10},{12... | collective-permute-start | bytes 344072 | tf_op jit(solution)/shard_map/ppermute | solution.py:430
  26.5 8.7 %collective-permute-start.4 = (f32[8,2,1024]{2,1,0:T(2,128)S(1)}, f32[8,2,1024]{2,1,0:T(2,128)S(1)}, u32[]{:S(2)}, u32[]{:S(2)}) collective-permute-start(f32[8,2,1024]{2,1,0:T(2,128)S(1)} %get-tuple-element.38), channel_id=1, source_target_pairs={{0,1},{1,2},{2,3},{3,4},{4,5},{5,6},{6,7},{8,9},{9,10},{10,11},{11... | collective-permute-start | bytes 196616 | tf_op jit(solution)/shard_map/ppermute | solution.py:425
  30.7 5.9 %collective-permute-start.5 = (f32[8,2,1024]{2,1,0:T(2,128)S(1)}, f32[8,2,1024]{2,1,0:T(2,128)S(1)}, u32[]{:S(2)}, u32[]{:S(2)}) collective-permute-start(f32[8,2,1024]{2,1,0:T(2,128)S(1)} %get-tuple-element.39), channel_id=1, source_target_pairs={{1,0},{2,1},{3,2},{4,3},{5,4},{6,5},{7,6},{9,8},{10,9},{11,10},{12... | collective-permute-start | bytes 196616 | tf_op jit(solution)/shard_map/ppermute | solution.py:430
  36.8 9.6 %collective-permute-start.6 = (f32[2,32,1024]{2,1,0:T(8,128)S(1)}, f32[2,32,1024]{2,1,0:T(8,128)S(1)}, u32[]{:S(2)}, u32[]{:S(2)}) collective-permute-start(f32[2,32,1024]{2,1,0:T(8,128)S(1)} %get-tuple-element.41), channel_id=1, source_target_pairs={{0,8},{8,16},{16,24},{1,9},{9,17},{17,25},{2,10},{10,18},{18,26},{... | collective-permute-start | bytes 786440 | tf_op jit(solution)/shard_map/ppermute | solution.py:425
  43.0 7.7 %collective-permute-start.7 = (f32[2,32,1024]{2,1,0:T(8,128)S(1)}, f32[2,32,1024]{2,1,0:T(8,128)S(1)}, u32[]{:S(2)}, u32[]{:S(2)}) collective-permute-start(f32[2,32,1024]{2,1,0:T(8,128)S(1)} %get-tuple-element.42), channel_id=1, source_target_pairs={{8,0},{16,8},{24,16},{9,1},{17,9},{25,17},{10,2},{18,10},{26,18},{... | collective-permute-start | bytes 786440 | tf_op jit(solution)/shard_map/ppermute | solution.py:430

commit v2 on v1

v2 whole, which is shorter than its diff:
```python
import functools
import math

import jax
import jax.numpy as jnp
from jax import lax
from jax.experimental import pallas as pl
from jax.experimental.pallas import tpu as pltpu
from jax.sharding import PartitionSpec as P


pade_weights = [2.0 / 9.0 * math.sin(j * math.pi / 9.0) ** 2 for j in range(1, 5)]
pade_decays = [math.cos(j * math.pi / 9.0) ** 2 for j in range(1, 5)]
TERMS = 4
SUB, LANE = 8, 128
F32 = jnp.float32
HBM = pl.BlockSpec(memory_space=pltpu.HBM)
VM = pl.BlockSpec(memory_space=pltpu.VMEM)


def params(mib):
    return pltpu.CompilerParams(vmem_limit_bytes=mib << 20)


def shape(*dims):
    return jax.ShapeDtypeStruct(dims, F32)


def cost(flops, count):
    return pl.CostEstimate(flops=flops, bytes_accessed=count, transcendentals=0)


def vm(*dims):
    return pltpu.VMEM(dims, F32)


def row_next(row):
    n = row.shape[1]
    at = lax.broadcasted_iota(jnp.int32, row.shape, 1)
    return jnp.where(at == n - 1, 0.0, pltpu.roll(row, n - 1, 1))


def row_prev(row):
    at = lax.broadcasted_iota(jnp.int32, row.shape, 1)
    return jnp.where(at == 0, 0.0, pltpu.roll(row, 1, 1))


def is_even(axis):
    return lax.rem(lax.axis_index(axis), 2) == 0


class Either:
    def __init__(self, choose, first, second):
        self.choose, self.first, self.second = choose, first, second

    def __getitem__(self, at):
        return jnp.where(self.choose, self.first[at], self.second[at])


def halo_views(near, far):
    even = is_even("tile")
    return Either(even, far, near), Either(even, near, far)


def upward(last, y_above):
    x, y, z = last
    return row_next(y) - y + x, z + (y_above - y)


def fixed_first(field, weight, low, z, zz):
    w = weight[z, 0:1, :]
    return field[0, zz, 0:1, :] + w * low[z, 0:1, :], field[2, zz, 0:1, :] + w * low[z, 1:2, :]


def fixed_last(field, weight, high, z, zz, ny):
    end = slice(ny - 1, ny)
    w = weight[z, end, :]
    hx, hz = high[z, 0:1, :], high[z, 1:2, :]
    rise = hz - high[z - 1, 1:2, :] if z else hz
    return (
        field[0, zz, end, :] + w * hx,
        field[1, zz, end, :] - w * (rise + (hx - row_prev(hx))),
        field[2, zz, end, :] + w * hz,
    )


def lane_masks():
    lane = lax.broadcasted_iota(jnp.int32, (SUB, LANE), 1)
    sub = lax.broadcasted_iota(jnp.int32, (SUB, LANE), 0)
    return lane == 0, lane == LANE - 1, sub == 0, sub == SUB - 1


def tile_at(i, c):
    return slice(i * SUB, (i + 1) * SUB), slice(c * LANE, (c + 1) * LANE)


def pack_kernel(dims, electric, faces, far, block, top, sem):
    nz, ny, _ = dims
    even = is_even("tile")
    start = pl.multiple_of(jnp.where(even, 0, ny - SUB), SUB)
    copies = [
        pltpu.make_async_copy(electric.at[:, :, pl.ds(start, SUB)], block, sem.at[0]),
        pltpu.make_async_copy(faces.at[0, 1, 1, pl.ds(ny - SUB, SUB)], top, sem.at[1]),
    ]
    for copy in copies:
        copy.start()
    for copy in copies:
        copy.wait()
    end = slice(SUB - 1, SUB)
    for z in range(nz):
        y_above = block[1, z + 1, end, :] if z + 1 < nz else top[end, :]
        up = upward([block[k, z, end, :] for k in range(3)], y_above)
        for q in range(2):
            far[z, q : q + 1, :] = jnp.where(even, block[2 * q, z, 0:1, :], up[q])


def sweep_plane(load, above, current, weight, store, hx_s, hy_s, dims, from_mass):
    _, ny, nx = dims
    rows, cols = ny // SUB, nx // LANE
    is_first_lane, is_last_lane, is_first_sub, is_last_sub = lane_masks()

    def left(k, i, c):
        return pltpu.roll(load(k, i, c), LANE - 1, 1)

    lefts = {(k, i): left(k, i, 0) for k in (1, 2) for i in range(rows)}
    right_y, right_z = {}, {}
    for c in range(cols):
        here = [[load(k, i, c) for k in range(3)] for i in range(rows)]
        ups = [{k: pltpu.roll(here[i][k], SUB - 1, 0) for k in (0, 2)} for i in range(rows)]
        down_x = down_z = None
        for i in range(rows):
            r, s = tile_at(i, c)

            def y_next(k):
                return jnp.where(is_last_sub, ups[i + 1][k] if i + 1 < rows else 0.0, ups[i][k])

            def x_next(k):
                after = left(k, i, c + 1) if c + 1 < cols else 0.0
                value = jnp.where(is_last_lane, after, lefts[k, i])
                lefts[k, i] = after
                return value

            ex, ey, ez = here[i]
            hx = (y_next(2) - ez) - (above(1, i, c) - ey)
            hy = (above(0, i, c) - ex) - (x_next(2) - ez)
            hz = (x_next(1) - ey) - (y_next(0) - ex)
            hx_low, hy_low = hx_s[r, s], hy_s[r, s]
            hx_s[r, s] = hx
            hy_s[r, s] = hy
            dx = pltpu.roll(hx, 1, 0)
            dz = pltpu.roll(hz, 1, 0)
            hx_y = jnp.where(is_first_sub, ez if i == 0 else down_x, dx)
            hz_y = jnp.where(is_first_sub, -ex if i == 0 else down_z, dz)
            down_x, down_z = dx, dz
            ry = pltpu.roll(hy, 1, 1)
            rz = pltpu.roll(hz, 1, 1)
            hy_x = jnp.where(is_first_lane, 0.0 if c == 0 else right_y[i], ry)
            hz_x = jnp.where(is_first_lane, 0.0 if c == 0 else right_z[i], rz)
            right_y[i], right_z[i] = ry, rz
            cx = (hz - hz_y) - (hy - hy_low)
            cy = (hx - hx_low) - (hz - hz_x)
            cz = (hy - hy_x) - (hx - hx_y)
            w = weight[r, s]
            if from_mass:
                w = 0.5 / (w + 4.0)
                weight[r, s] = w
            keep = 4.0 * w + 0.5
            store(0, i, c, keep * ex + w * (current(0, i, c) - cx))
            store(1, i, c, keep * ey + w * (current(1, i, c) - cy))
            store(2, i, c, keep * ez + w * (current(2, i, c) - cz))


def reader(ref, z):
    def load(k, i, c):
        r, s = tile_at(i, c)
        return ref[k, z, r, s]

    return load


def writer(ref, z):
    def store(k, i, c, value):
        r, s = tile_at(i, c)
        ref[k, z, r, s] = value

    return store


def ghost_flux(load, ghost, hx_s, hy_s, dims):
    _, ny, nx = dims
    for i in range(ny // SUB):
        for c in range(nx // LANE):
            r, s = tile_at(i, c)
            hx_s[r, s] = ghost[1, r, s] - load(1, i, c)
            hy_s[r, s] = load(0, i, c) - ghost[0, r, s]


def first_lower_kernel(
    dims, electric, current_h, mass, faces, aux_h,
    field, current, weight, ghost, aux, flux, near,
    field_sem, current_sem, weight_sem, face_sem,
):
    nz, ny, _ = dims
    half = nz // 2
    even = is_even("tile")
    end = slice(ny - 1, ny)
    copy = pltpu.make_async_copy

    def field_copy(z):
        return copy(electric.at[:, pl.ds(z, 1)], field.at[:, pl.ds(z, 1)], field_sem.at[z])

    def current_copy(z):
        return copy(current_h.at[:, pl.ds(z, 1)], current.at[:, pl.ds(z, 1)], current_sem.at[z])

    def weight_copy(z):
        return copy(mass.at[pl.ds(z, 1)], weight.at[pl.ds(z, 1)], weight_sem.at[z])

    low_copy = copy(faces.at[0, 0], ghost, face_sem.at[0])
    high_copies = [copy(faces.at[0, 1, k], field.at[k, nz], face_sem.at[1 + k]) for k in range(2)]
    aux_copy = copy(aux_h.at[0], aux, face_sem.at[3])
    low_copy.start()
    field_copy(0).start()

    def start(z, carry):
        field_copy(z + 1).start()
        current_copy(z).start()
        weight_copy(z).start()
        return carry

    lax.fori_loop(0, nz - 1, start, 0)
    current_copy(nz - 1).start()
    weight_copy(nz - 1).start()
    for high in high_copies:
        high.start()
    aux_copy.start()

    def pack(z):
        up = upward([field[k, z, end, :] for k in range(3)], field[1, z + 1, end, :])
        for q in range(2):
            near[z, q : q + 1, :] = jnp.where(even, up[q], field[2 * q, z, 0:1, :])

    low_copy.wait()
    field_copy(0).wait()
    hx_s, hy_s = flux.at[0], flux.at[1]
    ghost_flux(reader(field, 0), ghost, hx_s, hy_s, dims)

    def plane(z, carry):
        field_copy(z + 1).wait()
        pack(z)
        current_copy(z).wait()
        weight_copy(z).wait()
        sweep_plane(
            reader(field, z), reader(field, z + 1), reader(current, z), weight.at[z], writer(field, z), hx_s, hy_s, dims, True
        )
        return carry

    lax.fori_loop(0, half, plane, 0)

    def rest(z, carry):
        field_copy(z + 1).wait()
        pack(z)
        current_copy(z).wait()
        weight_copy(z).wait()
        return carry

    lax.fori_loop(half, nz - 1, rest, 0)
    for high in high_copies:
        high.wait()
    pack(nz - 1)
    current_copy(nz - 1).wait()
    weight_copy(nz - 1).wait()
    aux_copy.wait()


def first_upper_kernel(dims, old, current, mass, flux, field, weight, flux_s):
    nz, _, _ = dims
    half = nz // 2
    flux_s[...] = flux[...]
    for k in range(2):
        field[k, nz - half] = old[k, nz]

    def plane(z, carry):
        weight[z] = mass[z + half]
        sweep_plane(
            reader(old, z + half), reader(old, z + half + 1), reader(current, z + half),
            weight.at[z], writer(field, z), flux_s.at[0], flux_s.at[1], dims, True,
        )
        return carry

    lax.fori_loop(0, nz - half, plane, 0)


class Planes:
    def __init__(self, lower, upper, half, dim):
        self.lower, self.upper, self.half, self.dim = lower, upper, half, dim

    def __getitem__(self, at):
        z = at[self.dim]
        if z < self.half:
            return self.lower[at]
        return self.upper[at[: self.dim] + (z - self.half,) + at[self.dim + 1 :]]


def fix_pack_kernel(dims, field_a, field_b, weight_a, weight_b, near, far, head, tail, far_next):
    nz, ny, _ = dims
    half = nz // 2
    even = is_even("tile")
    end = slice(ny - 1, ny)
    field = Planes(field_a, field_b, half, 1)
    weight = Planes(weight_a, weight_b, half, 0)
    low, high = halo_views(near, far)
    for z in range(nz):
        head[z, 0:1, :], head[z, 1:2, :] = fixed_first(field, weight, low, z, z)
        x, y, zc = fixed_last(field, weight, high, z, z, ny)
        tail[z, 0:1, :], tail[z, 1:2, :], tail[z, 2:3, :] = x, y, zc
    head[nz, 0:1, :] = field[0, nz, 0:1, :]
    tail[nz, 0:1, :] = field[0, nz, end, :]
    tail[nz, 1:2, :] = field[1, nz, end, :]
    for z in range(nz):
        up = upward([tail[z, k : k + 1, :] for k in range(3)], tail[z + 1, 1:2, :])
        for q in range(2):
            far_next[z, q : q + 1, :] = jnp.where(even, head[z, q : q + 1, :], up[q])


def edged_reader(ref, z, head, tail, plane, ny):
    rows = ny // SUB
    _, _, is_first_sub, is_last_sub = lane_masks()

    def load(k, i, c):
        r, s = tile_at(i, c)
        value = ref[k, z, r, s]
        if i == 0 and k != 1:
            value = jnp.where(is_first_sub, head[plane, k // 2 : k // 2 + 1, s], value)
        if i == rows - 1:
            value = jnp.where(is_last_sub, tail[plane, k : k + 1, s], value)
        return value

    return load


def second_lower_kernel(dims, old_a, old_b, current, weight, ghost, head, tail, field, flux, near_next):
    nz, ny, _ = dims
    half = nz // 2
    even = is_even("tile")
    for z in range(nz):
        up = upward([tail[z, k : k + 1, :] for k in range(3)], tail[z + 1, 1:2, :])
        for q in range(2):
            near_next[z, q : q + 1, :] = jnp.where(even, up[q], head[z, q : q + 1, :])
    hx_s, hy_s = flux.at[0], flux.at[1]
    ghost_flux(edged_reader(old_a, 0, head, tail, 0, ny), ghost, hx_s, hy_s, dims)

    def sweep(z, above):
        sweep_plane(
            edged_reader(old_a, z, head, tail, z, ny), above, reader(current, z), weight.at[z],
            writer(field, z), hx_s, hy_s, dims, False,
        )

    def plane(z, carry):
        sweep(z, edged_reader(old_a, z + 1, head, tail, z + 1, ny))
        return carry

    lax.fori_loop(0, half - 1, plane, 0)
    sweep(half - 1, edged_reader(old_b, 0, head, tail, half, ny))


def second_upper_kernel(dims, old, current, weight, flux, head, tail, field, flux_s):
    nz, ny, _ = dims
    half = nz // 2
    flux_s[...] = flux[...]

    def plane(z, carry):
        at = z + half
        sweep_plane(
            edged_reader(old, z, head, tail, at, ny), edged_reader(old, z + 1, head, tail, at + 1, ny),
            reader(current, at), weight.at[z], writer(field, z), flux_s.at[0], flux_s.at[1], dims, False,
        )
        return carry

    lax.fori_loop(0, nz - half, plane, 0)


def fix_trace_kernel(
    dims, field_a, field_b, weight_a, weight_b, aux, near, far, head, tail, traces, far_next
):
    nz, ny, _ = dims
    half = nz // 2
    even = is_even("tile")
    end = slice(ny - 1, ny)
    field = Planes(field_a, field_b, half, 1)
    weight = Planes(weight_a, weight_b, half, 0)
    low, high = halo_views(near, far)
    for side in range(2):
        z = (nz - 1) * side
        for k in range(2):
            traces[side, k] = field[k, z]
    for z in range(nz):
        head[z, 0:1, :], head[z, 1:2, :] = fixed_first(field, weight, low, z, z)
        x, y, zc = fixed_last(field, weight, high, z, z, ny)
        tail[z, 0:1, :], tail[z, 1:2, :], tail[z, 2:3, :] = x, y, zc
        if z in (0, nz - 1):
            side = 0 if z == 0 else 1
            traces[side, 0, 0:1, :] = head[z, 0:1, :]
            traces[side, 0, end, :] = x
            traces[side, 1, end, :] = y
    pack_combined(even, traces, aux, far_next, ny, False)


def pack_combined(even, traces, aux, send, ny, up_from_even):
    end = slice(ny - 1, ny)
    for side in range(2):
        for k in range(2):
            first = traces[side, k, 0:1, :]
            last = traces[side, k, end, :]
            for j in range(TERMS):
                down = first - pade_decays[j] * aux[side, j, k, 0:1, :]
                up = last - pade_decays[j] * aux[side, j, k, end, :]
                pair = (up, down) if up_from_even else (down, up)
                send[side * TERMS + j, k : k + 1, :] = jnp.where(even, *pair)


def surface_kernel(dims, traces, aux, fresh, outgoing, near_next):
    _, ny, nx = dims
    rows, cols = ny // SUB, nx // LANE
    is_first_lane, is_last_lane, is_first_sub, is_last_sub = lane_masks()
    pack_combined(is_even("tile"), traces, aux, near_next, ny, True)

    def part(side, carry):
        outgoing[side] = traces[side]

        def term(j, carry):
            decay = weight = F32(0.0)
            for q in range(TERMS):
                decay = jnp.where(j == q, F32(pade_decays[q]), decay)
                weight = jnp.where(j == q, F32(pade_weights[q]), weight)
            for k in range(2):

                def value(i, c):
                    r, s = tile_at(i, c)
                    return traces[side, k, r, s] - decay * aux[side, j, k, r, s]

                column = [value(i, 0) for i in range(rows)]
                lefts = [pltpu.roll(u, LANE - 1, 1) for u in column]
                rights = [0.0] * rows
                for c in range(cols):
                    ups = [pltpu.roll(u, SUB - 1, 0) for u in column]
                    downs = [pltpu.roll(u, 1, 0) for u in column]
                    after = [value(i, c + 1) for i in range(rows)] if c + 1 < cols else None
                    for i in range(rows):
                        r, s = tile_at(i, c)
                        u = column[i]
                        y_next = jnp.where(is_last_sub, ups[i + 1] if i + 1 < rows else 0.0, ups[i])
                        y_prev = jnp.where(is_first_sub, downs[i - 1] if i else 0.0, downs[i])
                        if after is not None:
                            beyond = pltpu.roll(after[i], LANE - 1, 1)
                        else:
                            beyond = u if k == 0 else 0.0
                        x_next = jnp.where(is_last_lane, beyond, lefts[i])
                        lefts[i] = beyond
                        right = pltpu.roll(u, 1, 1)
                        before = rights[i] if c else (u if k == 1 else 0.0)
                        x_prev = jnp.where(is_first_lane, before, right)
                        rights[i] = right
                        new = 0.5 * u - 0.125 * ((y_next + y_prev) + (x_next + x_prev))
                        fresh[side, j, k, r, s] = new
                        outgoing[side, k, r, s] += weight * new
                    column = after
            return carry

        return lax.fori_loop(0, TERMS, term, carry)

    lax.fori_loop(0, 2, part, 0)


def write_kernel(dims, field_a, field_b, head, tail, smoothed, edges, sem):
    nz, ny, nx = dims
    half = nz // 2
    _, _, is_first_sub, is_last_sub = lane_masks()
    inner = pl.ds(SUB, ny - 2 * SUB)
    copies = []
    for n, (field, start, count) in enumerate(((field_a, 0, half), (field_b, half, nz - half))):
        planes = pl.ds(start, count)
        copies.append(pltpu.make_async_copy(field.at[:, :, inner], smoothed.at[:, planes, inner], sem.at[n]))
        copies[-1].start()
    for n, (field, start, count) in enumerate(((field_a, 0, half), (field_b, half, nz - half))):

        def merge(z, carry):
            at = z + start
            for c in range(nx // LANE):
                s = slice(c * LANE, (c + 1) * LANE)
                for k in range(3):
                    value = field[k, z, 0:SUB, s]
                    if k != 1:
                        value = jnp.where(is_first_sub, head[at, k // 2 : k // 2 + 1, s], value)
                    edges[0, k, at, :, s] = value
                    value = field[k, z, ny - SUB : ny, s]
                    edges[1, k, at, :, s] = jnp.where(is_last_sub, tail[at, k : k + 1, s], value)
            return carry

        lax.fori_loop(0, count, merge, 0)
        planes = pl.ds(start, count)
        for e, row in enumerate((0, ny - SUB)):
            copies.append(
                pltpu.make_async_copy(
                    edges.at[e, :, planes], smoothed.at[:, planes, pl.ds(row, SUB)], sem.at[2 + 2 * n + e]
                )
            )
            copies[-1].start()
    for copy in copies:
        copy.wait()


def close_kernel(dims, zero_halo, near, far, even_side, odd_side, outgoing):
    _, ny, _ = dims
    low, high = halo_views(near, far)
    for side in range(2):
        for k in range(2):
            outgoing[side, k] = zero_halo[side, k]
            for source, r in ((low, slice(0, 1)), (high, slice(ny - 1, ny))):
                total = 0.0
                for j in range(TERMS):
                    total = total + (0.125 * pade_weights[j]) * source[side * TERMS + j, k : k + 1, :]
                outgoing[side, k, r, :] = zero_halo[side, k, r, :] - total
    even = is_even("slab")
    even_side[...] = jnp.where(even, outgoing[1], outgoing[0])
    odd_side[...] = jnp.where(even, outgoing[0], outgoing[1])


def faces_kernel(even_side, odd_side, out, sem):
    below = jnp.where(is_even("slab"), 0, 1)
    copies = [
        pltpu.make_async_copy(odd_side, out.at[0, below], sem.at[0]),
        pltpu.make_async_copy(even_side, out.at[0, 1 - below], sem.at[1]),
    ]
    for copy in copies:
        copy.start()
    for copy in copies:
        copy.wait()


def store_kernel(dims, fresh, near, far, out, edges, sem):
    _, ny, nx = dims
    low, high = halo_views(near, far)
    inner = pl.ds(SUB, ny - 2 * SUB)
    middle = pltpu.make_async_copy(fresh.at[:, :, :, inner], out.at[0, :, :, :, inner], sem.at[0])
    middle.start()
    _, _, is_first_sub, is_last_sub = lane_masks()
    for side in range(2):
        for j in range(TERMS):
            for k in range(2):
                at = side * TERMS + j
                for c in range(nx // LANE):
                    s = slice(c * LANE, (c + 1) * LANE)
                    first = jnp.where(is_first_sub, 0.125 * low[at, k : k + 1, s], 0.0)
                    last = jnp.where(is_last_sub, 0.125 * high[at, k : k + 1, s], 0.0)
                    edges[0, side, j, k, :, s] = fresh[side, j, k, 0:SUB, s] - first
                    edges[1, side, j, k, :, s] = fresh[side, j, k, ny - SUB : ny, s] - last
    outer = [
        pltpu.make_async_copy(edges.at[e], out.at[0, :, :, :, pl.ds(start, SUB)], sem.at[1 + e])
        for e, start in enumerate((0, ny - SUB))
    ]
    for copy in outer:
        copy.start()
    middle.wait()
    for copy in outer:
        copy.wait()


def call(kernel, **options):
    return pl.pallas_call(kernel, **options)


def swap(block, axis, first):
    pairs = [(i, i + 1) for i in range(first, lax.axis_size(axis) - 1, 2)]
    return lax.ppermute(block, axis, [p for i, j in pairs for p in ((i, j), (j, i))])


def iteration(electric, current, mass, faces, aux):
    nz, ny, nx = mass.shape
    half = nz // 2
    dims = (nz, ny, nx)
    cells = nz * ny * nx
    bind = functools.partial
    rows = shape(nz, 2, nx)
    flux_shape = shape(2, ny, nx)
    dma = pltpu.SemaphoreType.DMA
    electric, current, mass, faces, aux = (
        pltpu.with_memory_space_constraint(a, pltpu.HBM) for a in (electric, current, mass, faces, aux)
    )

    far1 = call(
        bind(pack_kernel, dims),
        out_shape=rows,
        in_specs=[HBM] * 2,
        out_specs=VM,
        scratch_shapes=[vm(3, nz, SUB, nx), vm(SUB, nx), dma((2,))],
        compiler_params=params(12),
    )(electric, faces)
    far1 = swap(far1, "tile", 1)

    field, current_v, weight, ghost, aux_v, flux, near1 = call(
        bind(first_lower_kernel, dims),
        out_shape=(
            shape(3, nz + 1, ny, nx),
            shape(3, nz, ny, nx),
            shape(nz, ny, nx),
            shape(2, ny, nx),
            shape(2, TERMS, 2, ny, nx),
            flux_shape,
            rows,
        ),
        in_specs=[HBM] * 5,
        out_specs=(VM,) * 7,
        scratch_shapes=[dma((nz,)), dma((nz,)), dma((nz,)), dma((4,))],
        compiler_params=params(24),
        cost_estimate=cost(25 * cells, 28 * cells),
    )(electric, current, mass, faces, aux)
    near1 = swap(near1, "tile", 0)

    upper, weight_u = call(
        bind(first_upper_kernel, dims),
        out_shape=(shape(3, nz - half + 1, ny, nx), shape(nz - half, ny, nx)),
        in_specs=[VM] * 4,
        out_specs=(VM,) * 2,
        scratch_shapes=[vm(2, ny, nx)],
        compiler_params=params(12),
        cost_estimate=cost(25 * cells, 14 * cells),
    )(field, current_v, weight, flux)

    heads, tails = shape(nz + 1, 2, nx), shape(nz + 1, 3, nx)
    head, tail, far2 = call(
        bind(fix_pack_kernel, dims),
        out_shape=(heads, tails, rows),
        in_specs=[VM] * 6,
        out_specs=(VM,) * 3,
        compiler_params=params(12),
    )(field, upper, weight, weight_u, near1, far1)
    far2 = swap(far2, "tile", 1)

    lower2, flux, near2 = call(
        bind(second_lower_kernel, dims),
        out_shape=(shape(3, half, ny, nx), flux_shape, rows),
        in_specs=[VM] * 7,
        out_specs=(VM,) * 3,
        compiler_params=params(12),
        cost_estimate=cost(20 * cells, 14 * cells),
    )(field, upper, current_v, weight, ghost, head, tail)
    near2 = swap(near2, "tile", 0)

    upper2 = call(
        bind(second_upper_kernel, dims),
        out_shape=shape(3, nz - half, ny, nx),
        in_specs=[VM] * 6,
        out_specs=VM,
        scratch_shapes=[vm(2, ny, nx)],
        compiler_params=params(12),
        cost_estimate=cost(20 * cells, 14 * cells),
    )(upper, current_v, weight_u, flux, head, tail)

    edge_rows = shape(2 * TERMS, 2, nx)
    head, tail, traces, far3 = call(
        bind(fix_trace_kernel, dims),
        out_shape=(heads, tails, shape(2, 2, ny, nx), edge_rows),
        in_specs=[VM] * 7,
        out_specs=(VM,) * 4,
        compiler_params=params(12),
    )(lower2, upper2, weight, weight_u, aux_v, near2, far2)
    far3 = swap(far3, "tile", 1)

    fresh, outgoing, near3 = call(
        bind(surface_kernel, dims),
        out_shape=(shape(2, TERMS, 2, ny, nx), shape(2, 2, ny, nx), edge_rows),
        in_specs=[VM] * 2,
        out_specs=(VM,) * 3,
        compiler_params=params(12),
        cost_estimate=cost(20 * 16 * ny * nx, 12 * cells),
    )(traces, aux_v)
    near3 = swap(near3, "tile", 0)

    smoothed = call(
        bind(write_kernel, dims),
        out_shape=shape(3, nz, ny, nx),
        in_specs=[VM] * 4,
        out_specs=HBM,
        scratch_shapes=[vm(2, 3, nz, SUB, nx), dma((6,))],
        compiler_params=params(12),
        cost_estimate=cost(cells, 12 * cells),
    )(lower2, upper2, head, tail)

    side_shape = shape(2, ny, nx)
    even_side, odd_side = call(
        bind(close_kernel, dims),
        out_shape=(side_shape, side_shape),
        in_specs=[VM] * 3,
        out_specs=(VM,) * 2,
        scratch_shapes=[vm(2, 2, ny, nx)],
        compiler_params=params(8),
    )(outgoing, near3, far3)
    odd_side = swap(odd_side, "slab", 1)
    even_side = swap(even_side, "slab", 0)

    fresh = call(
        bind(store_kernel, dims),
        out_shape=shape(1, 2, TERMS, 2, ny, nx),
        in_specs=[VM] * 3,
        out_specs=HBM,
        scratch_shapes=[vm(2, 2, TERMS, 2, SUB, nx), dma((3,))],
        compiler_params=params(8),
        cost_estimate=cost(16 * ny * nx, 8 * 16 * ny * nx),
    )(fresh, near3, far3)

    next_faces = call(
        faces_kernel,
        out_shape=shape(1, 2, 2, ny, nx),
        in_specs=[VM] * 2,
        out_specs=HBM,
        scratch_shapes=[dma((2,))],
        compiler_params=params(8),
    )(even_side, odd_side)
    return smoothed, next_faces, fresh


def solution(mesh):
    placed = (
        P(None, "slab", "tile", None),
        P(None, "slab", "tile", None),
        P("slab", "tile", None),
        P("slab", None, None, "tile", None),
        P("slab", None, None, None, "tile", None),
    )
    return jax.shard_map(
        iteration,
        mesh=mesh,
        in_specs=placed,
        out_specs=(
            P(None, "slab", "tile", None),
            P("slab", None, None, "tile", None),
            P("slab", None, None, None, "tile", None),
        ),
        check_vma=False,
    )
```

time: 51.9 us -> 48.5 us (0.934)
  starting transfers between devices: 25.6 us -> 19 us
  Pallas kernels: 18.3 us -> 22.2 us
  other arithmetic: 0.84 us -> 0 us
    ppermute x8, starting transfers between devices: 25.6 us -> 19 us  [swap(): lax.ppermute(block, axis, [p for i, j in pairs for p in ((i, j), (j, i))])]
    pallas_call x8 -> x12, Pallas kernels: 18.3 us -> 22.2 us  [the longest x1 5.96 us: iteration(): call(bind(first_lower_kernel, dims), out_shape=(shape(3, nz + 1, ny, nx),...]
    broadcast_in_dim x1 -> x0, other arithmetic: 0.84 us -> none  [shards(): return (smoothed, jnp.stack([from_below, from_above])[None], fresh)]
  transfers between devices with their start and end apart: 8 -> 8, of which waited for: 2 -> 5; matrix products, arithmetic and copies ran while one was open for 0% -> 0% of each run, Pallas kernels for 30% -> 34%
where the time goes in v2:
time: 48.5 us; the launch traced here: 48 us
  Pallas kernels  22.2 us (46%)
  starting transfers between devices  19 us (39%)
  waiting for transfers between devices  5.92 us (12%)
  between operations  0.77 us (2%)
    ppermute x8, starting transfers between devices, swap(): lax.ppermute(block, axis, [p for i, j in pairs for p in ((i, j), (j, i))])  19 us
    pallas_call x1, Pallas kernels, iteration(): call(bind(first_lower_kernel, dims), out_shape=(shape(3, nz + 1, ny, nx),...  5.96 us
    ppermute x8, waiting for transfers between devices, swap(): lax.ppermute(block, axis, [p for i, j in pairs for p in ((i, j), (j, i))])  5.92 us
    pallas_call x1, Pallas kernels, iteration(): call(bind(second_lower_kernel, dims), out_shape=(shape(3, half, ny, nx),...  2.78 us
    pallas_call x1, Pallas kernels, iteration(): call(bind(write_kernel, dims), out_shape=shape(3, nz, ny, nx), in_specs=[...  2.49 us
    pallas_call x1, Pallas kernels, iteration(): call(bind(second_upper_kernel, dims), out_shape=shape(3, nz - half, ny, n...  2.46 us
    pallas_call x1, Pallas kernels, iteration(): call(bind(first_upper_kernel, dims), out_shape=(shape(3, nz - half + 1, n...  2.34 us
    pallas_call x1, Pallas kernels, iteration(): call(bind(surface_kernel, dims), out_shape=(shape(2, TERMS, 2, ny, nx), s...  1.83 us
  transfers between devices with their start and end apart: 8, of which 5 were waited for; matrix products, arithmetic and copies ran while one was open for 0% of the time, Pallas kernels for 34%

profile of v2, /device:TPU:3, one launch (start us, length us, event | category | flops | bytes accessed | tf_op | source)
XLA Modules:
  0.0 48.0 jit_solution(8941921888513766238)
XLA Ops:
  0.6 1.6 %shard_map.78 = f32[14,2,1024]{2,1,0:T(2,128)S(1)} custom-call(f32[3,14,32,1024]{3,2,1,0:T(8,128)} %electric.3, f32[1,2,2,32,1024]{4,3,2,1,0:T(8,128)} %faces.3), custom_call_target="tpu_custom_call" | custom-call | tf_op jit(solution)/shard_map/pallas_call | solution.py:590
  2.2 3.2 %collective-permute-start.1 = (f32[14,2,1024]{2,1,0:T(2,128)S(1)}, f32[14,2,1024]{2,1,0:T(2,128)S(1)}, u32[]{:S(2)}, u32[]{:S(2)}) collective-permute-start(f32[14,2,1024]{2,1,0:T(2,128)S(1)} %shard_map.78), channel_id=1, source_target_pairs={{1,2},{2,1},{3,4},{4,3},{5,6},{6,5},{9,10},{10,9},{11,12},{12,11},... | collective-permute-start | bytes 344072 | tf_op jit(solution)/shard_map/ppermute | solution.py:574
  5.4 6.0 %shard_map.76 = (f32[3,15,32,1024]{3,2,1,0:T(8,128)S(1)}, f32[3,14,32,1024]{3,2,1,0:T(8,128)S(1)}, f32[14,32,1024]{2,1,0:T(8,128)S(1)}, f32[2,32,1024]{2,1,0:T(8...) custom-call(f32[3,14,32,1024]{3,2,1,0:T(8,128)} %electric.3, ...), custom_call_target="tpu_custom_call" | custom-call | flops 11468800 | bytes 12845056 | tf_op jit(solution)/shard_map/pallas_call | solution.py:600
  11.4 0.1 collective-permute-start
  11.4 2.3 %shard_map.77 = (f32[3,8,32,1024]{3,2,1,0:T(8,128)S(1)}, f32[7,32,1024]{2,1,0:T(8,128)S(1)}) custom-call(f32[3,15,32,1024]{3,2,1,0:T(8,128)S(1)} %get-tuple-element.27.old.field_a.old_a, f32[3,14,32,1024]{3,2,1,0:T(8,128)S(1)} %get-tuple-element.28.current, f32[14,32,1024]{2,1,0:T(8,128)S(1)} %get-tuple-element.29.mass.weight_a.weight, ...), custom_call_target="tpu_custom_call" | custom-call | flops 11468800 | bytes 6422528 | tf_op jit(solution)/shard_map/pallas_call | solution.py:619
  13.8 0.0 collective-permute-done.1.far
  13.8 1.3 %collective-permute-done.near = f32[14,2,1024]{2,1,0:T(2,128)S(1)} collective-permute-done((f32[14,2,1024]{2,1,0:T(2,128)S(1)}, f32[14,2,1024]{2,1,0:T(2,128)S(1)}, u32[]{:S(2)}, u32[]{:S(2)}) %collective-permute-start) | collective-permute-done | bytes 114720 | tf_op jit(solution)/shard_map/ppermute | solution.py:574
  15.1 0.3 shard_map.79
  15.4 2.8 %shard_map.80 = (f32[3,7,32,1024]{3,2,1,0:T(8,128)S(1)}, f32[2,32,1024]{2,1,0:T(8,128)S(1)}, f32[14,2,1024]{2,1,0:T(2,128)S(1)}) custom-call(f32[3,15,32,1024]{3,2,1,0:T(8,128)S(1)} %get-tuple-element.27.old.field_a.old_a, f32[3,8,32,1024]{3,2,1,0:T(8,128)S(1)} %get-tuple-element.31.field_b.old_b.old, f32[3,14,32,1024]{3,2,1,0:T(8,128)S(1)} %get-tuple-element.28.current, ...), custom_call_target="tpu_custom_call" | custom-call | flops 9175040 | bytes 6422528 | tf_op jit(solution)/shard_map/pallas_call | solution.py:639
  18.2 0.5 collective-permute-start.2
  18.7 4.0 %collective-permute-start.3 = (f32[14,2,1024]{2,1,0:T(2,128)S(1)}, f32[14,2,1024]{2,1,0:T(2,128)S(1)}, u32[]{:S(2)}, u32[]{:S(2)}) collective-permute-start(f32[14,2,1024]{2,1,0:T(2,128)S(1)} %get-tuple-element.41), channel_id=1, source_target_pairs={{1,2},{2,1},{3,4},{4,3},{5,6},{6,5},{9,10},{10,9},{11,12},{12,11},... | collective-permute-start | bytes 344072 | tf_op jit(solution)/shard_map/ppermute | solution.py:574
  22.7 2.5 %shard_map.81.field_b = f32[3,7,32,1024]{3,2,1,0:T(8,128)S(1)} custom-call(f32[3,8,32,1024]{3,2,1,0:T(8,128)S(1)} %get-tuple-element.31.field_b.old_b.old, f32[3,14,32,1024]{3,2,1,0:T(8,128)S(1)} %get-tuple-element.28.current, f32[7,32,1024]{2,1,0:T(8,128)S(1)} %get-tuple-element.33.weight_b.weight, f32[2,32,1024]{2,1,0:T(8,128)S(1)} %get-tuple-element.38.flux, ...), custom_call_target="tpu_custom_call" | custom-call | flops 9175040 | bytes 6422528 | tf_op jit(solution)/shard_map/pallas_call | solution.py:649
  25.1 0.0 collective-permute-done.2.near
  25.1 0.1 collective-permute-done.3.far
  25.2 0.2 shard_map.82
  25.4 3.9 %collective-permute-start.5 = (f32[8,2,1024]{2,1,0:T(2,128)S(1)}, f32[8,2,1024]{2,1,0:T(2,128)S(1)}, u32[]{:S(2)}, u32[]{:S(2)}) collective-permute-start(f32[8,2,1024]{2,1,0:T(2,128)S(1)} %get-tuple-element.47), channel_id=1, source_target_pairs={{1,2},{2,1},{3,4},{4,3},{5,6},{6,5},{9,10},{10,9},{11,12},{12,11},... | collective-permute-start | bytes 196616 | tf_op jit(solution)/shard_map/ppermute | solution.py:574
  29.3 1.8 %shard_map.84 = (f32[2,4,2,32,1024]{4,3,2,1,0:T(8,128)S(1)}, f32[2,2,32,1024]{3,2,1,0:T(8,128)S(1)}, f32[8,2,1024]{2,1,0:T(2,128)S(1)}) custom-call(f32[2,2,32,1024]{3,2,1,0:T(8,128)S(1)} %get-tuple-element.44.traces, f32[2,4,2,32,1024]{4,3,2,1,0:T(8,128)S(1)} %get-tuple-element.39.aux), custom_call_target="tpu_custom_call" | custom-call | flops 10485760 | bytes 5505024 | tf_op jit(solution)/shard_map/pallas_call | solution.py:669
  31.2 0.1 collective-permute-start.4
  31.3 0.1 collective-permute-done.5.far
  31.3 3.7 %collective-permute-done.4.near = f32[8,2,1024]{2,1,0:T(2,128)S(1)} collective-permute-done((f32[8,2,1024]{2,1,0:T(2,128)S(1)}, f32[8,2,1024]{2,1,0:T(2,128)S(1)}, u32[]{:S(2)}, u32[]{:S(2)}) %collective-permute-start.4) | collective-permute-done | bytes 65568 | tf_op jit(solution)/shard_map/ppermute | solution.py:574
  35.1 0.1 shard_map.85
  35.1 4.3 %collective-permute-start.6 = (f32[2,32,1024]{2,1,0:T(8,128)S(1)}, f32[2,32,1024]{2,1,0:T(8,128)S(1)}, u32[]{:S(2)}, u32[]{:S(2)}) collective-permute-start(f32[2,32,1024]{2,1,0:T(8,128)S(1)} %get-tuple-element.48), channel_id=1, source_target_pairs={{0,8},{8,0},{16,24},{24,16},{1,9},{9,1},{17,25},{25,17},{2,10},{10... | collective-permute-start | bytes 786440 | tf_op jit(solution)/shard_map/ppermute | solution.py:574
  39.5 3.0 %collective-permute-start.7 = (f32[2,32,1024]{2,1,0:T(8,128)S(1)}, f32[2,32,1024]{2,1,0:T(8,128)S(1)}, u32[]{:S(2)}, u32[]{:S(2)}) collective-permute-start(f32[2,32,1024]{2,1,0:T(8,128)S(1)} %get-tuple-element.49), channel_id=1, source_target_pairs={{8,16},{16,8},{9,17},{17,9},{10,18},{18,10},{11,19},{19,11},{12,20... | collective-permute-start | bytes 786440 | tf_op jit(solution)/shard_map/ppermute | solution.py:574
  42.5 2.5 %shard_map.83 = f32[3,14,32,1024]{3,2,1,0:T(8,128)} custom-call(f32[3,7,32,1024]{3,2,1,0:T(8,128)S(1)} %get-tuple-element.37.field_a, f32[3,7,32,1024]{3,2,1,0:T(8,128)S(1)} %shard_map.81.field_b, f32[15,2,1024]{2,1,0:T(2,128)S(1)} %get-tuple-element.42.head, f32[15,3,1024]{2,1,0:T(4,128)S(1)} %get-tuple-element.43.tail), custom_call_target="tpu_custom_call" | custom-call | flops 458752 | bytes 5505024 | tf_op jit(solution)/shard_map/pallas_call | solution.py:679
  45.0 1.3 %shard_map.87 = f32[1,2,4,2,32,1024]{5,4,3,2,1,0:T(8,128)} custom-call(f32[2,4,2,32,1024]{4,3,2,1,0:T(8,128)S(1)} %get-tuple-element.50.fresh, f32[8,2,1024]{2,1,0:T(2,128)S(1)} %collective-permute-done.4.near, f32[8,2,1024]{2,1,0:T(2,128)S(1)} %collective-permute-done.5.far), custom_call_target="tpu_custom_call" | custom-call | flops 524288 | bytes 4194304 | tf_op jit(solution)/shard_map/pallas_call | solution.py:701
  46.4 0.0 collective-permute-done.6.even_side
  46.4 0.8 %collective-permute-done.7.odd_side = f32[2,32,1024]{2,1,0:T(8,128)S(1)} collective-permute-done((f32[2,32,1024]{2,1,0:T(8,128)S(1)}, f32[2,32,1024]{2,1,0:T(8,128)S(1)}, u32[]{:S(2)}, u32[]{:S(2)}) %collective-permute-start.7) | collective-permute-done | bytes 262176 | tf_op jit(solution)/shard_map/ppermute | solution.py:574
  47.2 0.8 %shard_map.86 = f32[1,2,2,32,1024]{4,3,2,1,0:T(8,128)} custom-call(f32[2,32,1024]{2,1,0:T(8,128)S(1)} %collective-permute-done.6.even_side, f32[2,32,1024]{2,1,0:T(8,128)S(1)} %collective-permute-done.7.odd_side), custom_call_target="tpu_custom_call" | custom-call | tf_op jit(solution)/shard_map/pallas_call | solution.py:711
Async XLA Ops:
  2.2 11.6 %collective-permute-start.1 = (f32[14,2,1024]{2,1,0:T(2,128)S(1)}, f32[14,2,1024]{2,1,0:T(2,128)S(1)}, u32[]{:S(2)}, u32[]{:S(2)}) collective-permute-start(f32[14,2,1024]{2,1,0:T(2,128)S(1)} %shard_map.78), channel_id=1, source_target_pairs={{1,2},{2,1},{3,4},{4,3},{5,6},{6,5},{9,10},{10,9},{11,12},{12,11},... | collective-permute-start | bytes 344072 | tf_op jit(solution)/shard_map/ppermute | solution.py:574
  11.4 3.7 %collective-permute-start = (f32[14,2,1024]{2,1,0:T(2,128)S(1)}, f32[14,2,1024]{2,1,0:T(2,128)S(1)}, u32[]{:S(2)}, u32[]{:S(2)}) collective-permute-start(f32[14,2,1024]{2,1,0:T(2,128)S(1)} %get-tuple-element.34), channel_id=1, source_target_pairs={{0,1},{1,0},{2,3},{3,2},{4,5},{5,4},{6,7},{7,6},{8,9},{9,8},{10,11... | collective-permute-start | bytes 344072 | tf_op jit(solution)/shard_map/ppermute | solution.py:574
  18.2 6.9 %collective-permute-start.2 = (f32[14,2,1024]{2,1,0:T(2,128)S(1)}, f32[14,2,1024]{2,1,0:T(2,128)S(1)}, u32[]{:S(2)}, u32[]{:S(2)}) collective-permute-start(f32[14,2,1024]{2,1,0:T(2,128)S(1)} %get-tuple-element.40), channel_id=1, source_target_pairs={{0,1},{1,0},{2,3},{3,2},{4,5},{5,4},{6,7},{7,6},{8,9},{9,8},{10,11... | collective-permute-start | bytes 344072 | tf_op jit(solution)/shard_map/ppermute | solution.py:574
  18.7 6.5 %collective-permute-start.3 = (f32[14,2,1024]{2,1,0:T(2,128)S(1)}, f32[14,2,1024]{2,1,0:T(2,128)S(1)}, u32[]{:S(2)}, u32[]{:S(2)}) collective-permute-start(f32[14,2,1024]{2,1,0:T(2,128)S(1)} %get-tuple-element.41), channel_id=1, source_target_pairs={{1,2},{2,1},{3,4},{4,3},{5,6},{6,5},{9,10},{10,9},{11,12},{12,11},... | collective-permute-start | bytes 344072 | tf_op jit(solution)/shard_map/ppermute | solution.py:574
  25.4 5.9 %collective-permute-start.5 = (f32[8,2,1024]{2,1,0:T(2,128)S(1)}, f32[8,2,1024]{2,1,0:T(2,128)S(1)}, u32[]{:S(2)}, u32[]{:S(2)}) collective-permute-start(f32[8,2,1024]{2,1,0:T(2,128)S(1)} %get-tuple-element.47), channel_id=1, source_target_pairs={{1,2},{2,1},{3,4},{4,3},{5,6},{6,5},{9,10},{10,9},{11,12},{12,11},... | collective-permute-start | bytes 196616 | tf_op jit(solution)/shard_map/ppermute | solution.py:574
  31.2 3.9 %collective-permute-start.4 = (f32[8,2,1024]{2,1,0:T(2,128)S(1)}, f32[8,2,1024]{2,1,0:T(2,128)S(1)}, u32[]{:S(2)}, u32[]{:S(2)}) collective-permute-start(f32[8,2,1024]{2,1,0:T(2,128)S(1)} %get-tuple-element.46), channel_id=1, source_target_pairs={{0,1},{1,0},{2,3},{3,2},{4,5},{5,4},{6,7},{7,6},{8,9},{9,8},{10,11... | collective-permute-start | bytes 196616 | tf_op jit(solution)/shard_map/ppermute | solution.py:574
  35.1 11.2 %collective-permute-start.6 = (f32[2,32,1024]{2,1,0:T(8,128)S(1)}, f32[2,32,1024]{2,1,0:T(8,128)S(1)}, u32[]{:S(2)}, u32[]{:S(2)}) collective-permute-start(f32[2,32,1024]{2,1,0:T(8,128)S(1)} %get-tuple-element.48), channel_id=1, source_target_pairs={{0,8},{8,0},{16,24},{24,16},{1,9},{9,1},{17,25},{25,17},{2,10},{10... | collective-permute-start | bytes 786440 | tf_op jit(solution)/shard_map/ppermute | solution.py:574
  39.5 7.7 %collective-permute-start.7 = (f32[2,32,1024]{2,1,0:T(8,128)S(1)}, f32[2,32,1024]{2,1,0:T(8,128)S(1)}, u32[]{:S(2)}, u32[]{:S(2)}) collective-permute-start(f32[2,32,1024]{2,1,0:T(8,128)S(1)} %get-tuple-element.49), channel_id=1, source_target_pairs={{8,16},{16,8},{9,17},{17,9},{10,18},{18,10},{11,19},{19,11},{12,20... | collective-permute-start | bytes 786440 | tf_op jit(solution)/shard_map/ppermute | solution.py:574

commit v3 on v2

--- a/solution.py
+++ b/solution.py
@@ -94,13 +94,14 @@
     return slice(i * SUB, (i + 1) * SUB), slice(c * LANE, (c + 1) * LANE)
 
 
-def pack_kernel(dims, electric, faces, far, block, top, sem):
+def pack_kernel(dims, electric, faces, aux, far, block, top, aux_block, sem):
     nz, ny, _ = dims
     even = is_even("tile")
     start = pl.multiple_of(jnp.where(even, 0, ny - SUB), SUB)
     copies = [
         pltpu.make_async_copy(electric.at[:, :, pl.ds(start, SUB)], block, sem.at[0]),
         pltpu.make_async_copy(faces.at[0, 1, 1, pl.ds(ny - SUB, SUB)], top, sem.at[1]),
+        pltpu.make_async_copy(aux.at[0, :, :, :, pl.ds(start, SUB)], aux_block, sem.at[2]),
     ]
     for copy in copies:
         copy.start()
@@ -112,6 +113,12 @@
         up = upward([block[k, z, end, :] for k in range(3)], y_above)
         for q in range(2):
             far[z, q : q + 1, :] = jnp.where(even, block[2 * q, z, 0:1, :], up[q])
+    for side in range(2):
+        for j in range(TERMS):
+            for k in range(2):
+                far[nz + side * TERMS + j, k : k + 1, :] = jnp.where(
+                    even, aux_block[side, j, k, 0:1, :], aux_block[side, j, k, end, :]
+                )
 
 
 def sweep_plane(load, above, current, weight, store, hx_s, hy_s, dims, from_mass):
@@ -197,14 +204,16 @@
 
 def first_lower_kernel(
     dims, electric, current_h, mass, faces, aux_h,
-    field, current, weight, ghost, aux, flux, near,
-    field_sem, current_sem, weight_sem, face_sem,
+    field, current, weight, ghost, flux, near,
+    block, top, aux_block, field_sem, current_sem, weight_sem, sem,
 ):
     nz, ny, _ = dims
     half = nz // 2
     even = is_even("tile")
     end = slice(ny - 1, ny)
+    tile_end = slice(SUB - 1, SUB)
     copy = pltpu.make_async_copy
+    row = pl.multiple_of(jnp.where(even, ny - SUB, 0), SUB)
 
     def field_copy(z):
         return copy(electric.at[:, pl.ds(z, 1)], field.at[:, pl.ds(z, 1)], field_sem.at[z])
@@ -215,9 +224,12 @@
     def weight_copy(z):
         return copy(mass.at[pl.ds(z, 1)], weight.at[pl.ds(z, 1)], weight_sem.at[z])
 
-    low_copy = copy(faces.at[0, 0], ghost, face_sem.at[0])
-    high_copies = [copy(faces.at[0, 1, k], field.at[k, nz], face_sem.at[1 + k]) for k in range(2)]
-    aux_copy = copy(aux_h.at[0], aux, face_sem.at[3])
+    low_copy = copy(faces.at[0, 0], ghost, sem.at[0])
+    edge_copies = [
+        copy(electric.at[:, pl.ds(half, nz - half), pl.ds(row, SUB)], block, sem.at[1]),
+        copy(faces.at[0, 1, 1, pl.ds(ny - SUB, SUB)], top, sem.at[2]),
+        copy(aux_h.at[0, :, :, :, pl.ds(row, SUB)], aux_block, sem.at[3]),
+    ]
     low_copy.start()
     field_copy(0).start()
 
@@ -227,17 +239,9 @@
         weight_copy(z).start()
         return carry
 
-    lax.fori_loop(0, nz - 1, start, 0)
-    current_copy(nz - 1).start()
-    weight_copy(nz - 1).start()
-    for high in high_copies:
-        high.start()
-    aux_copy.start()
-
-    def pack(z):
-        up = upward([field[k, z, end, :] for k in range(3)], field[1, z + 1, end, :])
-        for q in range(2):
-            near[z, q : q + 1, :] = jnp.where(even, up[q], field[2 * q, z, 0:1, :])
+    lax.fori_loop(0, half, start, 0)
+    for edge in edge_copies:
+        edge.start()
 
     low_copy.wait()
     field_copy(0).wait()
@@ -246,7 +250,9 @@
 
     def plane(z, carry):
         field_copy(z + 1).wait()
-        pack(z)
+        up = upward([field[k, z, end, :] for k in range(3)], field[1, z + 1, end, :])
+        for q in range(2):
+            near[z, q : q + 1, :] = jnp.where(even, up[q], field[2 * q, z, 0:1, :])
         current_copy(z).wait()
         weight_copy(z).wait()
         sweep_plane(
@@ -255,39 +261,79 @@
         return carry
 
     lax.fori_loop(0, half, plane, 0)
-
-    def rest(z, carry):
-        field_copy(z + 1).wait()
-        pack(z)
+    for edge in edge_copies:
+        edge.wait()
+    for z in range(nz - half):
+        y_above = block[1, z + 1, tile_end, :] if z + 1 < nz - half else top[tile_end, :]
+        up = upward([block[k, z, tile_end, :] for k in range(3)], y_above)
+        for q in range(2):
+            near[half + z, q : q + 1, :] = jnp.where(even, up[q], block[2 * q, z, 0:1, :])
+    for side in range(2):
+        for j in range(TERMS):
+            for k in range(2):
+                near[nz + side * TERMS + j, k : k + 1, :] = jnp.where(
+                    even, aux_block[side, j, k, tile_end, :], aux_block[side, j, k, 0:1, :]
+                )
+
+
+def first_upper_kernel(
+    dims, electric, current_h, mass, faces, aux_h, flux,
+    field, current, weight, aux,
+    flux_s, field_sem, current_sem, weight_sem, sem,
+):
+    nz, _, _ = dims
+    half = nz // 2
+    count = nz - half
+    copy = pltpu.make_async_copy
+
+    def field_copy(z):
+        return copy(electric.at[:, pl.ds(z + half, 1)], field.at[:, pl.ds(z, 1)], field_sem.at[z])
+
+    def current_copy(z):
+        return copy(current_h.at[:, pl.ds(z + half, 1)], current.at[:, pl.ds(z, 1)], current_sem.at[z])
+
+    def weight_copy(z):
+        return copy(mass.at[pl.ds(z + half, 1)], weight.at[pl.ds(z, 1)], weight_sem.at[z])
+
+    high_copies = [copy(faces.at[0, 1, k], field.at[k, count], sem.at[k]) for k in range(2)]
+    aux_copy = copy(aux_h.at[0], aux, sem.at[2])
+    field_copy(0).start()
+
+    def start(z, carry):
+        field_copy(z + 1).start()
+        current_copy(z).start()
+        weight_copy(z).start()
+        return carry
+
+    lax.fori_loop(0, count - 1, start, 0)
+    current_copy(count - 1).start()
+    weight_copy(count - 1).start()
+    for high in high_copies:
+        high.start()
+    aux_copy.start()
+    flux_s[...] = flux[...]
+    field_copy(0).wait()
+
+    def plane(z, carry):
+        @pl.when(z + 1 < count)
+        def _():
+            field_copy(z + 1).wait()
+
+        @pl.when(z + 1 == count)
+        def _():
+            for high in high_copies:
+                high.wait()
+
         current_copy(z).wait()
         weight_copy(z).wait()
-        return carry
-
-    lax.fori_loop(half, nz - 1, rest, 0)
-    for high in high_copies:
-        high.wait()
-    pack(nz - 1)
-    current_copy(nz - 1).wait()
-    weight_copy(nz - 1).wait()
-    aux_copy.wait()
-
-
-def first_upper_kernel(dims, old, current, mass, flux, field, weight, flux_s):
-    nz, _, _ = dims
-    half = nz // 2
-    flux_s[...] = flux[...]
-    for k in range(2):
-        field[k, nz - half] = old[k, nz]
-
-    def plane(z, carry):
-        weight[z] = mass[z + half]
         sweep_plane(
-            reader(old, z + half), reader(old, z + half + 1), reader(current, z + half),
+            reader(field, z), reader(field, z + 1), reader(current, z),
             weight.at[z], writer(field, z), flux_s.at[0], flux_s.at[1], dims, True,
         )
         return carry
 
-    lax.fori_loop(0, nz - half, plane, 0)
+    lax.fori_loop(0, count, plane, 0)
+    aux_copy.wait()
 
 
 class Planes:
@@ -301,12 +347,16 @@
         return self.upper[at[: self.dim] + (z - self.half,) + at[self.dim + 1 :]]
 
 
-def fix_pack_kernel(dims, field_a, field_b, weight_a, weight_b, near, far, head, tail, far_next):
-    nz, ny, _ = dims
+def fix_pack_kernel(
+    dims, field_a, field_b, current_a, current_b, weight_a, weight_b, ghost, near, far,
+    head, tail, far_next, near_extra,
+):
+    nz, ny, nx = dims
     half = nz // 2
     even = is_even("tile")
     end = slice(ny - 1, ny)
     field = Planes(field_a, field_b, half, 1)
+    current = Planes(current_a, current_b, half, 1)
     weight = Planes(weight_a, weight_b, half, 0)
     low, high = halo_views(near, far)
     for z in range(nz):
@@ -321,6 +371,51 @@
         for q in range(2):
             far_next[z, q : q + 1, :] = jnp.where(even, head[z, q : q + 1, :], up[q])
 
+    def value(k, z, r):
+        at = slice(r, r + 1)
+        if r in (-1, ny) or (k == 2 and z in (-1, nz)):
+            return jnp.zeros((1, nx), F32)
+        if z == -1:
+            return ghost[k, at, :]
+        if r == 0 and k != 1:
+            return head[z, k // 2 : k // 2 + 1, :]
+        if r == ny - 1:
+            return tail[z, k : k + 1, :]
+        return field[k, z, at, :]
+
+    def flux_x(z, r):
+        return (value(2, z, r + 1) - value(2, z, r)) - (value(1, z + 1, r) - value(1, z, r))
+
+    def flux_y(z, r):
+        here = value(2, z, r)
+        return (value(0, z + 1, r) - value(0, z, r)) - (row_next(here) - here)
+
+    def flux_z(z, r):
+        here = value(1, z, r)
+        return (row_next(here) - here) - (value(0, z, r + 1) - value(0, z, r))
+
+    def trace(z, r):
+        at = slice(r, r + 1)
+        hz = flux_z(z, r)
+        cx = (hz - flux_z(z, r - 1)) - (flux_y(z, r) - flux_y(z - 1, r))
+        cy = (flux_x(z, r) - flux_x(z - 1, r)) - (hz - row_prev(hz))
+        w = weight[z, at, :]
+        keep = 4.0 * w + 0.5
+        return (
+            keep * value(0, z, r) + w * (current[0, z, at, :] - cx),
+            keep * value(1, z, r) + w * (current[1, z, at, :] - cy),
+            w,
+        )
+
+    for side in range(2):
+        z = (nz - 1) * side
+        down, up = trace(z, 0), trace(z, ny - 1)
+        for k in range(2):
+            far_next[nz + side, k : k + 1, :] = jnp.where(even, down[k], up[k])
+            near_extra[side, k : k + 1, :] = jnp.where(even, up[k], down[k])
+        far_next[nz + 2, side : side + 1, :] = jnp.where(even, down[2], up[2])
+        near_extra[2, side : side + 1, :] = jnp.where(even, up[2], down[2])
+
 
 def edged_reader(ref, z, head, tail, plane, ny):
     rows = ny // SUB
@@ -338,7 +433,9 @@
     return load
 
 
-def second_lower_kernel(dims, old_a, old_b, current, weight, ghost, head, tail, field, flux, near_next):
+def second_lower_kernel(
+    dims, old_a, old_b, current, weight, ghost, head, tail, near_extra, field, flux, near_next
+):
     nz, ny, _ = dims
     half = nz // 2
     even = is_even("tile")
@@ -346,6 +443,7 @@
         up = upward([tail[z, k : k + 1, :] for k in range(3)], tail[z + 1, 1:2, :])
         for q in range(2):
             near_next[z, q : q + 1, :] = jnp.where(even, up[q], head[z, q : q + 1, :])
+    near_next[nz : nz + 3] = near_extra[...]
     hx_s, hy_s = flux.at[0], flux.at[1]
     ghost_flux(edged_reader(old_a, 0, head, tail, 0, ny), ghost, hx_s, hy_s, dims)
 
@@ -372,7 +470,7 @@
         at = z + half
         sweep_plane(
             edged_reader(old, z, head, tail, at, ny), edged_reader(old, z + 1, head, tail, at + 1, ny),
-            reader(current, at), weight.at[z], writer(field, z), flux_s.at[0], flux_s.at[1], dims, False,
+            reader(current, z), weight.at[z], writer(field, z), flux_s.at[0], flux_s.at[1], dims, False,
         )
         return carry
 
@@ -380,15 +478,16 @@
 
 
 def fix_trace_kernel(
-    dims, field_a, field_b, weight_a, weight_b, aux, near, far, head, tail, traces, far_next
+    dims, field_a, field_b, weight_a, weight_b, near1, far1, head1, tail1, near, far,
+    head, tail, traces, below, above,
 ):
     nz, ny, _ = dims
     half = nz // 2
-    even = is_even("tile")
     end = slice(ny - 1, ny)
     field = Planes(field_a, field_b, half, 1)
     weight = Planes(weight_a, weight_b, half, 0)
     low, high = halo_views(near, far)
+    low1, high1 = halo_views(near1, far1)
     for side in range(2):
         z = (nz - 1) * side
         for k in range(2):
@@ -402,27 +501,32 @@
             traces[side, 0, 0:1, :] = head[z, 0:1, :]
             traces[side, 0, end, :] = x
             traces[side, 1, end, :] = y
-    pack_combined(even, traces, aux, far_next, ny, False)
-
-
-def pack_combined(even, traces, aux, send, ny, up_from_even):
-    end = slice(ny - 1, ny)
     for side in range(2):
+        z = (nz - 1) * side
+        x, zc = head1[z, 0:1, :], head1[z, 1:2, :]
+        rise = zc - head1[z - 1, 1:2, :] if z else zc
+        w = low[nz + 2, side : side + 1, :]
+        trace_low = (
+            low[nz + side, 0:1, :] + w * x,
+            low[nz + side, 1:2, :] - w * (rise + (x - row_prev(x))),
+        )
+        y = tail1[z, 1:2, :]
+        w = high[nz + 2, side : side + 1, :]
+        trace_high = (
+            high[nz + side, 0:1, :] + w * (row_next(y) - y + tail1[z, 0:1, :]),
+            high[nz + side, 1:2, :],
+        )
         for k in range(2):
-            first = traces[side, k, 0:1, :]
-            last = traces[side, k, end, :]
             for j in range(TERMS):
-                down = first - pade_decays[j] * aux[side, j, k, 0:1, :]
-                up = last - pade_decays[j] * aux[side, j, k, end, :]
-                pair = (up, down) if up_from_even else (down, up)
-                send[side * TERMS + j, k : k + 1, :] = jnp.where(even, *pair)
-
-
-def surface_kernel(dims, traces, aux, fresh, outgoing, near_next):
+                at = side * TERMS + j
+                below[at, k : k + 1, :] = trace_low[k] - pade_decays[j] * low1[nz + at, k : k + 1, :]
+                above[at, k : k + 1, :] = trace_high[k] - pade_decays[j] * high1[nz + at, k : k + 1, :]
+
+
+def surface_kernel(dims, traces, aux, below, above, fresh, even_side, odd_side, outgoing):
     _, ny, nx = dims
     rows, cols = ny // SUB, nx // LANE
     is_first_lane, is_last_lane, is_first_sub, is_last_sub = lane_masks()
-    pack_combined(is_even("tile"), traces, aux, near_next, ny, True)
 
     def part(side, carry):
         outgoing[side] = traces[side]
@@ -469,6 +573,16 @@
         return lax.fori_loop(0, TERMS, term, carry)
 
     lax.fori_loop(0, 2, part, 0)
+    for side in range(2):
+        for k in range(2):
+            for source, r in ((below, slice(0, 1)), (above, slice(ny - 1, ny))):
+                total = 0.0
+                for j in range(TERMS):
+                    total = total + (0.125 * pade_weights[j]) * source[side * TERMS + j, k : k + 1, :]
+                outgoing[side, k, r, :] -= total
+    even = is_even("slab")
+    even_side[...] = jnp.where(even, outgoing[1], outgoing[0])
+    odd_side[...] = jnp.where(even, outgoing[0], outgoing[1])
 
 
 def write_kernel(dims, field_a, field_b, head, tail, smoothed, edges, sem):
@@ -509,22 +623,6 @@
         copy.wait()
 
 
-def close_kernel(dims, zero_halo, near, far, even_side, odd_side, outgoing):
-    _, ny, _ = dims
-    low, high = halo_views(near, far)
-    for side in range(2):
-        for k in range(2):
-            outgoing[side, k] = zero_halo[side, k]
-            for source, r in ((low, slice(0, 1)), (high, slice(ny - 1, ny))):
-                total = 0.0
-                for j in range(TERMS):
-                    total = total + (0.125 * pade_weights[j]) * source[side * TERMS + j, k : k + 1, :]
-                outgoing[side, k, r, :] = zero_halo[side, k, r, :] - total
-    even = is_even("slab")
-    even_side[...] = jnp.where(even, outgoing[1], outgoing[0])
-    odd_side[...] = jnp.where(even, outgoing[0], outgoing[1])
-
-
 def faces_kernel(even_side, odd_side, out, sem):
     below = jnp.where(is_even("slab"), 0, 1)
     copies = [
@@ -537,9 +635,8 @@
         copy.wait()
 
 
-def store_kernel(dims, fresh, near, far, out, edges, sem):
+def store_kernel(dims, fresh, low, high, out, edges, sem):
     _, ny, nx = dims
-    low, high = halo_views(near, far)
     inner = pl.ds(SUB, ny - 2 * SUB)
     middle = pltpu.make_async_copy(fresh.at[:, :, :, inner], out.at[0, :, :, :, inner], sem.at[0])
     middle.start()
@@ -580,101 +677,110 @@
     dims = (nz, ny, nx)
     cells = nz * ny * nx
     bind = functools.partial
-    rows = shape(nz, 2, nx)
+    rows1, rows2 = shape(nz + 2 * TERMS, 2, nx), shape(nz + 3, 2, nx)
     flux_shape = shape(2, ny, nx)
     dma = pltpu.SemaphoreType.DMA
     electric, current, mass, faces, aux = (
         pltpu.with_memory_space_constraint(a, pltpu.HBM) for a in (electric, current, mass, faces, aux)
     )
+    aux_block = vm(2, TERMS, 2, SUB, nx)
+    count = nz - half
 
     far1 = call(
         bind(pack_kernel, dims),
-        out_shape=rows,
-        in_specs=[HBM] * 2,
+        out_shape=rows1,
+        in_specs=[HBM] * 3,
         out_specs=VM,
-        scratch_shapes=[vm(3, nz, SUB, nx), vm(SUB, nx), dma((2,))],
+        scratch_shapes=[vm(3, nz, SUB, nx), vm(SUB, nx), aux_block, dma((3,))],
         compiler_params=params(12),
-    )(electric, faces)
+    )(electric, faces, aux)
     far1 = swap(far1, "tile", 1)
 
-    field, current_v, weight, ghost, aux_v, flux, near1 = call(
+    lower, current_a, weight_a, ghost, flux, near1 = call(
         bind(first_lower_kernel, dims),
         out_shape=(
-            shape(3, nz + 1, ny, nx),
-            shape(3, nz, ny, nx),
-            shape(nz, ny, nx),
-            shape(2, ny, nx),
-            shape(2, TERMS, 2, ny, nx),
+            shape(3, half + 1, ny, nx),
+            shape(3, half, ny, nx),
+            shape(half, ny, nx),
             flux_shape,
-            rows,
+            flux_shape,
+            rows1,
         ),
         in_specs=[HBM] * 5,
-        out_specs=(VM,) * 7,
-        scratch_shapes=[dma((nz,)), dma((nz,)), dma((nz,)), dma((4,))],
-        compiler_params=params(24),
-        cost_estimate=cost(25 * cells, 28 * cells),
+        out_specs=(VM,) * 6,
+        scratch_shapes=[vm(3, count, SUB, nx), vm(SUB, nx), aux_block]
+        + [dma((half + 1,)), dma((half,)), dma((half,)), dma((4,))],
+        compiler_params=params(16),
+        cost_estimate=cost(25 * cells, 14 * cells),
     )(electric, current, mass, faces, aux)
     near1 = swap(near1, "tile", 0)
 
-    upper, weight_u = call(
+    upper, current_b, weight_b, aux_v = call(
         bind(first_upper_kernel, dims),
-        out_shape=(shape(3, nz - half + 1, ny, nx), shape(nz - half, ny, nx)),
-        in_specs=[VM] * 4,
-        out_specs=(VM,) * 2,
-        scratch_shapes=[vm(2, ny, nx)],
+        out_shape=(
+            shape(3, count + 1, ny, nx),
+            shape(3, count, ny, nx),
+            shape(count, ny, nx),
+            shape(2, TERMS, 2, ny, nx),
+        ),
+        in_specs=[HBM] * 5 + [VM],
+        out_specs=(VM,) * 4,
+        scratch_shapes=[vm(2, ny, nx), dma((count,)), dma((count,)), dma((count,)), dma((3,))],
+        compiler_params=params(16),
+        cost_estimate=cost(25 * cells, 14 * cells),
+    )(electric, current, mass, faces, aux, flux)
+
+    heads, tails = shape(nz + 1, 2, nx), shape(nz + 1, 3, nx)
+    head1, tail1, far2, near_extra = call(
+        bind(fix_pack_kernel, dims),
+        out_shape=(heads, tails, rows2, shape(3, 2, nx)),
+        in_specs=[VM] * 9,
+        out_specs=(VM,) * 4,
         compiler_params=params(12),
-        cost_estimate=cost(25 * cells, 14 * cells),
-    )(field, current_v, weight, flux)
-
-    heads, tails = shape(nz + 1, 2, nx), shape(nz + 1, 3, nx)
-    head, tail, far2 = call(
-        bind(fix_pack_kernel, dims),
-        out_shape=(heads, tails, rows),
-        in_specs=[VM] * 6,
-        out_specs=(VM,) * 3,
-        compiler_params=params(12),
-    )(field, upper, weight, weight_u, near1, far1)
+    )(lower, upper, current_a, current_b, weight_a, weight_b, ghost, near1, far1)
     far2 = swap(far2, "tile", 1)
 
     lower2, flux, near2 = call(
         bind(second_lower_kernel, dims),
-        out_shape=(shape(3, half, ny, nx), flux_shape, rows),
-        in_specs=[VM] * 7,
+        out_shape=(shape(3, half, ny, nx), flux_shape, rows2),
+        in_specs=[VM] * 8,
         out_specs=(VM,) * 3,
         compiler_params=params(12),
         cost_estimate=cost(20 * cells, 14 * cells),
-    )(field, upper, current_v, weight, ghost, head, tail)
+    )(lower, upper, current_a, weight_a, ghost, head1, tail1, near_extra)
     near2 = swap(near2, "tile", 0)
 
     upper2 = call(
         bind(second_upper_kernel, dims),
-        out_shape=shape(3, nz - half, ny, nx),
+        out_shape=shape(3, count, ny, nx),
         in_specs=[VM] * 6,
         out_specs=VM,
         scratch_shapes=[vm(2, ny, nx)],
         compiler_params=params(12),
         cost_estimate=cost(20 * cells, 14 * cells),
-    )(upper, current_v, weight_u, flux, head, tail)
+    )(upper, current_b, weight_b, flux, head1, tail1)
 
     edge_rows = shape(2 * TERMS, 2, nx)
-    head, tail, traces, far3 = call(
+    head, tail, traces, below, above = call(
         bind(fix_trace_kernel, dims),
-        out_shape=(heads, tails, shape(2, 2, ny, nx), edge_rows),
-        in_specs=[VM] * 7,
-        out_specs=(VM,) * 4,
+        out_shape=(heads, tails, shape(2, 2, ny, nx), edge_rows, edge_rows),
+        in_specs=[VM] * 10,
+        out_specs=(VM,) * 5,
         compiler_params=params(12),
-    )(lower2, upper2, weight, weight_u, aux_v, near2, far2)
-    far3 = swap(far3, "tile", 1)
-
-    fresh, outgoing, near3 = call(
+    )(lower2, upper2, weight_a, weight_b, near1, far1, head1, tail1, near2, far2)
+
+    side_shape = shape(2, ny, nx)
+    fresh, even_side, odd_side = call(
         bind(surface_kernel, dims),
-        out_shape=(shape(2, TERMS, 2, ny, nx), shape(2, 2, ny, nx), edge_rows),
-        in_specs=[VM] * 2,
+        out_shape=(shape(2, TERMS, 2, ny, nx), side_shape, side_shape),
+        in_specs=[VM] * 4,
         out_specs=(VM,) * 3,
+        scratch_shapes=[vm(2, 2, ny, nx)],
         compiler_params=params(12),
         cost_estimate=cost(20 * 16 * ny * nx, 12 * cells),
-    )(traces, aux_v)
-    near3 = swap(near3, "tile", 0)
+    )(traces, aux_v, below, above)
+    odd_side = swap(odd_side, "slab", 1)
+    even_side = swap(even_side, "slab", 0)
 
     smoothed = call(
         bind(write_kernel, dims),
@@ -686,18 +792,6 @@
         cost_estimate=cost(cells, 12 * cells),
     )(lower2, upper2, head, tail)
 
-    side_shape = shape(2, ny, nx)
-    even_side, odd_side = call(
-        bind(close_kernel, dims),
-        out_shape=(side_shape, side_shape),
-        in_specs=[VM] * 3,
-        out_specs=(VM,) * 2,
-        scratch_shapes=[vm(2, 2, ny, nx)],
-        compiler_params=params(8),
-    )(outgoing, near3, far3)
-    odd_side = swap(odd_side, "slab", 1)
-    even_side = swap(even_side, "slab", 0)
-
     fresh = call(
         bind(store_kernel, dims),
         out_shape=shape(1, 2, TERMS, 2, ny, nx),
@@ -706,7 +800,7 @@
         scratch_shapes=[vm(2, 2, TERMS, 2, SUB, nx), dma((3,))],
         compiler_params=params(8),
         cost_estimate=cost(16 * ny * nx, 8 * 16 * ny * nx),
-    )(fresh, near3, far3)
+    )(fresh, below, above)
 
     next_faces = call(
         faces_kernel,

time: 48.5 us -> 40.9 us (0.84)
  the two profiles are of different devices: /device:TPU:3 before, /device:TPU:9 now
where the time goes in v3:
time: 40.9 us; the launch traced here: 40.7 us
  Pallas kernels  23 us (56%)
  starting transfers between devices  14.2 us (35%)
  waiting for transfers between devices  2.84 us (7%)
  between operations  0.76 us (2%)
    ppermute x6, starting transfers between devices, swap(): lax.ppermute(block, axis, [p for i, j in pairs for p in ((i, j), (j, i))])  14.2 us
    pallas_call x1, Pallas kernels, iteration(): call(bind(first_lower_kernel, dims), out_shape=(shape(3, half + 1, ny, nx...  4.72 us
    pallas_call x1, Pallas kernels, iteration(): call(bind(first_upper_kernel, dims), out_shape=(shape(3, count + 1, ny, n...  3.9 us
    ppermute x6, waiting for transfers between devices, swap(): lax.ppermute(block, axis, [p for i, j in pairs for p in ((i, j), (j, i))])  2.84 us
    pallas_call x1, Pallas kernels, iteration(): call(bind(second_lower_kernel, dims), out_shape=(shape(3, half, ny, nx),...  2.75 us
    pallas_call x1, Pallas kernels, iteration(): call(bind(second_upper_kernel, dims), out_shape=shape(3, count, ny, nx),...  2.53 us
    pallas_call x1, Pallas kernels, iteration(): call(bind(write_kernel, dims), out_shape=shape(3, nz, ny, nx), in_specs=[...  2.49 us
    pallas_call x1, Pallas kernels, iteration(): call(bind(surface_kernel, dims), out_shape=(shape(2, TERMS, 2, ny, nx), s...  1.86 us
  transfers between devices with their start and end apart: 6, of which 2 were waited for; matrix products, arithmetic and copies ran while one was open for 0% of the time, Pallas kernels for 37%

profile of v3, /device:TPU:9, one launch (start us, length us, event | category | flops | bytes accessed | tf_op | source)
XLA Modules:
  0.0 40.7 jit_solution(16017372339293351216)
XLA Ops:
  0.6 1.7 %shard_map.78 = f32[22,2,1024]{2,1,0:T(2,128)S(1)} custom-call(f32[3,14,32,1024]{3,2,1,0:T(8,128)} %electric.5, f32[1,2,2,32,1024]{4,3,2,1,0:T(8,128)} %faces.5, f32[1,2,4,2,32,1024]{5,4,3,2,1,0:T(8,128)} %aux.1), custom_call_target="tpu_custom_call" | custom-call | tf_op jit(solution)/shard_map/pallas_call | solution.py:689
  2.4 3.0 %collective-permute-start.1 = (f32[22,2,1024]{2,1,0:T(2,128)S(1)}, f32[22,2,1024]{2,1,0:T(2,128)S(1)}, u32[]{:S(2)}, u32[]{:S(2)}) collective-permute-start(f32[22,2,1024]{2,1,0:T(2,128)S(1)} %shard_map.78), channel_id=1, source_target_pairs={{1,2},{2,1},{3,4},{4,3},{5,6},{6,5},{9,10},{10,9},{11,12},{12,11},... | collective-permute-start | bytes 540680 | tf_op jit(solution)/shard_map/ppermute | solution.py:671
  5.4 4.7 %shard_map.76 = (f32[3,8,32,1024]{3,2,1,0:T(8,128)S(1)}, f32[3,7,32,1024]{3,2,1,0:T(8,128)S(1)}, f32[7,32,1024]{2,1,0:T(8,128)S(1)}, f32[2,32,1024]{2,1,0:T(8,12...) custom-call(f32[3,14,32,1024]{3,2,1,0:T(8,128)} %electric.5, f32[3,14,32,1024]{3,2,1,0:T(8,128)} %current_h.3, ...), custom_call_target="tpu_custom_call" | custom-call | flops 11468800 | bytes 6422528 | tf_op jit(solution)/shard_map/pallas_call | solution.py:699
  10.1 1.4 %collective-permute-start = (f32[22,2,1024]{2,1,0:T(2,128)S(1)}, f32[22,2,1024]{2,1,0:T(2,128)S(1)}, u32[]{:S(2)}, u32[]{:S(2)}) collective-permute-start(f32[22,2,1024]{2,1,0:T(2,128)S(1)} %get-tuple-element.36), channel_id=1, source_target_pairs={{0,1},{1,0},{2,3},{3,2},{4,5},{5,4},{6,7},{7,6},{8,9},{9,8},{10,11... | collective-permute-start | bytes 540680 | tf_op jit(solution)/shard_map/ppermute | solution.py:671
  11.6 3.9 %shard_map.77 = (f32[3,8,32,1024]{3,2,1,0:T(8,128)S(1)}, f32[3,7,32,1024]{3,2,1,0:T(8,128)S(1)}, f32[7,32,1024]{2,1,0:T(8,128)S(1)}, f32[2,4,2,32,1024]{4,3,2,1,0:T(8,128)S(1)}) custom-call(f32[3,14,32,1024]{3,2,1,0:T(8,128)} %electric.5, f32[3,14,32,1024]{3,2,1,0:T(8,128)} %current_h.3, f32[14,32,1024]{2,1,0:T(8,128)} %mass.3, ...), custom_call_target="tpu_custom_call" | custom-call | flops 11468800 | bytes 6422528 | tf_op jit(solution)/shard_map/pallas_call | solution.py:718
  15.5 0.0 collective-permute-done.1.far.far1
  15.5 0.0 collective-permute-done.near.near1
  15.5 0.6 %shard_map.79 = (f32[15,2,1024]{2,1,0:T(2,128)S(1)}, f32[15,3,1024]{2,1,0:T(4,128)S(1)}, f32[17,2,1024]{2,1,0:T(2,128)S(1)}, f32[3,2,1024]{2,1,0:T(2,128)S(1)}) custom-call(f32[3,8,32,1024]{3,2,1,0:T(8,128)S(1)} %get-tuple-element.28.field_a.old_a, f32[3,8,32,1024]{3,2,1,0:T(8,128)S(1)} %get-tuple-element.30.field_b.old_b.old, ...), custom_call_target="tpu_custom_call" | custom-call | tf_op jit(solution)/shard_map/pallas_call | solution.py:734
  16.1 2.7 %shard_map.80 = (f32[3,7,32,1024]{3,2,1,0:T(8,128)S(1)}, f32[2,32,1024]{2,1,0:T(8,128)S(1)}, f32[17,2,1024]{2,1,0:T(2,128)S(1)}) custom-call(f32[3,8,32,1024]{3,2,1,0:T(8,128)S(1)} %get-tuple-element.28.field_a.old_a, f32[3,8,32,1024]{3,2,1,0:T(8,128)S(1)} %get-tuple-element.30.field_b.old_b.old, f32[3,7,32,1024]{3,2,1,0:T(8,128)S(1)} %get-tuple-element.31.current_a.current, ...), custom_call_target="tpu_custom_call" | custom-call | flops 9175040 | bytes 6422528 | tf_op jit(solution)/shard_map/pallas_call | solution.py:743
  18.8 1.3 %collective-permute-start.2 = (f32[17,2,1024]{2,1,0:T(2,128)S(1)}, f32[17,2,1024]{2,1,0:T(2,128)S(1)}, u32[]{:S(2)}, u32[]{:S(2)}) collective-permute-start(f32[17,2,1024]{2,1,0:T(2,128)S(1)} %get-tuple-element.42), channel_id=1, source_target_pairs={{0,1},{1,0},{2,3},{3,2},{4,5},{5,4},{6,7},{7,6},{8,9},{9,8},{10,11... | collective-permute-start | bytes 417800 | tf_op jit(solution)/shard_map/ppermute | solution.py:671
  20.1 2.1 %collective-permute-start.3 = (f32[17,2,1024]{2,1,0:T(2,128)S(1)}, f32[17,2,1024]{2,1,0:T(2,128)S(1)}, u32[]{:S(2)}, u32[]{:S(2)}) collective-permute-start(f32[17,2,1024]{2,1,0:T(2,128)S(1)} %get-tuple-element.43), channel_id=1, source_target_pairs={{1,2},{2,1},{3,4},{4,3},{5,6},{6,5},{9,10},{10,9},{11,12},{12,11},... | collective-permute-start | bytes 417800 | tf_op jit(solution)/shard_map/ppermute | solution.py:671
  22.2 2.5 %shard_map.81.field_b = f32[3,7,32,1024]{3,2,1,0:T(8,128)S(1)} custom-call(f32[3,8,32,1024]{3,2,1,0:T(8,128)S(1)} %get-tuple-element.30.field_b.old_b.old, f32[3,7,32,1024]{3,2,1,0:T(8,128)S(1)} %get-tuple-element.34.current_b.current, f32[7,32,1024]{2,1,0:T(8,128)S(1)} %get-tuple-element.35.weight_b.weight, f32[2,32,1024]{2,1,0:T(8,128)S(1)} %get-tuple-element.41.flux, ...), custom_call_target="tpu_custom_call" | custom-call | flops 9175040 | bytes 6422528 | tf_op jit(solution)/shard_map/pallas_call | solution.py:753
  24.7 0.0 collective-permute-done.2.near
  24.7 2.1 %collective-permute-done.3.far = f32[17,2,1024]{2,1,0:T(2,128)S(1)} collective-permute-done((f32[17,2,1024]{2,1,0:T(2,128)S(1)}, f32[17,2,1024]{2,1,0:T(2,128)S(1)}, u32[]{:S(2)}, u32[]{:S(2)}) %collective-permute-start.3) | collective-permute-done | bytes 139296 | tf_op jit(solution)/shard_map/ppermute | solution.py:671
  26.8 0.3 shard_map.82
  27.1 1.9 %shard_map.84 = (f32[2,4,2,32,1024]{4,3,2,1,0:T(8,128)S(1)}, f32[2,32,1024]{2,1,0:T(8,128)S(1)}, f32[2,32,1024]{2,1,0:T(8,128)S(1)}) custom-call(f32[2,2,32,1024]{3,2,1,0:T(8,128)S(1)} %get-tuple-element.46.traces, f32[2,4,2,32,1024]{4,3,2,1,0:T(8,128)S(1)} %get-tuple-element.47.aux, f32[8,2,1024]{2,1,0:T(2,128)S(1)} %get-tuple-element.48.below.low, ...), custom_call_target="tpu_custom_call" | custom-call | flops 10485760 | bytes 5505024 | tf_op jit(solution)/shard_map/pallas_call | solution.py:773
  28.9 3.3 %collective-permute-start.4 = (f32[2,32,1024]{2,1,0:T(8,128)S(1)}, f32[2,32,1024]{2,1,0:T(8,128)S(1)}, u32[]{:S(2)}, u32[]{:S(2)}) collective-permute-start(f32[2,32,1024]{2,1,0:T(8,128)S(1)} %get-tuple-element.50), channel_id=1, source_target_pairs={{0,8},{8,0},{16,24},{24,16},{1,9},{9,1},{17,25},{25,17},{2,10},{10... | collective-permute-start | bytes 786440 | tf_op jit(solution)/shard_map/ppermute | solution.py:671
  32.2 3.0 %collective-permute-start.5 = (f32[2,32,1024]{2,1,0:T(8,128)S(1)}, f32[2,32,1024]{2,1,0:T(8,128)S(1)}, u32[]{:S(2)}, u32[]{:S(2)}) collective-permute-start(f32[2,32,1024]{2,1,0:T(8,128)S(1)} %get-tuple-element.51), channel_id=1, source_target_pairs={{8,16},{16,8},{9,17},{17,9},{10,18},{18,10},{11,19},{19,11},{12,20... | collective-permute-start | bytes 786440 | tf_op jit(solution)/shard_map/ppermute | solution.py:671
  35.3 2.5 %shard_map.83 = f32[3,14,32,1024]{3,2,1,0:T(8,128)} custom-call(f32[3,7,32,1024]{3,2,1,0:T(8,128)S(1)} %get-tuple-element.40.field_a, f32[3,7,32,1024]{3,2,1,0:T(8,128)S(1)} %shard_map.81.field_b, f32[15,2,1024]{2,1,0:T(2,128)S(1)} %get-tuple-element.44.head, f32[15,3,1024]{2,1,0:T(4,128)S(1)} %get-tuple-element.45.tail), custom_call_target="tpu_custom_call" | custom-call | flops 458752 | bytes 5505024 | tf_op jit(solution)/shard_map/pallas_call | solution.py:785
  37.8 1.3 %shard_map.86 = f32[1,2,4,2,32,1024]{5,4,3,2,1,0:T(8,128)} custom-call(f32[2,4,2,32,1024]{4,3,2,1,0:T(8,128)S(1)} %get-tuple-element.52.fresh, f32[8,2,1024]{2,1,0:T(2,128)S(1)} %get-tuple-element.48.below.low, f32[8,2,1024]{2,1,0:T(2,128)S(1)} %get-tuple-element.49.above.high), custom_call_target="tpu_custom_call" | custom-call | flops 524288 | bytes 4194304 | tf_op jit(solution)/shard_map/pallas_call | solution.py:795
  39.2 0.0 collective-permute-done.4.even_side
  39.2 0.8 %collective-permute-done.5.odd_side = f32[2,32,1024]{2,1,0:T(8,128)S(1)} collective-permute-done((f32[2,32,1024]{2,1,0:T(8,128)S(1)}, f32[2,32,1024]{2,1,0:T(8,128)S(1)}, u32[]{:S(2)}, u32[]{:S(2)}) %collective-permute-start.5) | collective-permute-done | bytes 262176 | tf_op jit(solution)/shard_map/ppermute | solution.py:671
  39.9 0.8 %shard_map.85 = f32[1,2,2,32,1024]{4,3,2,1,0:T(8,128)} custom-call(f32[2,32,1024]{2,1,0:T(8,128)S(1)} %collective-permute-done.4.even_side, f32[2,32,1024]{2,1,0:T(8,128)S(1)} %collective-permute-done.5.odd_side), custom_call_target="tpu_custom_call" | custom-call | tf_op jit(solution)/shard_map/pallas_call | solution.py:805
Async XLA Ops:
  2.4 13.1 %collective-permute-start.1 = (f32[22,2,1024]{2,1,0:T(2,128)S(1)}, f32[22,2,1024]{2,1,0:T(2,128)S(1)}, u32[]{:S(2)}, u32[]{:S(2)}) collective-permute-start(f32[22,2,1024]{2,1,0:T(2,128)S(1)} %shard_map.78), channel_id=1, source_target_pairs={{1,2},{2,1},{3,4},{4,3},{5,6},{6,5},{9,10},{10,9},{11,12},{12,11},... | collective-permute-start | bytes 540680 | tf_op jit(solution)/shard_map/ppermute | solution.py:671
  10.1 5.4 %collective-permute-start = (f32[22,2,1024]{2,1,0:T(2,128)S(1)}, f32[22,2,1024]{2,1,0:T(2,128)S(1)}, u32[]{:S(2)}, u32[]{:S(2)}) collective-permute-start(f32[22,2,1024]{2,1,0:T(2,128)S(1)} %get-tuple-element.36), channel_id=1, source_target_pairs={{0,1},{1,0},{2,3},{3,2},{4,5},{5,4},{6,7},{7,6},{8,9},{9,8},{10,11... | collective-permute-start | bytes 540680 | tf_op jit(solution)/shard_map/ppermute | solution.py:671
  18.8 5.9 %collective-permute-start.2 = (f32[17,2,1024]{2,1,0:T(2,128)S(1)}, f32[17,2,1024]{2,1,0:T(2,128)S(1)}, u32[]{:S(2)}, u32[]{:S(2)}) collective-permute-start(f32[17,2,1024]{2,1,0:T(2,128)S(1)} %get-tuple-element.42), channel_id=1, source_target_pairs={{0,1},{1,0},{2,3},{3,2},{4,5},{5,4},{6,7},{7,6},{8,9},{9,8},{10,11... | collective-permute-start | bytes 417800 | tf_op jit(solution)/shard_map/ppermute | solution.py:671
  20.1 6.7 %collective-permute-start.3 = (f32[17,2,1024]{2,1,0:T(2,128)S(1)}, f32[17,2,1024]{2,1,0:T(2,128)S(1)}, u32[]{:S(2)}, u32[]{:S(2)}) collective-permute-start(f32[17,2,1024]{2,1,0:T(2,128)S(1)} %get-tuple-element.43), channel_id=1, source_target_pairs={{1,2},{2,1},{3,4},{4,3},{5,6},{6,5},{9,10},{10,9},{11,12},{12,11},... | collective-permute-start | bytes 417800 | tf_op jit(solution)/shard_map/ppermute | solution.py:671
  28.9 10.2 %collective-permute-start.4 = (f32[2,32,1024]{2,1,0:T(8,128)S(1)}, f32[2,32,1024]{2,1,0:T(8,128)S(1)}, u32[]{:S(2)}, u32[]{:S(2)}) collective-permute-start(f32[2,32,1024]{2,1,0:T(8,128)S(1)} %get-tuple-element.50), channel_id=1, source_target_pairs={{0,8},{8,0},{16,24},{24,16},{1,9},{9,1},{17,25},{25,17},{2,10},{10... | collective-permute-start | bytes 786440 | tf_op jit(solution)/shard_map/ppermute | solution.py:671
  32.2 7.7 %collective-permute-start.5 = (f32[2,32,1024]{2,1,0:T(8,128)S(1)}, f32[2,32,1024]{2,1,0:T(8,128)S(1)}, u32[]{:S(2)}, u32[]{:S(2)}) collective-permute-start(f32[2,32,1024]{2,1,0:T(8,128)S(1)} %get-tuple-element.51), channel_id=1, source_target_pairs={{8,16},{16,8},{9,17},{17,9},{10,18},{18,10},{11,19},{19,11},{12,20... | collective-permute-start | bytes 786440 | tf_op jit(solution)/shard_map/ppermute | solution.py:671

commit v4 on v3

--- a/solution.py
+++ b/solution.py
@@ -461,10 +461,28 @@
     sweep(half - 1, edged_reader(old_b, 0, head, tail, half, ny))
 
 
-def second_upper_kernel(dims, old, current, weight, flux, head, tail, field, flux_s):
+def inner_copies(field, smoothed, sem, start, z, count, ny):
+    inner = pl.ds(SUB, ny - 2 * SUB)
+    return pltpu.make_async_copy(
+        field.at[:, pl.ds(z, count), inner], smoothed.at[:, pl.ds(start + z, count), inner], sem
+    )
+
+
+LATE = 2
+
+
+def second_upper_kernel(
+    dims, old, current, weight, flux, head, tail, lower, field, smoothed, flux_s, sem
+):
     nz, ny, _ = dims
     half = nz // 2
+    count = nz - half
+    early = inner_copies(lower, smoothed, sem.at[count], 0, 0, half, ny)
+    early.start()
     flux_s[...] = flux[...]
+
+    def out(z):
+        return inner_copies(field, smoothed, sem.at[z], half, z, 1, ny)
 
     def plane(z, carry):
         at = z + half
@@ -472,9 +490,17 @@
             edged_reader(old, z, head, tail, at, ny), edged_reader(old, z + 1, head, tail, at + 1, ny),
             reader(current, z), weight.at[z], writer(field, z), flux_s.at[0], flux_s.at[1], dims, False,
         )
+
+        @pl.when(z < count - LATE)
+        def _():
+            out(z).start()
+
         return carry
 
-    lax.fori_loop(0, nz - half, plane, 0)
+    lax.fori_loop(0, count, plane, 0)
+    for z in range(count - LATE):
+        out(z).wait()
+    early.wait()
 
 
 def fix_trace_kernel(
@@ -523,79 +549,104 @@
                 above[at, k : k + 1, :] = trace_high[k] - pade_decays[j] * high1[nz + at, k : k + 1, :]
 
 
-def surface_kernel(dims, traces, aux, below, above, fresh, even_side, odd_side, outgoing):
+def surface_tiles(dims, k, value, edge_low, edge_high, emit):
     _, ny, nx = dims
     rows, cols = ny // SUB, nx // LANE
     is_first_lane, is_last_lane, is_first_sub, is_last_sub = lane_masks()
-
-    def part(side, carry):
-        outgoing[side] = traces[side]
-
-        def term(j, carry):
-            decay = weight = F32(0.0)
-            for q in range(TERMS):
-                decay = jnp.where(j == q, F32(pade_decays[q]), decay)
-                weight = jnp.where(j == q, F32(pade_weights[q]), weight)
-            for k in range(2):
-
-                def value(i, c):
-                    r, s = tile_at(i, c)
-                    return traces[side, k, r, s] - decay * aux[side, j, k, r, s]
-
-                column = [value(i, 0) for i in range(rows)]
-                lefts = [pltpu.roll(u, LANE - 1, 1) for u in column]
-                rights = [0.0] * rows
-                for c in range(cols):
-                    ups = [pltpu.roll(u, SUB - 1, 0) for u in column]
-                    downs = [pltpu.roll(u, 1, 0) for u in column]
-                    after = [value(i, c + 1) for i in range(rows)] if c + 1 < cols else None
-                    for i in range(rows):
-                        r, s = tile_at(i, c)
-                        u = column[i]
-                        y_next = jnp.where(is_last_sub, ups[i + 1] if i + 1 < rows else 0.0, ups[i])
-                        y_prev = jnp.where(is_first_sub, downs[i - 1] if i else 0.0, downs[i])
-                        if after is not None:
-                            beyond = pltpu.roll(after[i], LANE - 1, 1)
-                        else:
-                            beyond = u if k == 0 else 0.0
-                        x_next = jnp.where(is_last_lane, beyond, lefts[i])
-                        lefts[i] = beyond
-                        right = pltpu.roll(u, 1, 1)
-                        before = rights[i] if c else (u if k == 1 else 0.0)
-                        x_prev = jnp.where(is_first_lane, before, right)
-                        rights[i] = right
-                        new = 0.5 * u - 0.125 * ((y_next + y_prev) + (x_next + x_prev))
-                        fresh[side, j, k, r, s] = new
-                        outgoing[side, k, r, s] += weight * new
-                    column = after
-            return carry
-
-        return lax.fori_loop(0, TERMS, term, carry)
-
-    lax.fori_loop(0, 2, part, 0)
+    column = [value(i, 0) for i in range(rows)]
+    lefts = [pltpu.roll(u, LANE - 1, 1) for u in column]
+    rights = [0.0] * rows
+    for c in range(cols):
+        s = slice(c * LANE, (c + 1) * LANE)
+        ups = [pltpu.roll(u, SUB - 1, 0) for u in column] + [edge_high(s)]
+        downs = [edge_low(s)] + [pltpu.roll(u, 1, 0) for u in column]
+        after = [value(i, c + 1) for i in range(rows)] if c + 1 < cols else None
+        for i in range(rows):
+            u = column[i]
+            y_next = jnp.where(is_last_sub, ups[i + 1], ups[i])
+            y_prev = jnp.where(is_first_sub, downs[i], downs[i + 1])
+            if after is not None:
+                beyond = pltpu.roll(after[i], LANE - 1, 1)
+            else:
+                beyond = u if k == 0 else 0.0
+            x_next = jnp.where(is_last_lane, beyond, lefts[i])
+            lefts[i] = beyond
+            right = pltpu.roll(u, 1, 1)
+            before = rights[i] if c else (u if k == 1 else 0.0)
+            x_prev = jnp.where(is_first_lane, before, right)
+            rights[i] = right
+            emit(i, c, 0.5 * u - 0.125 * ((y_next + y_prev) + (x_next + x_prev)))
+        column = after
+
+
+def outgoing_kernel(dims, traces, aux, below, above, even_side, odd_side):
+    even = is_even("slab")
+    total = sum(pade_weights)
+    for out, side in ((even_side, jnp.where(even, 1, 0)), (odd_side, jnp.where(even, 0, 1))):
+        for k in range(2):
+
+            def value(i, c):
+                r, s = tile_at(i, c)
+                u = total * traces[side, k, r, s]
+                for j in range(TERMS):
+                    u = u - (pade_weights[j] * pade_decays[j]) * aux[side, j, k, r, s]
+                return u
+
+            def edge(source):
+                def row(s):
+                    u = 0.0
+                    for j in range(TERMS):
+                        u = u + pade_weights[j] * source[side * TERMS + j, k : k + 1, s]
+                    return u
+
+                return row
+
+            def emit(i, c, new):
+                r, s = tile_at(i, c)
+                out[k, r, s] = traces[side, k, r, s] + new
+
+            surface_tiles(dims, k, value, edge(below), edge(above), emit)
+
+
+def surface_kernel(dims, traces, aux, below, above, out, fresh, sem):
+    def copy(side, j):
+        return pltpu.make_async_copy(fresh.at[side, j], out.at[0, side, j], sem.at[side * TERMS + j])
+
+    def term(at, carry):
+        side, j = at // TERMS, at % TERMS
+        decay = F32(0.0)
+        for q in range(TERMS):
+            decay = jnp.where(j == q, F32(pade_decays[q]), decay)
+        for k in range(2):
+
+            def value(i, c):
+                r, s = tile_at(i, c)
+                return traces[side, k, r, s] - decay * aux[side, j, k, r, s]
+
+            def emit(i, c, new):
+                r, s = tile_at(i, c)
+                fresh[side, j, k, r, s] = new
+
+            surface_tiles(
+                dims, k, value, lambda s: below[at, k : k + 1, s], lambda s: above[at, k : k + 1, s], emit
+            )
+        copy(side, j).start()
+        return carry
+
+    lax.fori_loop(0, 2 * TERMS, term, 0)
     for side in range(2):
-        for k in range(2):
-            for source, r in ((below, slice(0, 1)), (above, slice(ny - 1, ny))):
-                total = 0.0
-                for j in range(TERMS):
-                    total = total + (0.125 * pade_weights[j]) * source[side * TERMS + j, k : k + 1, :]
-                outgoing[side, k, r, :] -= total
-    even = is_even("slab")
-    even_side[...] = jnp.where(even, outgoing[1], outgoing[0])
-    odd_side[...] = jnp.where(even, outgoing[0], outgoing[1])
-
-
-def write_kernel(dims, field_a, field_b, head, tail, smoothed, edges, sem):
+        for j in range(TERMS):
+            copy(side, j).wait()
+
+
+def write_kernel(dims, field_a, field_b, head, tail, old, smoothed, edges, sem):
     nz, ny, nx = dims
     half = nz // 2
+    count = nz - half
     _, _, is_first_sub, is_last_sub = lane_masks()
-    inner = pl.ds(SUB, ny - 2 * SUB)
-    copies = []
-    for n, (field, start, count) in enumerate(((field_a, 0, half), (field_b, half, nz - half))):
-        planes = pl.ds(start, count)
-        copies.append(pltpu.make_async_copy(field.at[:, :, inner], smoothed.at[:, planes, inner], sem.at[n]))
-        copies[-1].start()
-    for n, (field, start, count) in enumerate(((field_a, 0, half), (field_b, half, nz - half))):
+    copies = [inner_copies(field_b, smoothed, sem.at[0], half, count - LATE, LATE, ny)]
+    copies[0].start()
+    for n, (field, start, planes) in enumerate(((field_a, 0, half), (field_b, half, count))):
 
         def merge(z, carry):
             at = z + start
@@ -610,12 +661,12 @@
                     edges[1, k, at, :, s] = jnp.where(is_last_sub, tail[at, k : k + 1, s], value)
             return carry
 
-        lax.fori_loop(0, count, merge, 0)
-        planes = pl.ds(start, count)
+        lax.fori_loop(0, planes, merge, 0)
+        span = pl.ds(start, planes)
         for e, row in enumerate((0, ny - SUB)):
             copies.append(
                 pltpu.make_async_copy(
-                    edges.at[e, :, planes], smoothed.at[:, planes, pl.ds(row, SUB)], sem.at[2 + 2 * n + e]
+                    edges.at[e, :, span], smoothed.at[:, span, pl.ds(row, SUB)], sem.at[1 + 2 * n + e]
                 )
             )
             copies[-1].start()
@@ -632,33 +683,6 @@
     for copy in copies:
         copy.start()
     for copy in copies:
-        copy.wait()
-
-
-def store_kernel(dims, fresh, low, high, out, edges, sem):
-    _, ny, nx = dims
-    inner = pl.ds(SUB, ny - 2 * SUB)
-    middle = pltpu.make_async_copy(fresh.at[:, :, :, inner], out.at[0, :, :, :, inner], sem.at[0])
-    middle.start()
-    _, _, is_first_sub, is_last_sub = lane_masks()
-    for side in range(2):
-        for j in range(TERMS):
-            for k in range(2):
-                at = side * TERMS + j
-                for c in range(nx // LANE):
-                    s = slice(c * LANE, (c + 1) * LANE)
-                    first = jnp.where(is_first_sub, 0.125 * low[at, k : k + 1, s], 0.0)
-                    last = jnp.where(is_last_sub, 0.125 * high[at, k : k + 1, s], 0.0)
-                    edges[0, side, j, k, :, s] = fresh[side, j, k, 0:SUB, s] - first
-                    edges[1, side, j, k, :, s] = fresh[side, j, k, ny - SUB : ny, s] - last
-    outer = [
-        pltpu.make_async_copy(edges.at[e], out.at[0, :, :, :, pl.ds(start, SUB)], sem.at[1 + e])
-        for e, start in enumerate((0, ny - SUB))
-    ]
-    for copy in outer:
-        copy.start()
-    middle.wait()
-    for copy in outer:
         copy.wait()
 
 
@@ -750,15 +774,15 @@
     )(lower, upper, current_a, weight_a, ghost, head1, tail1, near_extra)
     near2 = swap(near2, "tile", 0)
 
-    upper2 = call(
+    upper2, smoothed = call(
         bind(second_upper_kernel, dims),
-        out_shape=shape(3, count, ny, nx),
-        in_specs=[VM] * 6,
-        out_specs=VM,
-        scratch_shapes=[vm(2, ny, nx)],
+        out_shape=(shape(3, count, ny, nx), shape(3, nz, ny, nx)),
+        in_specs=[VM] * 7,
+        out_specs=(VM, HBM),
+        scratch_shapes=[vm(2, ny, nx), dma((count + 1,))],
         compiler_params=params(12),
         cost_estimate=cost(20 * cells, 14 * cells),
-    )(upper, current_b, weight_b, flux, head1, tail1)
+    )(upper, current_b, weight_b, flux, head1, tail1, lower2)
 
     edge_rows = shape(2 * TERMS, 2, nx)
     head, tail, traces, below, above = call(
@@ -769,38 +793,36 @@
         compiler_params=params(12),
     )(lower2, upper2, weight_a, weight_b, near1, far1, head1, tail1, near2, far2)
 
-    side_shape = shape(2, ny, nx)
-    fresh, even_side, odd_side = call(
-        bind(surface_kernel, dims),
-        out_shape=(shape(2, TERMS, 2, ny, nx), side_shape, side_shape),
+    even_side, odd_side = call(
+        bind(outgoing_kernel, dims),
+        out_shape=(flux_shape, flux_shape),
         in_specs=[VM] * 4,
-        out_specs=(VM,) * 3,
-        scratch_shapes=[vm(2, 2, ny, nx)],
-        compiler_params=params(12),
-        cost_estimate=cost(20 * 16 * ny * nx, 12 * cells),
+        out_specs=(VM,) * 2,
+        compiler_params=params(8),
     )(traces, aux_v, below, above)
     odd_side = swap(odd_side, "slab", 1)
     even_side = swap(even_side, "slab", 0)
 
+    fresh = call(
+        bind(surface_kernel, dims),
+        out_shape=shape(1, 2, TERMS, 2, ny, nx),
+        in_specs=[VM] * 4,
+        out_specs=HBM,
+        scratch_shapes=[vm(2, TERMS, 2, ny, nx), dma((2 * TERMS,))],
+        compiler_params=params(8),
+        cost_estimate=cost(12 * 16 * ny * nx, 12 * 16 * ny * nx),
+    )(traces, aux_v, below, above)
+
     smoothed = call(
         bind(write_kernel, dims),
         out_shape=shape(3, nz, ny, nx),
-        in_specs=[VM] * 4,
+        in_specs=[VM] * 4 + [HBM],
         out_specs=HBM,
-        scratch_shapes=[vm(2, 3, nz, SUB, nx), dma((6,))],
+        input_output_aliases={4: 0},
+        scratch_shapes=[vm(2, 3, nz, SUB, nx), dma((5,))],
         compiler_params=params(12),
         cost_estimate=cost(cells, 12 * cells),
-    )(lower2, upper2, head, tail)
-
-    fresh = call(
-        bind(store_kernel, dims),
-        out_shape=shape(1, 2, TERMS, 2, ny, nx),
-        in_specs=[VM] * 3,
-        out_specs=HBM,
-        scratch_shapes=[vm(2, 2, TERMS, 2, SUB, nx), dma((3,))],
-        compiler_params=params(8),
-        cost_estimate=cost(16 * ny * nx, 8 * 16 * ny * nx),
-    )(fresh, below, above)
+    )(lower2, upper2, head, tail, smoothed)
 
     next_faces = call(
         faces_kernel,

time: 40.9 us -> 39.7 us (0.971)
  Pallas kernels: 23 us -> 22.3 us
  waiting for transfers between devices: 2.84 us -> 2.29 us
    pallas_call x1, Pallas kernels: 2.49 us -> 1.76 us  [iteration(): call(bind(write_kernel, dims), out_shape=shape(3, nz, ny, nx), in_specs=[...]
    ppermute x6, waiting for transfers between devices: 2.84 us -> 2.29 us  [swap(): lax.ppermute(block, axis, [p for i, j in pairs for p in ((i, j), (j, i))])]
  transfers between devices with their start and end apart: 6 -> 6, of which waited for: 2 -> 2; matrix products, arithmetic and copies ran while one was open for 0% -> 0% of each run, Pallas kernels for 37% -> 39%
where the time goes in v4:
time: 39.7 us; the launch traced here: 39.5 us
  Pallas kernels  22.3 us (56%)
  starting transfers between devices  14.2 us (36%)
  waiting for transfers between devices  2.29 us (6%)
  between operations  0.75 us (2%)
    ppermute x6, starting transfers between devices, swap(): lax.ppermute(block, axis, [p for i, j in pairs for p in ((i, j), (j, i))])  14.2 us
    pallas_call x1, Pallas kernels, iteration(): call(bind(first_lower_kernel, dims), out_shape=(shape(3, half + 1, ny, nx...  4.75 us
    pallas_call x1, Pallas kernels, iteration(): call(bind(first_upper_kernel, dims), out_shape=(shape(3, count + 1, ny, n...  3.9 us
    pallas_call x1, Pallas kernels, iteration(): call(bind(second_lower_kernel, dims), out_shape=(shape(3, half, ny, nx),...  2.82 us
    pallas_call x1, Pallas kernels, iteration(): call(bind(second_upper_kernel, dims), out_shape=(shape(3, count, ny, nx),...  2.63 us
    pallas_call x1, Pallas kernels, iteration(): call(bind(surface_kernel, dims), out_shape=shape(1, 2, TERMS, 2, ny, nx),...  2.52 us
    ppermute x6, waiting for transfers between devices, swap(): lax.ppermute(block, axis, [p for i, j in pairs for p in ((i, j), (j, i))])  2.29 us
    pallas_call x1, Pallas kernels, iteration(): call(bind(write_kernel, dims), out_shape=shape(3, nz, ny, nx), in_specs=[...  1.76 us
  transfers between devices with their start and end apart: 6, of which 2 were waited for; matrix products, arithmetic and copies ran while one was open for 0% of the time, Pallas kernels for 39%

profile of v4, /device:TPU:9, one launch (start us, length us, event | category | flops | bytes accessed | tf_op | source)
XLA Modules:
  0.0 39.5 jit_solution(18333378541370124204)
XLA Ops:
  0.6 1.7 %shard_map.78 = f32[22,2,1024]{2,1,0:T(2,128)S(1)} custom-call(f32[3,14,32,1024]{3,2,1,0:T(8,128)} %electric.5, f32[1,2,2,32,1024]{4,3,2,1,0:T(8,128)} %faces.5, f32[1,2,4,2,32,1024]{5,4,3,2,1,0:T(8,128)} %aux.1), custom_call_target="tpu_custom_call" | custom-call | tf_op jit(solution)/shard_map/pallas_call | solution.py:713
  2.4 3.0 %collective-permute-start.1 = (f32[22,2,1024]{2,1,0:T(2,128)S(1)}, f32[22,2,1024]{2,1,0:T(2,128)S(1)}, u32[]{:S(2)}, u32[]{:S(2)}) collective-permute-start(f32[22,2,1024]{2,1,0:T(2,128)S(1)} %shard_map.78), channel_id=1, source_target_pairs={{1,2},{2,1},{3,4},{4,3},{5,6},{6,5},{9,10},{10,9},{11,12},{12,11},... | collective-permute-start | bytes 540680 | tf_op jit(solution)/shard_map/ppermute | solution.py:695
  5.4 4.8 %shard_map.76 = (f32[3,8,32,1024]{3,2,1,0:T(8,128)S(1)}, f32[3,7,32,1024]{3,2,1,0:T(8,128)S(1)}, f32[7,32,1024]{2,1,0:T(8,128)S(1)}, f32[2,32,1024]{2,1,0:T(8,12...) custom-call(f32[3,14,32,1024]{3,2,1,0:T(8,128)} %electric.5, f32[3,14,32,1024]{3,2,1,0:T(8,128)} %current_h.3, ...), custom_call_target="tpu_custom_call" | custom-call | flops 11468800 | bytes 6422528 | tf_op jit(solution)/shard_map/pallas_call | solution.py:723
  10.1 1.4 %collective-permute-start = (f32[22,2,1024]{2,1,0:T(2,128)S(1)}, f32[22,2,1024]{2,1,0:T(2,128)S(1)}, u32[]{:S(2)}, u32[]{:S(2)}) collective-permute-start(f32[22,2,1024]{2,1,0:T(2,128)S(1)} %get-tuple-element.37), channel_id=1, source_target_pairs={{0,1},{1,0},{2,3},{3,2},{4,5},{5,4},{6,7},{7,6},{8,9},{9,8},{10,11... | collective-permute-start | bytes 540680 | tf_op jit(solution)/shard_map/ppermute | solution.py:695
  11.6 3.9 %shard_map.77 = (f32[3,8,32,1024]{3,2,1,0:T(8,128)S(1)}, f32[3,7,32,1024]{3,2,1,0:T(8,128)S(1)}, f32[7,32,1024]{2,1,0:T(8,128)S(1)}, f32[2,4,2,32,1024]{4,3,2,1,0:T(8,128)S(1)}) custom-call(f32[3,14,32,1024]{3,2,1,0:T(8,128)} %electric.5, f32[3,14,32,1024]{3,2,1,0:T(8,128)} %current_h.3, f32[14,32,1024]{2,1,0:T(8,128)} %mass.3, ...), custom_call_target="tpu_custom_call" | custom-call | flops 11468800 | bytes 6422528 | tf_op jit(solution)/shard_map/pallas_call | solution.py:742
  15.5 0.0 collective-permute-done.1.far.far1
  15.5 0.0 collective-permute-done.near.near1
  15.5 0.6 %shard_map.79 = (f32[15,2,1024]{2,1,0:T(2,128)S(1)}, f32[15,3,1024]{2,1,0:T(4,128)S(1)}, f32[17,2,1024]{2,1,0:T(2,128)S(1)}, f32[3,2,1024]{2,1,0:T(2,128)S(1)}) custom-call(f32[3,8,32,1024]{3,2,1,0:T(8,128)S(1)} %get-tuple-element.29.field_a.old_a, f32[3,8,32,1024]{3,2,1,0:T(8,128)S(1)} %get-tuple-element.31.field_b.old_b.old, ...), custom_call_target="tpu_custom_call" | custom-call | tf_op jit(solution)/shard_map/pallas_call | solution.py:758
  16.1 2.8 %shard_map.80 = (f32[3,7,32,1024]{3,2,1,0:T(8,128)S(1)}, f32[2,32,1024]{2,1,0:T(8,128)S(1)}, f32[17,2,1024]{2,1,0:T(2,128)S(1)}) custom-call(f32[3,8,32,1024]{3,2,1,0:T(8,128)S(1)} %get-tuple-element.29.field_a.old_a, f32[3,8,32,1024]{3,2,1,0:T(8,128)S(1)} %get-tuple-element.31.field_b.old_b.old, f32[3,7,32,1024]{3,2,1,0:T(8,128)S(1)} %get-tuple-element.32.current_a.current, ...), custom_call_target="tpu_custom_call" | custom-call | flops 9175040 | bytes 6422528 | tf_op jit(solution)/shard_map/pallas_call | solution.py:767
  18.9 1.3 %collective-permute-start.2 = (f32[17,2,1024]{2,1,0:T(2,128)S(1)}, f32[17,2,1024]{2,1,0:T(2,128)S(1)}, u32[]{:S(2)}, u32[]{:S(2)}) collective-permute-start(f32[17,2,1024]{2,1,0:T(2,128)S(1)} %get-tuple-element.44), channel_id=1, source_target_pairs={{0,1},{1,0},{2,3},{3,2},{4,5},{5,4},{6,7},{7,6},{8,9},{9,8},{10,11... | collective-permute-start | bytes 417800 | tf_op jit(solution)/shard_map/ppermute | solution.py:695
  20.2 2.1 %collective-permute-start.3 = (f32[17,2,1024]{2,1,0:T(2,128)S(1)}, f32[17,2,1024]{2,1,0:T(2,128)S(1)}, u32[]{:S(2)}, u32[]{:S(2)}) collective-permute-start(f32[17,2,1024]{2,1,0:T(2,128)S(1)} %get-tuple-element.45), channel_id=1, source_target_pairs={{1,2},{2,1},{3,4},{4,3},{5,6},{6,5},{9,10},{10,9},{11,12},{12,11},... | collective-permute-start | bytes 417800 | tf_op jit(solution)/shard_map/ppermute | solution.py:695
  22.3 2.6 %shard_map.81 = (f32[3,7,32,1024]{3,2,1,0:T(8,128)S(1)}, f32[3,14,32,1024]{3,2,1,0:T(8,128)}) custom-call(f32[3,8,32,1024]{3,2,1,0:T(8,128)S(1)} %get-tuple-element.31.field_b.old_b.old, f32[3,7,32,1024]{3,2,1,0:T(8,128)S(1)} %get-tuple-element.35.current_b.current, f32[7,32,1024]{2,1,0:T(8,128)S(1)} %get-tuple-element.36.weight_b.weight, ...), custom_call_target="tpu_custom_call" | custom-call | flops 9175040 | bytes 6422528 | tf_op jit(solution)/shard_map/pallas_call | solution.py:777
  24.9 0.0 collective-permute-done.2.near
  25.0 2.0 %collective-permute-done.3.far = f32[17,2,1024]{2,1,0:T(2,128)S(1)} collective-permute-done((f32[17,2,1024]{2,1,0:T(2,128)S(1)}, f32[17,2,1024]{2,1,0:T(2,128)S(1)}, u32[]{:S(2)}, u32[]{:S(2)}) %collective-permute-start.3) | collective-permute-done | bytes 139296 | tf_op jit(solution)/shard_map/ppermute | solution.py:695
  26.9 0.3 shard_map.82
  27.2 0.5 %shard_map.84 = (f32[2,32,1024]{2,1,0:T(8,128)S(1)}, f32[2,32,1024]{2,1,0:T(8,128)S(1)}) custom-call(f32[2,2,32,1024]{3,2,1,0:T(8,128)S(1)} %get-tuple-element.49.traces, f32[2,4,2,32,1024]{4,3,2,1,0:T(8,128)S(1)} %get-tuple-element.50.aux, f32[8,2,1024]{2,1,0:T(2,128)S(1)} %get-tuple-element.51.below, f32[8,2,1024]{2,1,0:T(2,128)S(1)} %get-tuple-element.52.above), custom_call_target="tpu_custom_call" | custom-call | tf_op jit(solution)/shard_map/pallas_call | solution.py:796
  27.7 3.3 %collective-permute-start.4 = (f32[2,32,1024]{2,1,0:T(8,128)S(1)}, f32[2,32,1024]{2,1,0:T(8,128)S(1)}, u32[]{:S(2)}, u32[]{:S(2)}) collective-permute-start(f32[2,32,1024]{2,1,0:T(8,128)S(1)} %get-tuple-element.53), channel_id=1, source_target_pairs={{0,8},{8,0},{16,24},{24,16},{1,9},{9,1},{17,25},{25,17},{2,10},{10... | collective-permute-start | bytes 786440 | tf_op jit(solution)/shard_map/ppermute | solution.py:695
  31.0 3.0 %collective-permute-start.5 = (f32[2,32,1024]{2,1,0:T(8,128)S(1)}, f32[2,32,1024]{2,1,0:T(8,128)S(1)}, u32[]{:S(2)}, u32[]{:S(2)}) collective-permute-start(f32[2,32,1024]{2,1,0:T(8,128)S(1)} %get-tuple-element.54), channel_id=1, source_target_pairs={{8,16},{16,8},{9,17},{17,9},{10,18},{18,10},{11,19},{19,11},{12,20... | collective-permute-start | bytes 786440 | tf_op jit(solution)/shard_map/ppermute | solution.py:695
  34.1 1.8 %shard_map.83 = f32[3,14,32,1024]{3,2,1,0:T(8,128)} custom-call(f32[3,7,32,1024]{3,2,1,0:T(8,128)S(1)} %get-tuple-element.41.lower.field_a, f32[3,7,32,1024]{3,2,1,0:T(8,128)S(1)} %get-tuple-element.43.field_b, f32[15,2,1024]{2,1,0:T(2,128)S(1)} %get-tuple-element.46.head, ...), custom_call_target="tpu_custom_call", output_to_operand_aliasing={{}: (4, {})} | custom-call | flops 458752 | bytes 5505024 | tf_op jit(solution)/shard_map/pallas_call | solution.py:816
  35.8 2.5 %shard_map.86 = f32[1,2,4,2,32,1024]{5,4,3,2,1,0:T(8,128)} custom-call(f32[2,2,32,1024]{3,2,1,0:T(8,128)S(1)} %get-tuple-element.49.traces, f32[2,4,2,32,1024]{4,3,2,1,0:T(8,128)S(1)} %get-tuple-element.50.aux, f32[8,2,1024]{2,1,0:T(2,128)S(1)} %get-tuple-element.51.below, f32[8,2,1024]{2,1,0:T(2,128)S(1)} %get-tuple-element.52.above), custom_call_target="tpu_custom_call" | custom-call | flops 6291456 | bytes 6291456 | tf_op jit(solution)/shard_map/pallas_call | solution.py:806
  38.4 0.0 collective-permute-done.4.even_side
  38.4 0.3 collective-permute-done.5.odd_side
  38.7 0.8 %shard_map.85 = f32[1,2,2,32,1024]{4,3,2,1,0:T(8,128)} custom-call(f32[2,32,1024]{2,1,0:T(8,128)S(1)} %collective-permute-done.4.even_side, f32[2,32,1024]{2,1,0:T(8,128)S(1)} %collective-permute-done.5.odd_side), custom_call_target="tpu_custom_call" | custom-call | tf_op jit(solution)/shard_map/pallas_call | solution.py:827
Async XLA Ops:
  2.4 13.1 %collective-permute-start.1 = (f32[22,2,1024]{2,1,0:T(2,128)S(1)}, f32[22,2,1024]{2,1,0:T(2,128)S(1)}, u32[]{:S(2)}, u32[]{:S(2)}) collective-permute-start(f32[22,2,1024]{2,1,0:T(2,128)S(1)} %shard_map.78), channel_id=1, source_target_pairs={{1,2},{2,1},{3,4},{4,3},{5,6},{6,5},{9,10},{10,9},{11,12},{12,11},... | collective-permute-start | bytes 540680 | tf_op jit(solution)/shard_map/ppermute | solution.py:695
  10.1 5.4 %collective-permute-start = (f32[22,2,1024]{2,1,0:T(2,128)S(1)}, f32[22,2,1024]{2,1,0:T(2,128)S(1)}, u32[]{:S(2)}, u32[]{:S(2)}) collective-permute-start(f32[22,2,1024]{2,1,0:T(2,128)S(1)} %get-tuple-element.37), channel_id=1, source_target_pairs={{0,1},{1,0},{2,3},{3,2},{4,5},{5,4},{6,7},{7,6},{8,9},{9,8},{10,11... | collective-permute-start | bytes 540680 | tf_op jit(solution)/shard_map/ppermute | solution.py:695
  18.9 6.0 %collective-permute-start.2 = (f32[17,2,1024]{2,1,0:T(2,128)S(1)}, f32[17,2,1024]{2,1,0:T(2,128)S(1)}, u32[]{:S(2)}, u32[]{:S(2)}) collective-permute-start(f32[17,2,1024]{2,1,0:T(2,128)S(1)} %get-tuple-element.44), channel_id=1, source_target_pairs={{0,1},{1,0},{2,3},{3,2},{4,5},{5,4},{6,7},{7,6},{8,9},{9,8},{10,11... | collective-permute-start | bytes 417800 | tf_op jit(solution)/shard_map/ppermute | solution.py:695
  20.2 6.7 %collective-permute-start.3 = (f32[17,2,1024]{2,1,0:T(2,128)S(1)}, f32[17,2,1024]{2,1,0:T(2,128)S(1)}, u32[]{:S(2)}, u32[]{:S(2)}) collective-permute-start(f32[17,2,1024]{2,1,0:T(2,128)S(1)} %get-tuple-element.45), channel_id=1, source_target_pairs={{1,2},{2,1},{3,4},{4,3},{5,6},{6,5},{9,10},{10,9},{11,12},{12,11},... | collective-permute-start | bytes 417800 | tf_op jit(solution)/shard_map/ppermute | solution.py:695
  27.7 10.7 %collective-permute-start.4 = (f32[2,32,1024]{2,1,0:T(8,128)S(1)}, f32[2,32,1024]{2,1,0:T(8,128)S(1)}, u32[]{:S(2)}, u32[]{:S(2)}) collective-permute-start(f32[2,32,1024]{2,1,0:T(8,128)S(1)} %get-tuple-element.53), channel_id=1, source_target_pairs={{0,8},{8,0},{16,24},{24,16},{1,9},{9,1},{17,25},{25,17},{2,10},{10... | collective-permute-start | bytes 786440 | tf_op jit(solution)/shard_map/ppermute | solution.py:695
  31.0 7.7 %collective-permute-start.5 = (f32[2,32,1024]{2,1,0:T(8,128)S(1)}, f32[2,32,1024]{2,1,0:T(8,128)S(1)}, u32[]{:S(2)}, u32[]{:S(2)}) collective-permute-start(f32[2,32,1024]{2,1,0:T(8,128)S(1)} %get-tuple-element.54), channel_id=1, source_target_pairs={{8,16},{16,8},{9,17},{17,9},{10,18},{18,10},{11,19},{19,11},{12,20... | collective-permute-start | bytes 786440 | tf_op jit(solution)/shard_map/ppermute | solution.py:695

commit v5 on v4

--- a/solution.py
+++ b/solution.py
@@ -277,8 +277,8 @@
 
 
 def first_upper_kernel(
-    dims, electric, current_h, mass, faces, aux_h, flux,
-    field, current, weight, aux,
+    dims, electric, current_h, mass, faces, flux,
+    field, current, weight,
     flux_s, field_sem, current_sem, weight_sem, sem,
 ):
     nz, _, _ = dims
@@ -296,7 +296,6 @@
         return copy(mass.at[pl.ds(z + half, 1)], weight.at[pl.ds(z, 1)], weight_sem.at[z])
 
     high_copies = [copy(faces.at[0, 1, k], field.at[k, count], sem.at[k]) for k in range(2)]
-    aux_copy = copy(aux_h.at[0], aux, sem.at[2])
     field_copy(0).start()
 
     def start(z, carry):
@@ -310,7 +309,6 @@
     weight_copy(count - 1).start()
     for high in high_copies:
         high.start()
-    aux_copy.start()
     flux_s[...] = flux[...]
     field_copy(0).wait()
 
@@ -333,7 +331,6 @@
         return carry
 
     lax.fori_loop(0, count, plane, 0)
-    aux_copy.wait()
 
 
 class Planes:
@@ -347,29 +344,12 @@
         return self.upper[at[: self.dim] + (z - self.half,) + at[self.dim + 1 :]]
 
 
-def fix_pack_kernel(
-    dims, field_a, field_b, current_a, current_b, weight_a, weight_b, ghost, near, far,
-    head, tail, far_next, near_extra,
-):
+def fix_rows(dims, fields, ghost, halo, from_below, head, tail, send):
     nz, ny, nx = dims
     half = nz // 2
-    even = is_even("tile")
     end = slice(ny - 1, ny)
-    field = Planes(field_a, field_b, half, 1)
-    current = Planes(current_a, current_b, half, 1)
-    weight = Planes(weight_a, weight_b, half, 0)
-    low, high = halo_views(near, far)
-    for z in range(nz):
-        head[z, 0:1, :], head[z, 1:2, :] = fixed_first(field, weight, low, z, z)
-        x, y, zc = fixed_last(field, weight, high, z, z, ny)
-        tail[z, 0:1, :], tail[z, 1:2, :], tail[z, 2:3, :] = x, y, zc
-    head[nz, 0:1, :] = field[0, nz, 0:1, :]
-    tail[nz, 0:1, :] = field[0, nz, end, :]
-    tail[nz, 1:2, :] = field[1, nz, end, :]
-    for z in range(nz):
-        up = upward([tail[z, k : k + 1, :] for k in range(3)], tail[z + 1, 1:2, :])
-        for q in range(2):
-            far_next[z, q : q + 1, :] = jnp.where(even, head[z, q : q + 1, :], up[q])
+    field, current = (Planes(lower, upper, half, 1) for lower, upper in fields[:2])
+    weight = Planes(*fields[2], half, 0)
 
     def value(k, z, r):
         at = slice(r, r + 1)
@@ -407,14 +387,58 @@
             w,
         )
 
-    for side in range(2):
-        z = (nz - 1) * side
-        down, up = trace(z, 0), trace(z, ny - 1)
-        for k in range(2):
-            far_next[nz + side, k : k + 1, :] = jnp.where(even, down[k], up[k])
-            near_extra[side, k : k + 1, :] = jnp.where(even, up[k], down[k])
-        far_next[nz + 2, side : side + 1, :] = jnp.where(even, down[2], up[2])
-        near_extra[2, side : side + 1, :] = jnp.where(even, up[2], down[2])
+    def pack_traces(r):
+        for side in range(2):
+            x, y, w = trace((nz - 1) * side, r)
+            send[nz + side, 0:1, :] = x
+            send[nz + side, 1:2, :] = y
+            send[nz + 2, side : side + 1, :] = w
+
+    @pl.when(from_below)
+    def _():
+        for z in range(nz):
+            x, zc = fixed_first(field, weight, halo, z, z)
+            head[z, 0:1, :], head[z, 1:2, :] = x, zc
+            send[z, 0:1, :], send[z, 1:2, :] = x, zc
+        head[nz, 0:1, :] = field[0, nz, 0:1, :]
+        pack_traces(0)
+
+    @pl.when(jnp.logical_not(from_below))
+    def _():
+        for z in range(nz):
+            x, y, zc = fixed_last(field, weight, halo, z, z, ny)
+            tail[z, 0:1, :], tail[z, 1:2, :], tail[z, 2:3, :] = x, y, zc
+        tail[nz, 0:1, :] = field[0, nz, end, :]
+        tail[nz, 1:2, :] = field[1, nz, end, :]
+        for z in range(nz):
+            up = upward([tail[z, k : k + 1, :] for k in range(3)], tail[z + 1, 1:2, :])
+            send[z, 0:1, :], send[z, 1:2, :] = up
+        pack_traces(ny - 1)
+
+
+def fix_far_kernel(
+    dims, field_a, field_b, current_a, current_b, weight_a, weight_b, ghost, far, head, tail, send
+):
+    fields = ((field_a, field_b), (current_a, current_b), (weight_a, weight_b))
+    fix_rows(dims, fields, ghost, far, is_even("tile"), head, tail, send)
+
+
+def fix_near_kernel(
+    dims, field_a, field_b, current_a, current_b, weight_a, weight_b, ghost, near, head_f, tail_f,
+    head, tail, send,
+):
+    even = is_even("tile")
+    fields = ((field_a, field_b), (current_a, current_b), (weight_a, weight_b))
+
+    @pl.when(even)
+    def _():
+        head[...] = head_f[...]
+
+    @pl.when(jnp.logical_not(even))
+    def _():
+        tail[...] = tail_f[...]
+
+    fix_rows(dims, fields, ghost, near, jnp.logical_not(even), head, tail, send)
 
 
 def edged_reader(ref, z, head, tail, plane, ny):
@@ -434,16 +458,11 @@
 
 
 def second_lower_kernel(
-    dims, old_a, old_b, current, weight, ghost, head, tail, near_extra, field, flux, near_next
+    dims, old_a, old_b, current, weight, ghost, head, tail, near_rows, field, flux, near_next
 ):
     nz, ny, _ = dims
     half = nz // 2
-    even = is_even("tile")
-    for z in range(nz):
-        up = upward([tail[z, k : k + 1, :] for k in range(3)], tail[z + 1, 1:2, :])
-        for q in range(2):
-            near_next[z, q : q + 1, :] = jnp.where(even, up[q], head[z, q : q + 1, :])
-    near_next[nz : nz + 3] = near_extra[...]
+    near_next[...] = near_rows[...]
     hx_s, hy_s = flux.at[0], flux.at[1]
     ghost_flux(edged_reader(old_a, 0, head, tail, 0, ny), ghost, hx_s, hy_s, dims)
 
@@ -472,13 +491,15 @@
 
 
 def second_upper_kernel(
-    dims, old, current, weight, flux, head, tail, lower, field, smoothed, flux_s, sem
+    dims, old, current, weight, flux, head, tail, lower, aux_h, field, smoothed, aux, flux_s, sem
 ):
     nz, ny, _ = dims
     half = nz // 2
     count = nz - half
     early = inner_copies(lower, smoothed, sem.at[count], 0, 0, half, ny)
     early.start()
+    load = pltpu.make_async_copy(aux_h.at[0], aux, sem.at[count + 1])
+    load.start()
     flux_s[...] = flux[...]
 
     def out(z):
@@ -501,6 +522,7 @@
     for z in range(count - LATE):
         out(z).wait()
     early.wait()
+    load.wait()
 
 
 def fix_trace_kernel(
@@ -739,30 +761,37 @@
     )(electric, current, mass, faces, aux)
     near1 = swap(near1, "tile", 0)
 
-    upper, current_b, weight_b, aux_v = call(
+    upper, current_b, weight_b = call(
         bind(first_upper_kernel, dims),
         out_shape=(
             shape(3, count + 1, ny, nx),
             shape(3, count, ny, nx),
             shape(count, ny, nx),
-            shape(2, TERMS, 2, ny, nx),
         ),
-        in_specs=[HBM] * 5 + [VM],
-        out_specs=(VM,) * 4,
-        scratch_shapes=[vm(2, ny, nx), dma((count,)), dma((count,)), dma((count,)), dma((3,))],
+        in_specs=[HBM] * 4 + [VM],
+        out_specs=(VM,) * 3,
+        scratch_shapes=[vm(2, ny, nx), dma((count,)), dma((count,)), dma((count,)), dma((2,))],
         compiler_params=params(16),
         cost_estimate=cost(25 * cells, 14 * cells),
-    )(electric, current, mass, faces, aux, flux)
+    )(electric, current, mass, faces, flux)
 
     heads, tails = shape(nz + 1, 2, nx), shape(nz + 1, 3, nx)
-    head1, tail1, far2, near_extra = call(
-        bind(fix_pack_kernel, dims),
-        out_shape=(heads, tails, rows2, shape(3, 2, nx)),
-        in_specs=[VM] * 9,
-        out_specs=(VM,) * 4,
-        compiler_params=params(12),
-    )(lower, upper, current_a, current_b, weight_a, weight_b, ghost, near1, far1)
+    state = (lower, upper, current_a, current_b, weight_a, weight_b, ghost)
+    head_f, tail_f, far2 = call(
+        bind(fix_far_kernel, dims),
+        out_shape=(heads, tails, rows2),
+        in_specs=[VM] * 8,
+        out_specs=(VM,) * 3,
+        compiler_params=params(8),
+    )(*state, far1)
     far2 = swap(far2, "tile", 1)
+    head1, tail1, near_rows = call(
+        bind(fix_near_kernel, dims),
+        out_shape=(heads, tails, rows2),
+        in_specs=[VM] * 10,
+        out_specs=(VM,) * 3,
+        compiler_params=params(8),
+    )(*state, near1, head_f, tail_f)
 
     lower2, flux, near2 = call(
         bind(second_lower_kernel, dims),
@@ -771,18 +800,18 @@
         out_specs=(VM,) * 3,
         compiler_params=params(12),
         cost_estimate=cost(20 * cells, 14 * cells),
-    )(lower, upper, current_a, weight_a, ghost, head1, tail1, near_extra)
+    )(lower, upper, current_a, weight_a, ghost, head1, tail1, near_rows)
     near2 = swap(near2, "tile", 0)
 
-    upper2, smoothed = call(
+    upper2, smoothed, aux_v = call(
         bind(second_upper_kernel, dims),
-        out_shape=(shape(3, count, ny, nx), shape(3, nz, ny, nx)),
-        in_specs=[VM] * 7,
-        out_specs=(VM, HBM),
-        scratch_shapes=[vm(2, ny, nx), dma((count + 1,))],
+        out_shape=(shape(3, count, ny, nx), shape(3, nz, ny, nx), shape(2, TERMS, 2, ny, nx)),
+        in_specs=[VM] * 7 + [HBM],
+        out_specs=(VM, HBM, VM),
+        scratch_shapes=[vm(2, ny, nx), dma((count + 2,))],
         compiler_params=params(12),
         cost_estimate=cost(20 * cells, 14 * cells),
-    )(upper, current_b, weight_b, flux, head1, tail1, lower2)
+    )(upper, current_b, weight_b, flux, head1, tail1, lower2, aux)
 
     edge_rows = shape(2 * TERMS, 2, nx)
     head, tail, traces, below, above = call(

time: 39.7 us -> 39.2 us (0.987)
  waiting for transfers between devices: 2.29 us -> 1.74 us
    ppermute x6, waiting for transfers between devices: 2.29 us -> 1.74 us  [swap(): lax.ppermute(block, axis, [p for i, j in pairs for p in ((i, j), (j, i))])]
  transfers between devices with their start and end apart: 6 -> 6, of which waited for: 2 -> 2; matrix products, arithmetic and copies ran while one was open for 0% -> 0% of each run, Pallas kernels for 39% -> 41%
where the time goes in v5:
time: 39.2 us; the launch traced here: 39 us
  Pallas kernels  22.4 us (57%)
  starting transfers between devices  14.1 us (36%)
  waiting for transfers between devices  1.74 us (4%)
  between operations  0.76 us (2%)
    ppermute x6, starting transfers between devices, swap(): lax.ppermute(block, axis, [p for i, j in pairs for p in ((i, j), (j, i))])  14.1 us
    pallas_call x1, Pallas kernels, iteration(): call(bind(first_lower_kernel, dims), out_shape=(shape(3, half + 1, ny, nx...  4.84 us
    pallas_call x1, Pallas kernels, iteration(): call(bind(first_upper_kernel, dims), out_shape=(shape(3, count + 1, ny, n...  3.93 us
    pallas_call x1, Pallas kernels, iteration(): call(bind(second_upper_kernel, dims), out_shape=(shape(3, count, ny, nx),...  2.74 us
    pallas_call x1, Pallas kernels, iteration(): call(bind(second_lower_kernel, dims), out_shape=(shape(3, half, ny, nx),...  2.68 us
    pallas_call x1, Pallas kernels, iteration(): call(bind(surface_kernel, dims), out_shape=shape(1, 2, TERMS, 2, ny, nx),...  2.52 us
    pallas_call x1, Pallas kernels, iteration(): call(bind(write_kernel, dims), out_shape=shape(3, nz, ny, nx), in_specs=[...  1.77 us
    ppermute x6, waiting for transfers between devices, swap(): lax.ppermute(block, axis, [p for i, j in pairs for p in ((i, j), (j, i))])  1.74 us
  transfers between devices with their start and end apart: 6, of which 2 were waited for; matrix products, arithmetic and copies ran while one was open for 0% of the time, Pallas kernels for 41%

profile of v5, /device:TPU:9, one launch (start us, length us, event | category | flops | bytes accessed | tf_op | source)
XLA Modules:
  0.0 39.0 jit_solution(2822859877542506607)
XLA Ops:
  0.6 1.7 %shard_map.78 = f32[22,2,1024]{2,1,0:T(2,128)S(1)} custom-call(f32[3,14,32,1024]{3,2,1,0:T(8,128)} %electric.5, f32[1,2,2,32,1024]{4,3,2,1,0:T(8,128)} %faces.5, f32[1,2,4,2,32,1024]{5,4,3,2,1,0:T(8,128)} %aux_h.3), custom_call_target="tpu_custom_call" | custom-call | tf_op jit(solution)/shard_map/pallas_call | solution.py:735
  2.4 3.0 %collective-permute-start.1 = (f32[22,2,1024]{2,1,0:T(2,128)S(1)}, f32[22,2,1024]{2,1,0:T(2,128)S(1)}, u32[]{:S(2)}, u32[]{:S(2)}) collective-permute-start(f32[22,2,1024]{2,1,0:T(2,128)S(1)} %shard_map.78), channel_id=1, source_target_pairs={{1,2},{2,1},{3,4},{4,3},{5,6},{6,5},{9,10},{10,9},{11,12},{12,11},... | collective-permute-start | bytes 540680 | tf_op jit(solution)/shard_map/ppermute | solution.py:717
  5.4 4.8 %shard_map.76 = (f32[3,8,32,1024]{3,2,1,0:T(8,128)S(1)}, f32[3,7,32,1024]{3,2,1,0:T(8,128)S(1)}, f32[7,32,1024]{2,1,0:T(8,128)S(1)}, f32[2,32,1024]{2,1,0:T(8,12...) custom-call(f32[3,14,32,1024]{3,2,1,0:T(8,128)} %electric.5, f32[3,14,32,1024]{3,2,1,0:T(8,128)} %current_h.3, ...), custom_call_target="tpu_custom_call" | custom-call | flops 11468800 | bytes 6422528 | tf_op jit(solution)/shard_map/pallas_call | solution.py:745
  10.2 1.4 %collective-permute-start = (f32[22,2,1024]{2,1,0:T(2,128)S(1)}, f32[22,2,1024]{2,1,0:T(2,128)S(1)}, u32[]{:S(2)}, u32[]{:S(2)}) collective-permute-start(f32[22,2,1024]{2,1,0:T(2,128)S(1)} %get-tuple-element.39), channel_id=1, source_target_pairs={{0,1},{1,0},{2,3},{3,2},{4,5},{5,4},{6,7},{7,6},{8,9},{9,8},{10,11... | collective-permute-start | bytes 540680 | tf_op jit(solution)/shard_map/ppermute | solution.py:717
  11.7 3.9 %shard_map.77 = (f32[3,8,32,1024]{3,2,1,0:T(8,128)S(1)}, f32[3,7,32,1024]{3,2,1,0:T(8,128)S(1)}, f32[7,32,1024]{2,1,0:T(8,128)S(1)}) custom-call(f32[3,14,32,1024]{3,2,1,0:T(8,128)} %electric.5, f32[3,14,32,1024]{3,2,1,0:T(8,128)} %current_h.3, f32[14,32,1024]{2,1,0:T(8,128)} %mass.3, f32[1,2,2,32,1024]{4,3,2,1,0:T(8,128)} %faces.5, ...), custom_call_target="tpu_custom_call" | custom-call | flops 11468800 | bytes 6422528 | tf_op jit(solution)/shard_map/pallas_call | solution.py:764
  15.6 0.0 collective-permute-done.1.far.far1
  15.6 0.2 shard_map.79
  15.8 0.0 collective-permute-done.near.near1
  15.8 0.4 %shard_map.80 = (f32[15,2,1024]{2,1,0:T(2,128)S(1)}, f32[15,3,1024]{2,1,0:T(4,128)S(1)}, f32[17,2,1024]{2,1,0:T(2,128)S(1)}) custom-call(f32[3,8,32,1024]{3,2,1,0:T(8,128)S(1)} %get-tuple-element.31.field_a.old_a, f32[3,8,32,1024]{3,2,1,0:T(8,128)S(1)} %get-tuple-element.33.field_b.old_b.old, f32[3,7,32,1024]{3,2,1,0:T(8,128)S(1)} %get-tuple-element.34.current_a.current, ...), custom_call_target="tpu_custom_call" | custom-call | tf_op jit(solution)/shard_map/pallas_call | solution.py:788
  16.3 2.7 %shard_map.81 = (f32[3,7,32,1024]{3,2,1,0:T(8,128)S(1)}, f32[2,32,1024]{2,1,0:T(8,128)S(1)}, f32[17,2,1024]{2,1,0:T(2,128)S(1)}) custom-call(f32[3,8,32,1024]{3,2,1,0:T(8,128)S(1)} %get-tuple-element.31.field_a.old_a, f32[3,8,32,1024]{3,2,1,0:T(8,128)S(1)} %get-tuple-element.33.field_b.old_b.old, f32[3,7,32,1024]{3,2,1,0:T(8,128)S(1)} %get-tuple-element.34.current_a.current, ...), custom_call_target="tpu_custom_call" | custom-call | flops 9175040 | bytes 6422528 | tf_op jit(solution)/shard_map/pallas_call | solution.py:796
  19.0 0.8 %collective-permute-start.2 = (f32[17,2,1024]{2,1,0:T(2,128)S(1)}, f32[17,2,1024]{2,1,0:T(2,128)S(1)}, u32[]{:S(2)}, u32[]{:S(2)}) collective-permute-start(f32[17,2,1024]{2,1,0:T(2,128)S(1)} %get-tuple-element.48), channel_id=1, source_target_pairs={{0,1},{1,0},{2,3},{3,2},{4,5},{5,4},{6,7},{7,6},{8,9},{9,8},{10,11... | collective-permute-start | bytes 417800 | tf_op jit(solution)/shard_map/ppermute | solution.py:717
  19.8 2.5 %collective-permute-start.3 = (f32[17,2,1024]{2,1,0:T(2,128)S(1)}, f32[17,2,1024]{2,1,0:T(2,128)S(1)}, u32[]{:S(2)}, u32[]{:S(2)}) collective-permute-start(f32[17,2,1024]{2,1,0:T(2,128)S(1)} %get-tuple-element.49), channel_id=1, source_target_pairs={{1,2},{2,1},{3,4},{4,3},{5,6},{6,5},{9,10},{10,9},{11,12},{12,11},... | collective-permute-start | bytes 417800 | tf_op jit(solution)/shard_map/ppermute | solution.py:717
  22.3 2.7 %shard_map.82 = (f32[3,7,32,1024]{3,2,1,0:T(8,128)S(1)}, f32[3,14,32,1024]{3,2,1,0:T(8,128)}, f32[2,4,2,32,1024]{4,3,2,1,0:T(8,128)S(1)}) custom-call(f32[3,8,32,1024]{3,2,1,0:T(8,128)S(1)} %get-tuple-element.33.field_b.old_b.old, f32[3,7,32,1024]{3,2,1,0:T(8,128)S(1)} %get-tuple-element.37.current_b.current, ...), custom_call_target="tpu_custom_call" | custom-call | flops 9175040 | bytes 6422528 | tf_op jit(solution)/shard_map/pallas_call | solution.py:806
  25.0 0.0 collective-permute-done.2.near
  25.0 1.4 %collective-permute-done.3.far = f32[17,2,1024]{2,1,0:T(2,128)S(1)} collective-permute-done((f32[17,2,1024]{2,1,0:T(2,128)S(1)}, f32[17,2,1024]{2,1,0:T(2,128)S(1)}, u32[]{:S(2)}, u32[]{:S(2)}) %collective-permute-start.3) | collective-permute-done | bytes 139296 | tf_op jit(solution)/shard_map/ppermute | solution.py:717
  26.5 0.3 shard_map.83
  26.7 0.5 %shard_map.85 = (f32[2,32,1024]{2,1,0:T(8,128)S(1)}, f32[2,32,1024]{2,1,0:T(8,128)S(1)}) custom-call(f32[2,2,32,1024]{3,2,1,0:T(8,128)S(1)} %get-tuple-element.53.traces, f32[2,4,2,32,1024]{4,3,2,1,0:T(8,128)S(1)} %get-tuple-element.54.aux, f32[8,2,1024]{2,1,0:T(2,128)S(1)} %get-tuple-element.55.below, f32[8,2,1024]{2,1,0:T(2,128)S(1)} %get-tuple-element.56.above), custom_call_target="tpu_custom_call" | custom-call | tf_op jit(solution)/shard_map/pallas_call | solution.py:825
  27.2 3.3 %collective-permute-start.4 = (f32[2,32,1024]{2,1,0:T(8,128)S(1)}, f32[2,32,1024]{2,1,0:T(8,128)S(1)}, u32[]{:S(2)}, u32[]{:S(2)}) collective-permute-start(f32[2,32,1024]{2,1,0:T(8,128)S(1)} %get-tuple-element.57), channel_id=1, source_target_pairs={{0,8},{8,0},{16,24},{24,16},{1,9},{9,1},{17,25},{25,17},{2,10},{10... | collective-permute-start | bytes 786440 | tf_op jit(solution)/shard_map/ppermute | solution.py:717
  30.6 3.0 %collective-permute-start.5 = (f32[2,32,1024]{2,1,0:T(8,128)S(1)}, f32[2,32,1024]{2,1,0:T(8,128)S(1)}, u32[]{:S(2)}, u32[]{:S(2)}) collective-permute-start(f32[2,32,1024]{2,1,0:T(8,128)S(1)} %get-tuple-element.58), channel_id=1, source_target_pairs={{8,16},{16,8},{9,17},{17,9},{10,18},{18,10},{11,19},{19,11},{12,20... | collective-permute-start | bytes 786440 | tf_op jit(solution)/shard_map/ppermute | solution.py:717
  33.6 1.8 %shard_map.84 = f32[3,14,32,1024]{3,2,1,0:T(8,128)} custom-call(f32[3,7,32,1024]{3,2,1,0:T(8,128)S(1)} %get-tuple-element.45.lower.field_a, f32[3,7,32,1024]{3,2,1,0:T(8,128)S(1)} %get-tuple-element.47.field_b, f32[15,2,1024]{2,1,0:T(2,128)S(1)} %get-tuple-element.50.head, ...), custom_call_target="tpu_custom_call", output_to_operand_aliasing={{}: (4, {})} | custom-call | flops 458752 | bytes 5505024 | tf_op jit(solution)/shard_map/pallas_call | solution.py:845
  35.4 2.5 %shard_map.87 = f32[1,2,4,2,32,1024]{5,4,3,2,1,0:T(8,128)} custom-call(f32[2,2,32,1024]{3,2,1,0:T(8,128)S(1)} %get-tuple-element.53.traces, f32[2,4,2,32,1024]{4,3,2,1,0:T(8,128)S(1)} %get-tuple-element.54.aux, f32[8,2,1024]{2,1,0:T(2,128)S(1)} %get-tuple-element.55.below, f32[8,2,1024]{2,1,0:T(2,128)S(1)} %get-tuple-element.56.above), custom_call_target="tpu_custom_call" | custom-call | flops 6291456 | bytes 6291456 | tf_op jit(solution)/shard_map/pallas_call | solution.py:835
  37.9 0.0 collective-permute-done.4.even_side
  37.9 0.3 collective-permute-done.5.odd_side
  38.2 0.8 %shard_map.86 = f32[1,2,2,32,1024]{4,3,2,1,0:T(8,128)} custom-call(f32[2,32,1024]{2,1,0:T(8,128)S(1)} %collective-permute-done.4.even_side, f32[2,32,1024]{2,1,0:T(8,128)S(1)} %collective-permute-done.5.odd_side), custom_call_target="tpu_custom_call" | custom-call | tf_op jit(solution)/shard_map/pallas_call | solution.py:856
Async XLA Ops:
  2.4 13.3 %collective-permute-start.1 = (f32[22,2,1024]{2,1,0:T(2,128)S(1)}, f32[22,2,1024]{2,1,0:T(2,128)S(1)}, u32[]{:S(2)}, u32[]{:S(2)}) collective-permute-start(f32[22,2,1024]{2,1,0:T(2,128)S(1)} %shard_map.78), channel_id=1, source_target_pairs={{1,2},{2,1},{3,4},{4,3},{5,6},{6,5},{9,10},{10,9},{11,12},{12,11},... | collective-permute-start | bytes 540680 | tf_op jit(solution)/shard_map/ppermute | solution.py:717
  10.2 5.6 %collective-permute-start = (f32[22,2,1024]{2,1,0:T(2,128)S(1)}, f32[22,2,1024]{2,1,0:T(2,128)S(1)}, u32[]{:S(2)}, u32[]{:S(2)}) collective-permute-start(f32[22,2,1024]{2,1,0:T(2,128)S(1)} %get-tuple-element.39), channel_id=1, source_target_pairs={{0,1},{1,0},{2,3},{3,2},{4,5},{5,4},{6,7},{7,6},{8,9},{9,8},{10,11... | collective-permute-start | bytes 540680 | tf_op jit(solution)/shard_map/ppermute | solution.py:717
  19.0 6.1 %collective-permute-start.2 = (f32[17,2,1024]{2,1,0:T(2,128)S(1)}, f32[17,2,1024]{2,1,0:T(2,128)S(1)}, u32[]{:S(2)}, u32[]{:S(2)}) collective-permute-start(f32[17,2,1024]{2,1,0:T(2,128)S(1)} %get-tuple-element.48), channel_id=1, source_target_pairs={{0,1},{1,0},{2,3},{3,2},{4,5},{5,4},{6,7},{7,6},{8,9},{9,8},{10,11... | collective-permute-start | bytes 417800 | tf_op jit(solution)/shard_map/ppermute | solution.py:717
  19.8 6.7 %collective-permute-start.3 = (f32[17,2,1024]{2,1,0:T(2,128)S(1)}, f32[17,2,1024]{2,1,0:T(2,128)S(1)}, u32[]{:S(2)}, u32[]{:S(2)}) collective-permute-start(f32[17,2,1024]{2,1,0:T(2,128)S(1)} %get-tuple-element.49), channel_id=1, source_target_pairs={{1,2},{2,1},{3,4},{4,3},{5,6},{6,5},{9,10},{10,9},{11,12},{12,11},... | collective-permute-start | bytes 417800 | tf_op jit(solution)/shard_map/ppermute | solution.py:717
  27.2 10.7 %collective-permute-start.4 = (f32[2,32,1024]{2,1,0:T(8,128)S(1)}, f32[2,32,1024]{2,1,0:T(8,128)S(1)}, u32[]{:S(2)}, u32[]{:S(2)}) collective-permute-start(f32[2,32,1024]{2,1,0:T(8,128)S(1)} %get-tuple-element.57), channel_id=1, source_target_pairs={{0,8},{8,0},{16,24},{24,16},{1,9},{9,1},{17,25},{25,17},{2,10},{10... | collective-permute-start | bytes 786440 | tf_op jit(solution)/shard_map/ppermute | solution.py:717
  30.6 7.7 %collective-permute-start.5 = (f32[2,32,1024]{2,1,0:T(8,128)S(1)}, f32[2,32,1024]{2,1,0:T(8,128)S(1)}, u32[]{:S(2)}, u32[]{:S(2)}) collective-permute-start(f32[2,32,1024]{2,1,0:T(8,128)S(1)} %get-tuple-element.58), channel_id=1, source_target_pairs={{8,16},{16,8},{9,17},{17,9},{10,18},{18,10},{11,19},{19,11},{12,20... | collective-permute-start | bytes 786440 | tf_op jit(solution)/shard_map/ppermute | solution.py:717
